TPU v7x, 32 devices: a whole 2x2x4 slice. The times are simulated.
32 devices in a mesh: dp: 4 (over z), gx: 4 (over y, core), gy: 2 (over x).
Axes of the slice: x: 2, y: 2, z: 4, core: 2. Of those that a mesh axis runs over, the one named last changes fastest.
Arguments:
- features: bfloat16 [64, 96, 512], P(('dp', 'gx', 'gy')), parts along dimension 0, may hold values from -6 to 6
- occupancy: int32 [64, 18], P(('dp', 'gx', 'gy')), parts along dimension 0, may hold values from 0 to 1073741823, as said below
- neighbours: int32 [64, 27], P(('dp', 'gx', 'gy')), parts along dimension 0, may hold values from -1 to 33, as said below
- send_slots: int32 [32, 4, 2], P(('dp', 'gx'), 'gy'), parts along dimension 0, may hold values from -1 to 1, as said below
- weight_a: bfloat16 [27, 96, 96], replicated, may hold values from -0.125 to 0.125
- weight_b: bfloat16 [27, 96, 256], replicated, may hold values from -0.125 to 0.125
- cotangent: bfloat16 [64, 256, 512], P(('dp', 'gx', 'gy')), parts along dimension 0, may hold values from -6 to 6
Outputs:
- layer_out: bfloat16 [64, 256, 512], P(('dp', 'gx', 'gy')), parts along dimension 0
- grad_features: bfloat16 [64, 96, 512], P(('dp', 'gx', 'gy')), parts along dimension 0
- grad_weight_a: float32 [108, 96, 96], P('dp'), parts along dimension 0
- grad_weight_b: float32 [108, 96, 256], P('dp'), parts along dimension 0
There are 4 independent parts, one for each index of `dp`. A program takes and returns all parts, laid end to end along the dimension named above; an argument that names none is the same for every part. Nothing has to cross between parts.
Inputs may be any that keep to these rules, and one draw needn't show every extreme that they name: Tile (i, j) covers brick positions X in 2 i, 2 i + 1 and Y in 2 j, 2 j + 1 with all Z; its bricks fill its slots from 0 upward in the order of (X, Y, Z), and send_slots names each of them at its position; every tile holds 1 to 2 bricks, and some tile holds 2. `neighbours`: for a slot holding a brick, entry 9 (a+1) + 3 (b+1) + (c+1) is the table index of the brick at brick offset (a, b, c): its slot if that brick lies in the same tile, the index of its cell in the table if it lies in a neighbouring tile, -1 if no brick is there; entry 13 is the slot itself; slots without a brick hold -1 throughout. `occupancy`: slots without a brick are all zero.
All inputs are finite; a program needn't handle non-finite values.
Results may differ from a plain program's by a relative error of at most 0.0051.
Values may be sent and summed in bfloat16 or wider, within the bound.
No kernel may reach another device: no remote copies, remote signals or barrier semaphores. Data moves between devices by JAX's collectives and lax.ppermute only.
A program may use at most 128 MiB of HBM per device.

v0:
```python
import functools

import jax
import jax.numpy as jnp
from jax import lax
from jax.experimental import pallas as pl
from jax.experimental.pallas import tpu as pltpu
from jax.sharding import PartitionSpec as P

EDGE = 8
VOX = 512
TAPS = 27
PLANE = 80
PADDED = 896
OUTER = 640
FIRST = 88
FACE = 128
FAR = 100
BF = jnp.bfloat16
F32 = jnp.float32
VMEM = pl.BlockSpec(memory_space=pltpu.VMEM)
SMEM = pl.BlockSpec(memory_space=pltpu.SMEM)
LIMIT = 58 * 1024 * 1024


def iota(shape, dim):
    return lax.broadcasted_iota(jnp.int32, shape, dim)


def one_hot(cond):
    return jnp.where(cond, 1.0, 0.0).astype(BF)


def slot_places(send_ref):
    places = []
    for slot in range(2):
        px = py = pz = held = jnp.int32(0)
        for x in range(2):
            for y in range(2):
                for z in range(2):
                    here = (send_ref[x, y, z] == slot).astype(jnp.int32)
                    held = held + here
                    px = px + here * x
                    py = py + here * y
                    pz = pz + here * z
        places.append((px, py, pz, held))
    return places


def lane_mask(occ_ref, slot, width, plane, shift):
    lane = iota((8, width), 1)
    if plane == 64:
        voxel = lane
        inside = lane >= 0
    else:
        x = lax.shift_right_logical(lane * 205, 14)
        rest = lane - x * plane
        voxel = x * 64 + rest
        inside = rest < 64
    word = lax.shift_right_logical(voxel * 2185, 16)
    bit = voxel - word * 30
    total = jnp.zeros((8, width), jnp.int32)
    for w in range(18):
        total = jnp.where(word == w, occ_ref[slot, w], total)
    on = lax.shift_right_logical(total, bit) & 1
    return jnp.where(inside, on, 0).astype(F32)[:1]


def pack_sends(bricks, send_ref, sign_ref, dirs, plus_ref, minus_ref, y_ref, out_rows):
    channels = bricks.shape[0]
    group = channels // 4
    places = slot_places(send_ref)
    lane = iota((VOX, FACE), 1)
    row = iota((VOX, FACE), 0)
    i = row >> 6
    j = (row >> 3) & 7
    l = row & 7

    def product(targets, match):
        acc = None
        for slot in range(2):
            part = jnp.dot(
                bricks[:, VOX * slot : VOX * slot + VOX],
                one_hot(targets[slot] == match),
                preferred_element_type=F32,
            )
            acc = part if acc is None else acc + part
        return acc

    for side, ref in ((1, plus_ref), (0, minus_ref)):
        faces = []
        ahead = jnp.int32(0)
        for px, py, pz, held in places:
            facing = (px == side).astype(jnp.int32) * held
            target = jnp.where(
                (i == 7 * side) & (facing == 1), ahead * 64 + j * 8 + l, -1
            )
            faces.append(target)
            ahead = ahead + facing
        ref[:channels, :] = product(faces, lane).astype(BF)
        for q in range(dirs):
            col = (sign_ref[q] + 1) >> 1
            edges = []
            for px, py, pz, held in places:
                facing = (px == side) & (py == col) & (held == 1)
                target = jnp.where(
                    (i == 7 * side) & (j == 7 * col) & facing,
                    16 * (1 - side) + pz * 8 + l,
                    -1,
                )
                edges.append(target)
            wide = product(edges, lane & 31)
            packed = jnp.zeros((group, FACE), F32)
            glane = iota((group, FACE), 1) >> 5
            for g in range(4):
                packed = jnp.where(glane == g, wide[group * g : group * g + group], packed)
            ref[channels + group * q : channels + group * q + group, :] = packed.astype(BF)
    for q in range(dirs):
        col = (sign_ref[q] + 1) >> 1
        faces = []
        ahead = jnp.int32(0)
        for px, py, pz, held in places:
            facing = (py == col).astype(jnp.int32) * held
            target = jnp.where(
                (j == 7 * col) & (facing == 1), ahead * 64 + i * 8 + l, -1
            )
            faces.append(target)
            ahead = ahead + facing
        y_ref[q, :, :] = product(faces, lane).astype(BF)


def encode(x, y, z, ok):
    ok = ok & (x >= 0) & (x <= 9) & (y >= 0) & (y <= 9) & (z >= -1) & (z <= 8)
    deep = jnp.where(z < 0, PADDED, jnp.where(z > 7, PADDED + 7, z))
    return jnp.where(ok, x * PLANE + y * 8 + deep, -1)


def fill_targets(t_ref, n, send_ref, near_ref, sign_ref, dirs):
    places = slot_places(send_ref)
    nx, ny, nz, held = places[n]
    row = iota((VOX, FACE), 0)
    for slot in range(2):
        px, py, pz, _ = places[slot]
        t_ref[VOX * slot : VOX * slot + VOX, :] = encode(
            (row >> 6) + 1 + 8 * (px - nx),
            ((row >> 3) & 7) + 1 + 8 * (py - ny),
            (row & 7) + 8 * (pz - nz),
            row >= 0,
        )

    def ranked(offset_of):
        count = jnp.int32(0)
        firsts = [jnp.int32(FAR), jnp.int32(FAR)]
        depths = [jnp.int32(0), jnp.int32(0)]
        for across in range(2):
            for z in range(2):
                there = (near_ref[n, offset_of(across, z)] >= 0).astype(jnp.int32)
                for rank in range(2):
                    take = (there == 1) & (count == rank)
                    firsts[rank] = jnp.where(take, across, firsts[rank])
                    depths[rank] = jnp.where(take, z, depths[rank])
                count = count + there
        return firsts, depths

    row = iota((FACE, FACE), 0)
    high = row >= 64
    u = (row >> 3) & 7
    l = row & 7
    firsts, depths = ranked(
        lambda across, z: 18 * nx + 3 * (across - ny + 1) + (z - nz + 1)
    )
    across = jnp.where(high, firsts[1], firsts[0])
    depth = jnp.where(high, depths[1], depths[0])
    for side in range(2):
        t_ref[1024 + FACE * side : 1024 + FACE * side + FACE, :] = encode(
            jnp.full((FACE, FACE), 9 * side, jnp.int32),
            u + 1 + 8 * (across - ny),
            l + 8 * (depth - nz),
            jnp.broadcast_to(nx == side, (FACE, FACE)),
        )
    firsts, depths = ranked(
        lambda across, z: 9 * (across - nx + 1) + 6 * ny + (z - nz + 1)
    )
    across = jnp.where(high, firsts[1], firsts[0])
    depth = jnp.where(high, depths[1], depths[0])
    for q in range(dirs):
        side = (sign_ref[dirs + q] + 1) >> 1
        at = 1280 + FACE * q
        t_ref[at : at + FACE, :] = encode(
            u + 1 + 8 * (across - nx),
            jnp.zeros((FACE, FACE), jnp.int32) + 9 * side,
            l + 8 * (depth - nz),
            jnp.broadcast_to(ny == side, (FACE, FACE)),
        )
        at = 1280 + FACE * dirs + FACE * q
        e = row & 31
        from_side = e >> 4
        t_ref[at : at + FACE, :] = encode(
            9 * from_side,
            jnp.zeros((FACE, FACE), jnp.int32) + 9 * side,
            (e & 7) + 8 * (((e >> 3) & 1) - nz),
            (from_side == nx) & (ny == side),
        )


def gather_sources(d_ref, own, recv_minus, recv_plus, recv_y, dirs):
    channels = own.shape[0]
    group = channels // 4
    d_ref[:, :1024] = own
    d_ref[:, 1024:1152] = recv_minus[:channels, :]
    d_ref[:, 1152:1280] = recv_plus[:channels, :]
    glane = iota((group, FACE), 1) >> 5
    for q in range(dirs):
        at = 1280 + FACE * q
        d_ref[:, at : at + FACE] = recv_y[q, :channels, :]
        packed = recv_y[q, channels : channels + group, :].astype(F32)
        spread = jnp.concatenate(
            [jnp.where(glane == g, packed, 0.0) for g in range(4)], axis=0
        )
        at = 1280 + FACE * dirs + FACE * q
        d_ref[:, at : at + FACE] = spread.astype(BF)


def fill_padded(d_ref, t_ref, sel_ref, z_refs, send_ref, near_ref, sign_ref, dirs):
    sources = d_ref.shape[1]
    for n in range(2):
        fill_targets(t_ref, n, send_ref, near_ref, sign_ref, dirs)
        parts = []
        for half in range(2):
            for b in range(7):
                sel_ref[:, 128 * b : 128 * b + 128] = one_hot(
                    t_ref[...] == iota((sources, 128), 1) + (PADDED * half + 128 * b)
                )
            if half == 0:
                out = jnp.dot(d_ref[...], sel_ref[...], preferred_element_type=F32)
            else:
                other = VOX * (1 - n)
                out = jnp.dot(
                    d_ref[:, other : other + VOX],
                    sel_ref[other : other + VOX, :],
                    preferred_element_type=F32,
                ) + jnp.dot(
                    d_ref[:, 1024:], sel_ref[1024:, :], preferred_element_type=F32
                )
            parts.append(out)
        middle, ends = parts
        for ref, start, rows in z_refs:
            mid = middle[start : start + rows]
            end = ends[start : start + rows]
            l = iota((rows, PADDED), 1) & 7
            at = slice(PADDED * n, PADDED * n + PADDED)
            ref[1, :, at] = mid.astype(BF)
            ref[0, :, at] = jnp.where(l == 0, end, pltpu.roll(mid, 1, 1)).astype(BF)
            ref[2, :, at] = jnp.where(l == 7, end, pltpu.roll(mid, PADDED - 1, 1)).astype(BF)


def tap_lanes(k, n, flip):
    a, b, c = k // 9, k // 3 % 3, k % 3
    if flip:
        a, b, c = 2 - a, 2 - b, 2 - c
    at = PADDED * n + PLANE * a + 8 * b
    return c, slice(at, at + OUTER)


def fill_patches(p_ref, z_ref, flip):
    channels = z_ref.shape[1]
    for k in range(TAPS):
        for n in range(2):
            c, lanes = tap_lanes(k, n, flip)
            p_ref[channels * k : channels * k + channels, OUTER * n : OUTER * n + OUTER] = z_ref[
                c, :, lanes
            ]


def compaction():
    row = iota((OUTER, VOX), 0)
    x = lax.shift_right_logical(row * 205, 14)
    rest = row - x * PLANE
    return one_hot(jnp.where(rest < 64, x * 64 + rest, -1) == iota((OUTER, VOX), 1))


def mask_outer(occ_ref):
    return jnp.concatenate(
        [lane_mask(occ_ref, n, OUTER, PLANE, 0) for n in range(2)], axis=1
    )


def pack_kernel(dirs, feat_ref, cot_ref, occ_ref, send_ref, sign_ref, own_ref, plus_ref, minus_ref, y_ref):
    for n in range(2):
        mask = lane_mask(occ_ref, n, VOX, 64, 0)
        at = slice(VOX * n, VOX * n + VOX)
        own_ref[:96, at] = jnp.where(mask > 0.5, feat_ref[n].astype(F32), 0.0).astype(BF)
        own_ref[96:, at] = jnp.where(mask > 0.5, cot_ref[n].astype(F32), 0.0).astype(BF)
    pack_sends(own_ref[...], send_ref, sign_ref, dirs, plus_ref, minus_ref, y_ref, 352)


def first_kernel(
    dirs, own_ref, fm_ref, fp_ref, fy_ref, occ_ref, near_ref, send_ref, sign_ref, wat_ref, wb_ref,
    zx_ref, gpre_ref, gout_ref, hid_ref, plus_ref, minus_ref, y_ref,
    d_ref, t_ref, sel_ref, zg_ref, p_ref, acc_ref,
):
    gather_sources(d_ref, own_ref[...], fm_ref, fp_ref, fy_ref, dirs)
    fill_padded(
        d_ref, t_ref, sel_ref, ((zx_ref, 0, 96), (zg_ref, 96, 256)), send_ref, near_ref, sign_ref, dirs
    )
    mask = mask_outer(occ_ref)
    for n in range(2):
        c, lanes = tap_lanes(13, n, False)
        at = slice(OUTER * n, OUTER * n + OUTER)
        gout_ref[:, at] = jnp.where(mask[:, at] > 0.5, zg_ref[c, :, lanes].astype(F32), 0.0).astype(BF)
    fill_patches(p_ref, zx_ref, False)
    pre = jnp.dot(wat_ref[...], p_ref[...], preferred_element_type=F32)
    for k in range(TAPS):
        parts = []
        for n in range(2):
            c, lanes = tap_lanes(k, n, True)
            parts.append(
                jnp.dot(wb_ref[k], zg_ref[c, :, lanes], preferred_element_type=F32)
            )
        both = jnp.concatenate(parts, axis=1)
        if k == 0:
            acc_ref[...] = both
        else:
            acc_ref[...] += both
    pre = pre * mask
    gate = 1.0 / (1.0 + jnp.exp(-pre))
    hidden = (pre * gate).astype(BF)
    grad_pre = (acc_ref[...] * gate * (1.0 + pre * (1.0 - gate)) * mask).astype(BF)
    gpre_ref[...] = grad_pre
    squeeze = compaction()
    for n in range(2):
        at = slice(OUTER * n, OUTER * n + OUTER)
        to = slice(VOX * n, VOX * n + VOX)
        hid_ref[:96, to] = jnp.dot(hidden[:, at], squeeze, preferred_element_type=F32).astype(BF)
        hid_ref[96:, to] = jnp.dot(grad_pre[:, at], squeeze, preferred_element_type=F32).astype(BF)
    pack_sends(hid_ref[...], send_ref, sign_ref, dirs, plus_ref, minus_ref, y_ref, 192)


NT = (((1,), (1,)), ((), ()))


def weight_a_kernel(scale, zx_ref, gpre_ref, out_ref, p_ref):
    fill_patches(p_ref, zx_ref, False)
    out_ref[...] = scale * lax.dot_general(
        p_ref[...], gpre_ref[...], NT, preferred_element_type=F32
    )


def weight_b_kernel(
    scale, dirs, own_ref, fm_ref, fp_ref, fy_ref, near_ref, send_ref, sign_ref, gout_ref,
    out_ref, zh_ref, zp_ref, d_ref, t_ref, sel_ref, p_ref,
):
    gather_sources(d_ref, own_ref[...], fm_ref, fp_ref, fy_ref, dirs)
    fill_padded(
        d_ref, t_ref, sel_ref, ((zh_ref, 0, 96), (zp_ref, 96, 96)), send_ref, near_ref, sign_ref, dirs
    )
    fill_patches(p_ref, zh_ref, False)
    rows = TAPS * 96
    out_ref[:rows, :] = scale * lax.dot_general(
        p_ref[...], gout_ref[...], NT, preferred_element_type=F32
    )
    out_ref[rows:, :] = jnp.zeros((out_ref.shape[0] - rows, 256), F32)


def last_kernel(occ_ref, zh_ref, zp_ref, wbt_ref, wag_ref, out_ref, grad_ref, p_ref):
    mask = mask_outer(occ_ref)
    squeeze = compaction()
    fill_patches(p_ref, zh_ref, False)
    out = (jnp.dot(wbt_ref[...], p_ref[...], preferred_element_type=F32) * mask).astype(BF)
    for n in range(2):
        at = slice(OUTER * n, OUTER * n + OUTER)
        out_ref[n] = jnp.dot(out[:, at], squeeze, preferred_element_type=F32).astype(BF)
    fill_patches(p_ref, zp_ref, True)
    grad = (jnp.dot(wag_ref[...], p_ref[...], preferred_element_type=F32) * mask).astype(BF)
    for n in range(2):
        at = slice(OUTER * n, OUTER * n + OUTER)
        grad_ref[n] = jnp.dot(grad[:, at], squeeze, preferred_element_type=F32).astype(BF)


def call(kernel, outs, ins, scratch=(), flops=0, moved=0):
    specs = [SMEM if jnp.issubdtype(x.dtype, jnp.integer) else VMEM for x in ins]
    return pl.pallas_call(
        kernel,
        out_shape=[jax.ShapeDtypeStruct(s, d) for s, d in outs],
        in_specs=specs,
        out_specs=[VMEM] * len(outs),
        scratch_shapes=[pltpu.VMEM(s, d) for s, d in scratch],
        compiler_params=pltpu.CompilerParams(vmem_limit_bytes=LIMIT),
        cost_estimate=pl.CostEstimate(flops=flops, bytes_accessed=moved, transcendentals=0),
    )(*ins)


def exchange(channels, plus, minus, faces, count_x, count_y):
    up = [(k, k + 1) for k in range(count_x - 1)]
    down = [(k + 1, k) for k in range(count_x - 1)]
    from_minus = lax.ppermute(plus, "gx", up)
    from_plus = lax.ppermute(minus, "gx", down)
    group = channels // 4
    dirs = faces.shape[0]
    if dirs == 1:
        perms = [[(0, 1), (1, 0)]]
    else:
        perms = [
            [(k, k + 1) for k in range(count_y - 1)],
            [(k + 1, k) for k in range(count_y - 1)],
        ]
    arrived = []
    for q in range(dirs):
        at = channels + group * q
        edges = from_minus[at : at + group] + from_plus[at : at + group]
        arrived.append(
            lax.ppermute(jnp.concatenate([faces[q], edges], axis=0), "gy", perms[q])
        )
    return from_minus, from_plus, jnp.stack(arrived, axis=0)


def sum_region(value, count_x, count_y):
    if count_x != 4 or count_y != 2:
        return lax.psum(value, ("gx", "gy"))
    gx = lax.axis_index("gx")
    bits = {"c": gx & 1, "y": gx >> 1, "x": lax.axis_index("gy")}
    perms = {
        "c": ("gx", [(k, k ^ 1) for k in range(4)]),
        "y": ("gx", [(k, k ^ 2) for k in range(4)]),
        "x": ("gy", [(0, 1), (1, 0)]),
    }
    half = value.shape[1] // 2
    pieces = [(value[:, :half], "cyx"), (value[:, half:], "cxy")]
    parts = []
    for piece, order in pieces:
        for step in order:
            rows = piece.shape[0] // 2
            low, high = piece[:rows], piece[rows:]
            sent = jnp.where(bits[step] == 0, high, low).astype(BF)
            kept = jnp.where(bits[step] == 0, low, high)
            piece = kept + lax.ppermute(sent, *perms[step]).astype(F32)
        piece = piece.astype(BF)
        for step in order[::-1]:
            other = lax.ppermute(piece, *perms[step])
            first = bits[step] == 0
            piece = jnp.concatenate(
                [jnp.where(first, piece, other), jnp.where(first, other, piece)], axis=0
            )
        parts.append(piece.astype(F32))
    return jnp.concatenate(parts, axis=1)


def body(features, occupancy, neighbours, send_slots, weight_a, weight_b, cotangent):
    count_x = lax.axis_size("gx")
    count_y = lax.axis_size("gy")
    dirs = 1 if count_y == 2 else 2
    if dirs == 1:
        toward = 1 - 2 * lax.axis_index("gy")
        signs = jnp.stack([toward, toward]).astype(jnp.int32)
    else:
        signs = jnp.array([1, -1, -1, 1], jnp.int32)
    scale = float(features.shape[0] * VOX * count_x * count_y) ** -0.5
    sources = 1280 + 2 * FACE * dirs
    wat = weight_a.transpose(2, 0, 1).reshape(96, TAPS * 96)
    wag = weight_a.transpose(1, 0, 2).reshape(96, TAPS * 96)
    wbt = weight_b.transpose(2, 0, 1).reshape(256, TAPS * 96)

    rows = 352 + 88 * dirs
    own, plus, minus, faces = call(
        functools.partial(pack_kernel, dirs),
        [((352, 1024), BF), ((rows, FACE), BF), ((rows, FACE), BF), ((dirs, 352, FACE), BF)],
        [features, cotangent, occupancy, send_slots, signs],
        flops=352 * 1024 * 1024,
        moved=2 * 1024 * 1024,
    )
    from_minus, from_plus, from_y = exchange(352, plus, minus, faces, count_x, count_y)

    rows = 192 + 48 * dirs
    zx, gpre, gout, hid, plus, minus, faces = call(
        functools.partial(first_kernel, dirs),
        [
            ((3, 96, 2 * PADDED), BF),
            ((96, 2 * OUTER), BF),
            ((256, 2 * OUTER), BF),
            ((192, 1024), BF),
            ((rows, FACE), BF),
            ((rows, FACE), BF),
            ((dirs, 192, FACE), BF),
        ],
        [own, from_minus, from_plus, from_y, occupancy, neighbours, send_slots, signs, wat, weight_b],
        [
            ((352, sources), BF),
            ((sources, 128), jnp.int32),
            ((sources, PADDED), BF),
            ((3, 256, 2 * PADDED), BF),
            ((TAPS * 96, 2 * OUTER), BF),
            ((96, 2 * OUTER), F32),
        ],
        flops=5 * 10**9,
        moved=8 * 1024 * 1024,
    )
    from_minus, from_plus, from_y = exchange(192, plus, minus, faces, count_x, count_y)
    (grad_wa,) = call(
        functools.partial(weight_a_kernel, scale),
        [((TAPS * 96, 96), F32)],
        [zx, gpre],
        [((TAPS * 96, 2 * OUTER), BF)],
        flops=10**9,
        moved=2 * 1024 * 1024,
    )
    grad_wb, zh, zp = call(
        functools.partial(weight_b_kernel, scale, dirs),
        [((2688, 256), F32), ((3, 96, 2 * PADDED), BF), ((3, 96, 2 * PADDED), BF)],
        [hid, from_minus, from_plus, from_y, neighbours, send_slots, signs, gout],
        [
            ((192, sources), BF),
            ((sources, 128), jnp.int32),
            ((sources, PADDED), BF),
            ((TAPS * 96, 2 * OUTER), BF),
        ],
        flops=2 * 10**9,
        moved=4 * 1024 * 1024,
    )
    grad_wa = lax.psum(grad_wa, ("gx", "gy")).reshape(TAPS, 96, 96)
    layer_out, grad_features = call(
        last_kernel,
        [((2, 256, VOX), BF), ((2, 96, VOX), BF)],
        [occupancy, zh, zp, wbt, wag],
        [((TAPS * 96, 2 * OUTER), BF)],
        flops=3 * 10**9,
        moved=6 * 1024 * 1024,
    )
    grad_wb = sum_region(grad_wb, count_x, count_y)[: TAPS * 96].reshape(TAPS, 96, 256)
    return layer_out, grad_features, grad_wa, grad_wb


def solution(mesh):
    in_specs = (
        P(("dp", "gx", "gy"), None, None),
        P(("dp", "gx", "gy"), None),
        P(("dp", "gx", "gy"), None),
        P(("dp", "gx"), "gy", None),
        P(),
        P(),
        P(("dp", "gx", "gy"), None, None),
    )
    out_specs = (
        P(("dp", "gx", "gy"), None, None),
        P(("dp", "gx", "gy"), None, None),
        P("dp", None, None),
        P("dp", None, None),
    )
    return jax.shard_map(body, mesh=mesh, in_specs=in_specs, out_specs=out_specs, check_vma=False)
```

profile of v0, /device:TPU:0, one launch (start us, length us, event | category | flops | bytes accessed | tf_op | source)
XLA Modules:
  0.0 149.1 jit_solution(16645826865051033549)
XLA Ops:
  7.2 0.6 pad_add_fusion.sign_ref
  7.8 3.2 %shard_map.102 = (bf16[352,1024]{1,0:T(8,128)(2,1)}, bf16[440,128]{1,0:T(8,128)(2,1)}, bf16[440,128]{1,0:T(8,128)(2,1)}, bf16[1,352,128]{2,1,0:T(8,128)(2,1)}) custom-call(bf16[2,96,512]{2,1,0:T(8,128)(2,1)} %feat_ref.1, bf16[2,256,512]{2,1,0:T(8,128)(2,1)} %cot_ref.1, s32[2,18]{1,0:T(2,128)} %occ_ref.5, s32[2,2,2]{2,1,0:T(2,128)} %send_ref.5, ...), custom_call_target="tpu_custom_call" | custom-call | flops 369098752 | bytes 2097152 | tf_op jit(solution)/shard_map/pallas_call | solution.py:382
  11.0 2.4 %collective-permute-start = (bf16[440,128]{1,0:T(8,128)(2,1)}, bf16[440,128]{1,0:T(8,128)(2,1)S(1)}, u32[]{:S(2)}, u32[]{:S(2)}) collective-permute-start(bf16[440,128]{1,0:T(8,128)(2,1)} %get-tuple-element.21), channel_id=1, source_target_pairs={{0,2},{2,4},{4,6},{1,3},{3,5},{5,7},{8,10},{10,12},{12,14},{9,11},... | collective-permute-start | bytes 337928 | tf_op jit(solution)/shard_map/ppermute | solution.py:396
  13.4 1.3 collective-permute-start.1
  14.7 4.2 %collective-permute-done.1.fp_ref = bf16[440,128]{1,0:T(8,128)(2,1)S(1)} collective-permute-done((bf16[440,128]{1,0:T(8,128)(2,1)}, bf16[440,128]{1,0:T(8,128)(2,1)S(1)}, u32[]{:S(2)}, u32[]{:S(2)}) %collective-permute-start.1) | collective-permute-done | bytes 112672 | tf_op jit(solution)/shard_map/ppermute | solution.py:397
  18.9 0.9 pad_maximum_fusion.6
  19.9 1.5 %collective-permute-start.2 = (bf16[440,128]{1,0:T(8,128)(2,1)S(1)}, bf16[440,128]{1,0:T(8,128)(2,1)S(1)}, u32[]{:S(2)}, u32[]{:S(2)}) collective-permute-start(bf16[440,128]{1,0:T(8,128)(2,1)S(1)} %pad_maximum_fusion.6), channel_id=1, source_target_pairs={{0,1},{1,0},{2,3},{3,2},{4,5},{5,4},{6,7},{7,6},{8,9},{9,8},{10,11... | collective-permute-start | bytes 337928 | tf_op jit(solution)/shard_map/ppermute | solution.py:412
  21.4 2.1 %copy.14.wat_ref = bf16[96,2592]{1,0:T(8,128)(2,1)} copy(bf16[96,2592]{0,1:T(8,128)(2,1)} %bitcast.17) | data formatting | bytes 995328 | tf_op jit(solution)/shard_map/reshape | solution.py:459
  23.5 1.1 collective-permute-done.2
  24.7 0.6 copy-done.7
  25.3 17.3 %shard_map.103 = (bf16[3,96,1792]{2,1,0:T(8,128)(2,1)}, bf16[96,1280]{1,0:T(8,128)(2,1)}, bf16[256,1280]{1,0:T(8,128)(2,1)}, bf16[192,1024]{1,0:T(8,128)(2,1)}, ...) custom-call(bf16[352,1024]{1,0:T(8,128)(2,1)} %get-tuple-element.20.own_ref, ...), custom_call_target="tpu_custom_call" | custom-call | flops 5000000000 | bytes 8388608 | tf_op jit(solution)/shard_map/pallas_call | solution.py:382
  42.6 4.2 %collective-permute-start.3 = (bf16[240,128]{1,0:T(8,128)(2,1)}, bf16[240,128]{1,0:T(8,128)(2,1)S(1)}, u32[]{:S(2)}, u32[]{:S(2)}) collective-permute-start(bf16[240,128]{1,0:T(8,128)(2,1)} %get-tuple-element.25), channel_id=1, source_target_pairs={{0,2},{2,4},{4,6},{1,3},{3,5},{5,7},{8,10},{10,12},{12,14},{9,11},... | collective-permute-start | bytes 184328 | tf_op jit(solution)/shard_map/ppermute | solution.py:396
  46.9 1.3 collective-permute-start.4
  48.2 2.7 %collective-permute-done.4.fp_ref = bf16[240,128]{1,0:T(8,128)(2,1)S(1)} collective-permute-done((bf16[240,128]{1,0:T(8,128)(2,1)}, bf16[240,128]{1,0:T(8,128)(2,1)S(1)}, u32[]{:S(2)}, u32[]{:S(2)}) %collective-permute-start.4) | collective-permute-done | bytes 61472 | tf_op jit(solution)/shard_map/ppermute | solution.py:397
  50.9 0.8 pad_maximum_fusion.7
  51.7 1.5 collective-permute-start.5
  53.2 1.6 %copy.16.wbt_ref = bf16[256,2592]{1,0:T(8,128)(2,1)} copy(bf16[256,2592]{0,1:T(8,128)(2,1)S(1)} %bitcast.21) | data formatting | bytes 2654208 | tf_op jit(solution)/shard_map/reshape | solution.py:461
  54.9 0.3 copy.15
  55.2 1.1 copy.17.wag_ref
  56.3 0.6 copy-done.8
  56.9 11.1 %shard_map.104 = (f32[2688,256]{1,0:T(8,128)}, bf16[3,96,1792]{2,1,0:T(8,128)(2,1)}, bf16[3,96,1792]{2,1,0:T(8,128)(2,1)}) custom-call(bf16[192,1024]{1,0:T(8,128)(2,1)} %get-tuple-element.24.own_ref, bf16[240,128]{1,0:T(8,128)(2,1)} %copy-done.5, bf16[240,128]{1,0:T(8,128)(2,1)} %copy-done.6, bf16[1,240,128]{2,1,0:T(8,128)(2,1)} %bitcast.25, ...), custom_call_target="tpu_custom_call" | custom-call | flops 2000000000 | bytes 4194304 | tf_op jit(solution)/shard_map/pallas_call | solution.py:382
  68.1 1.8 %select_convert_fusion.1 = (bf16[1344,128]{1,0:T(8,128)(2,1)S(1)}, bf16[1344,128]{1,0:T(8,128)(2,1)S(1)}) fusion(f32[2688,256]{1,0:T(8,128)} %get-tuple-element.35, pred[]{:T(512)S(6)} %eq.6), kind=kLoop, calls=%fused_computation.6 | loop fusion | flops 344064 | bytes 2064385 | tf_op jit(solution)/shard_map/convert_element_type | solution.py:434
  69.9 2.7 %collective-permute-start.12 = (bf16[1344,128]{1,0:T(8,128)(2,1)S(1)}, bf16[1344,128]{1,0:T(8,128)(2,1)S(1)}, u32[]{:S(2)}, u32[]{:S(2)}) collective-permute-start(bf16[1344,128]{1,0:T(8,128)(2,1)S(1)} %get-tuple-element.39), channel_id=1, source_target_pairs={{0,2},{2,0},{4,6},{6,4},{1,3},{3,1},{5,7},{7,5},{8,10},{10,8},{12,... | collective-permute-start | bytes 1032200 | tf_op jit(solution)/shard_map/ppermute | solution.py:436
  72.7 5.2 %shard_map.106 = f32[2592,96]{1,0:T(8,128)} custom-call(bf16[3,96,1792]{2,1,0:T(8,128)(2,1)} %get-tuple-element.33.zx_ref, bf16[96,1280]{1,0:T(8,128)(2,1)} %get-tuple-element.34.gpre_ref), custom_call_target="tpu_custom_call" | custom-call | flops 1000000000 | bytes 2097152 | tf_op jit(solution)/shard_map/pallas_call | solution.py:382
  78.0 8.2 %shard_map.105 = (bf16[2,256,512]{2,1,0:T(8,128)(2,1)}, bf16[2,96,512]{2,1,0:T(8,128)(2,1)}) custom-call(s32[2,18]{1,0:T(2,128)} %occ_ref.5, bf16[3,96,1792]{2,1,0:T(8,128)(2,1)} %get-tuple-element.29.zh_ref, bf16[3,96,1792]{2,1,0:T(8,128)(2,1)} %get-tuple-element.30.zp_ref, bf16[256,2592]{1,0:T(8,128)(2,1)} %copy.16.wbt_ref, bf16[96,2592]{1,0:T(8,128)(2,1)} %copy.17.wag_ref), custom_call_target="tpu_custom_call" | custom-call | flops 3000000000 | bytes 6291456 | tf_op jit(solution)/shard_map/pallas_call | solution.py:382
  86.2 0.2 convert_add_fusion.1
  86.4 0.7 collective-permute-start.7
  87.2 1.2 collective-permute-start.13
  88.4 7.9 %collective-permute-done.7 = bf16[672,128]{1,0:T(8,128)(2,1)S(1)} collective-permute-done((bf16[672,128]{1,0:T(8,128)(2,1)S(1)}, bf16[672,128]{1,0:T(8,128)(2,1)S(1)}, u32[]{:S(2)}, u32[]{:S(2)}) %collective-permute-start.7) | collective-permute-done | bytes 172064 | tf_op jit(solution)/shard_map/ppermute | solution.py:436
  96.4 0.4 collective-permute-start.8
  97.0 1.5 collective-permute-start.14
  98.4 2.6 %collective-permute-done.8 = bf16[336,128]{1,0:T(8,128)(2,1)S(1)} collective-permute-done((bf16[336,128]{1,0:T(8,128)(2,1)S(1)}, bf16[336,128]{1,0:T(8,128)(2,1)S(1)}, u32[]{:S(2)}, u32[]{:S(2)}) %collective-permute-start.8) | collective-permute-done | bytes 86048 | tf_op jit(solution)/shard_map/ppermute | solution.py:436
  101.1 0.4 collective-permute-start.9
  101.6 1.5 collective-permute-start.15
  103.0 4.2 %collective-permute-done.9 = bf16[336,128]{1,0:T(8,128)(2,1)S(1)} collective-permute-done((bf16[336,128]{1,0:T(8,128)(2,1)S(1)}, bf16[336,128]{1,0:T(8,128)(2,1)S(1)}, u32[]{:S(2)}, u32[]{:S(2)}) %collective-permute-start.9) | collective-permute-done | bytes 86048 | tf_op jit(solution)/shard_map/ppermute | solution.py:439
  107.3 0.2 collective-permute-done.15
  107.6 2.1 %collective-permute-start.16 = (bf16[672,128]{1,0:T(8,128)(2,1)S(1)}, bf16[672,128]{1,0:T(8,128)(2,1)S(1)}, u32[]{:S(2)}, u32[]{:S(2)}) collective-permute-start(bf16[672,128]{1,0:T(8,128)(2,1)S(1)} %pad_maximum_fusion.5), channel_id=1, source_target_pairs={{0,1},{1,0},{2,3},{3,2},{4,5},{5,4},{6,7},{7,6},{8,9},{9,8},{10,11... | collective-permute-start | bytes 516104 | tf_op jit(solution)/shard_map/ppermute | solution.py:439
  109.7 3.1 %collective-permute-done.10 = bf16[672,128]{1,0:T(8,128)(2,1)S(1)} collective-permute-done((bf16[672,128]{1,0:T(8,128)(2,1)S(1)}, bf16[672,128]{1,0:T(8,128)(2,1)S(1)}, u32[]{:S(2)}, u32[]{:S(2)}) %collective-permute-start.10) | collective-permute-done | bytes 172064 | tf_op jit(solution)/shard_map/ppermute | solution.py:439
  112.9 0.2 collective-permute-done.16
  113.2 0.4 collective-permute-start.17
  113.6 1.0 collective-permute-done.11
  114.5 0.2 broadcast_select_fusion.3
  114.7 0.3 collective-permute-done.17
  115.0 0.2 broadcast_select_fusion.1
  115.2 0.1 fusion
  115.4 1.8 %convert.3 = f32[27,96,256]{2,1,0:T(8,128)} convert(bf16[27,96,256]{2,1,0:T(8,128)(2,1)S(1)} %bitcast.16) | non-fusion elementwise | flops 663552 | bytes 3981312 | tf_op jit(solution)/shard_map/reshape | solution.py:528
  117.2 22.6 %all-reduce.2.cloned.1.call-done = f32[27,96,96]{2,1,0:T(8,128)} async-done(((f32[27,96,96]{2,1,0:T(8,128)}), f32[27,96,96]{2,1,0:T(8,128)}) %all-reduce.2.cloned.1.call-update) | async-done | bytes 995344 | tf_op jit(solution)/shard_map/psum | solution.py:519
  139.8 2.5 %copy.19 = f32[27,96,96]{2,1,0:T(8,128)} copy(f32[27,96,96]{2,1,0:T(8,128)} %all-reduce.2.cloned.1.call-done) | data formatting | bytes 1990656
  (46 shorter events, 0.9 us)
Async XLA Ops:
  7.2 132.6 %all-reduce.2.cloned.1.call-start = ((), (), s32[]{:S(2)}) async-start(), calls=%async_computation | async-start | bytes 2654208 | tf_op jit(solution)/shard_map/psum | solution.py:519
  11.0 3.7 %collective-permute-start = (bf16[440,128]{1,0:T(8,128)(2,1)}, bf16[440,128]{1,0:T(8,128)(2,1)S(1)}, u32[]{:S(2)}, u32[]{:S(2)}) collective-permute-start(bf16[440,128]{1,0:T(8,128)(2,1)} %get-tuple-element.21), channel_id=1, source_target_pairs={{0,2},{2,4},{4,6},{1,3},{3,5},{5,7},{8,10},{10,12},{12,14},{9,11},... | collective-permute-start | bytes 337928 | tf_op jit(solution)/shard_map/ppermute | solution.py:396
  13.4 5.6 %collective-permute-start.1 = (bf16[440,128]{1,0:T(8,128)(2,1)}, bf16[440,128]{1,0:T(8,128)(2,1)S(1)}, u32[]{:S(2)}, u32[]{:S(2)}) collective-permute-start(bf16[440,128]{1,0:T(8,128)(2,1)} %get-tuple-element.22), channel_id=1, source_target_pairs={{2,0},{4,2},{6,4},{3,1},{5,3},{7,5},{10,8},{12,10},{14,12},{11,9},... | collective-permute-start | bytes 337928 | tf_op jit(solution)/shard_map/ppermute | solution.py:397
  14.7 10.0 %copy-start.3 = (bf16[440,128]{1,0:T(8,128)(2,1)}, bf16[440,128]{1,0:T(8,128)(2,1)S(1)}, u32[]{:S(2)}) copy-start(bf16[440,128]{1,0:T(8,128)(2,1)S(1)} %collective-permute-done.fm_ref) | copy-start | bytes 337924
  18.9 5.7 %copy-start.4 = (bf16[440,128]{1,0:T(8,128)(2,1)}, bf16[440,128]{1,0:T(8,128)(2,1)S(1)}, u32[]{:S(2)}) copy-start(bf16[440,128]{1,0:T(8,128)(2,1)S(1)} %collective-permute-done.1.fp_ref) | copy-start | bytes 337924
  19.9 4.8 %collective-permute-start.2 = (bf16[440,128]{1,0:T(8,128)(2,1)S(1)}, bf16[440,128]{1,0:T(8,128)(2,1)S(1)}, u32[]{:S(2)}, u32[]{:S(2)}) collective-permute-start(bf16[440,128]{1,0:T(8,128)(2,1)S(1)} %pad_maximum_fusion.6), channel_id=1, source_target_pairs={{0,1},{1,0},{2,3},{3,2},{4,5},{5,4},{6,7},{7,6},{8,9},{9,8},{10,11... | collective-permute-start | bytes 337928 | tf_op jit(solution)/shard_map/ppermute | solution.py:412
  24.6 0.7 copy-start.7
  25.3 27.9 %copy-start.2 = (bf16[27,96,256]{2,1,0:T(8,128)(2,1)S(1)}, bf16[27,96,256]{2,1,0:T(8,128)(2,1)}, u32[]{:S(2)}) copy-start(bf16[27,96,256]{2,1,0:T(8,128)(2,1)} %wb_ref.1) | copy-start | bytes 3981316
  42.6 12.2 %copy-start.1 = (bf16[27,96,96]{2,1,0:T(8,128)(2,1)S(1)}, bf16[27,96,96]{2,1,0:T(8,128)(2,1)}, u32[]{:S(2)}) copy-start(bf16[27,96,96]{2,1,0:T(8,128)(2,1)} %param.11) | copy-start | bytes 1492996
  42.6 5.6 %collective-permute-start.3 = (bf16[240,128]{1,0:T(8,128)(2,1)}, bf16[240,128]{1,0:T(8,128)(2,1)S(1)}, u32[]{:S(2)}, u32[]{:S(2)}) collective-permute-start(bf16[240,128]{1,0:T(8,128)(2,1)} %get-tuple-element.25), channel_id=1, source_target_pairs={{0,2},{2,4},{4,6},{1,3},{3,5},{5,7},{8,10},{10,12},{12,14},{9,11},... | collective-permute-start | bytes 184328 | tf_op jit(solution)/shard_map/ppermute | solution.py:396
  46.9 4.0 %collective-permute-start.4 = (bf16[240,128]{1,0:T(8,128)(2,1)}, bf16[240,128]{1,0:T(8,128)(2,1)S(1)}, u32[]{:S(2)}, u32[]{:S(2)}) collective-permute-start(bf16[240,128]{1,0:T(8,128)(2,1)} %get-tuple-element.26), channel_id=1, source_target_pairs={{2,0},{4,2},{6,4},{3,1},{5,3},{7,5},{10,8},{12,10},{14,12},{11,9},... | collective-permute-start | bytes 184328 | tf_op jit(solution)/shard_map/ppermute | solution.py:397
  48.2 8.1 %copy-start.5 = (bf16[240,128]{1,0:T(8,128)(2,1)}, bf16[240,128]{1,0:T(8,128)(2,1)S(1)}, u32[]{:S(2)}) copy-start(bf16[240,128]{1,0:T(8,128)(2,1)S(1)} %collective-permute-done.3.fm_ref) | copy-start | bytes 184324
  50.9 5.4 %copy-start.6 = (bf16[240,128]{1,0:T(8,128)(2,1)}, bf16[240,128]{1,0:T(8,128)(2,1)S(1)}, u32[]{:S(2)}) copy-start(bf16[240,128]{1,0:T(8,128)(2,1)S(1)} %collective-permute-done.4.fp_ref) | copy-start | bytes 184324
  51.7 4.6 %collective-permute-start.5 = (bf16[240,128]{1,0:T(8,128)(2,1)S(1)}, bf16[240,128]{1,0:T(8,128)(2,1)S(1)}, u32[]{:S(2)}, u32[]{:S(2)}) collective-permute-start(bf16[240,128]{1,0:T(8,128)(2,1)S(1)} %pad_maximum_fusion.7), channel_id=1, source_target_pairs={{0,1},{1,0},{2,3},{3,2},{4,5},{5,4},{6,7},{7,6},{8,9},{9,8},{10,11... | collective-permute-start | bytes 184328 | tf_op jit(solution)/shard_map/ppermute | solution.py:412
  56.3 0.6 copy-start.8
  69.9 16.3 %collective-permute-start.12 = (bf16[1344,128]{1,0:T(8,128)(2,1)S(1)}, bf16[1344,128]{1,0:T(8,128)(2,1)S(1)}, u32[]{:S(2)}, u32[]{:S(2)}) collective-permute-start(bf16[1344,128]{1,0:T(8,128)(2,1)S(1)} %get-tuple-element.39), channel_id=1, source_target_pairs={{0,2},{2,0},{4,6},{6,4},{1,3},{3,1},{5,7},{7,5},{8,10},{10,8},{12,... | collective-permute-start | bytes 1032200 | tf_op jit(solution)/shard_map/ppermute | solution.py:436
  72.6 13.6 %collective-permute-start.6 = (bf16[1344,128]{1,0:T(8,128)(2,1)S(1)}, bf16[1344,128]{1,0:T(8,128)(2,1)S(1)}, u32[]{:S(2)}, u32[]{:S(2)}) collective-permute-start(bf16[1344,128]{1,0:T(8,128)(2,1)S(1)} %get-tuple-element.38), channel_id=1, source_target_pairs={{0,2},{2,0},{4,6},{6,4},{1,3},{3,1},{5,7},{7,5},{8,10},{10,8},{12,... | collective-permute-start | bytes 1032200 | tf_op jit(solution)/shard_map/ppermute | solution.py:436
  77.9 8.3 %copy-start = (f32[2688,256]{1,0:T(8,128)S(1)}, f32[2688,256]{1,0:T(8,128)}, u32[]{:S(2)}) copy-start(f32[2688,256]{1,0:T(8,128)} %get-tuple-element.35) | copy-start | bytes 8257540
  86.4 9.9 %collective-permute-start.7 = (bf16[672,128]{1,0:T(8,128)(2,1)S(1)}, bf16[672,128]{1,0:T(8,128)(2,1)S(1)}, u32[]{:S(2)}, u32[]{:S(2)}) collective-permute-start(bf16[672,128]{1,0:T(8,128)(2,1)S(1)} %select_convert_fusion.3), channel_id=1, source_target_pairs={{0,4},{2,6},{4,0},{6,2},{1,5},{3,7},{5,1},{7,3},{8,12},{10,14},{12... | collective-permute-start | bytes 516104 | tf_op jit(solution)/shard_map/ppermute | solution.py:436
  87.2 9.7 %collective-permute-start.13 = (bf16[672,128]{1,0:T(8,128)(2,1)S(1)}, bf16[672,128]{1,0:T(8,128)(2,1)S(1)}, u32[]{:S(2)}, u32[]{:S(2)}) collective-permute-start(bf16[672,128]{1,0:T(8,128)(2,1)S(1)} %select_convert_fusion.2), channel_id=1, source_target_pairs={{0,1},{1,0},{2,3},{3,2},{4,5},{5,4},{6,7},{7,6},{8,9},{9,8},{10,11... | collective-permute-start | bytes 516104 | tf_op jit(solution)/shard_map/ppermute | solution.py:436
  96.4 4.6 %collective-permute-start.8 = (bf16[336,128]{1,0:T(8,128)(2,1)S(1)}, bf16[336,128]{1,0:T(8,128)(2,1)S(1)}, u32[]{:S(2)}, u32[]{:S(2)}) collective-permute-start(bf16[336,128]{1,0:T(8,128)(2,1)S(1)} %select_convert_fusion.5), channel_id=1, source_target_pairs={{0,1},{1,0},{2,3},{3,2},{4,5},{5,4},{6,7},{7,6},{8,9},{9,8},{10,11... | collective-permute-start | bytes 258056 | tf_op jit(solution)/shard_map/ppermute | solution.py:436
  97.0 4.6 %collective-permute-start.14 = (bf16[336,128]{1,0:T(8,128)(2,1)S(1)}, bf16[336,128]{1,0:T(8,128)(2,1)S(1)}, u32[]{:S(2)}, u32[]{:S(2)}) collective-permute-start(bf16[336,128]{1,0:T(8,128)(2,1)S(1)} %select_convert_fusion.4), channel_id=1, source_target_pairs={{0,4},{2,6},{4,0},{6,2},{1,5},{3,7},{5,1},{7,3},{8,12},{10,14},{12... | collective-permute-start | bytes 258056 | tf_op jit(solution)/shard_map/ppermute | solution.py:436
  101.1 6.1 %collective-permute-start.9 = (bf16[336,128]{1,0:T(8,128)(2,1)S(1)}, bf16[336,128]{1,0:T(8,128)(2,1)S(1)}, u32[]{:S(2)}, u32[]{:S(2)}) collective-permute-start(bf16[336,128]{1,0:T(8,128)(2,1)S(1)} %add_convert_fusion.1), channel_id=1, source_target_pairs={{0,1},{1,0},{2,3},{3,2},{4,5},{5,4},{6,7},{7,6},{8,9},{9,8},{10,11... | collective-permute-start | bytes 258056 | tf_op jit(solution)/shard_map/ppermute | solution.py:439
  101.6 6.0 %collective-permute-start.15 = (bf16[336,128]{1,0:T(8,128)(2,1)S(1)}, bf16[336,128]{1,0:T(8,128)(2,1)S(1)}, u32[]{:S(2)}, u32[]{:S(2)}) collective-permute-start(bf16[336,128]{1,0:T(8,128)(2,1)S(1)} %add_convert_fusion), channel_id=1, source_target_pairs={{0,4},{2,6},{4,0},{6,2},{1,5},{3,7},{5,1},{7,3},{8,12},{10,14},{12... | collective-permute-start | bytes 258056 | tf_op jit(solution)/shard_map/ppermute | solution.py:439
  107.2 5.5 %collective-permute-start.10 = (bf16[672,128]{1,0:T(8,128)(2,1)S(1)}, bf16[672,128]{1,0:T(8,128)(2,1)S(1)}, u32[]{:S(2)}, u32[]{:S(2)}) collective-permute-start(bf16[672,128]{1,0:T(8,128)(2,1)S(1)} %pad_maximum_fusion.4), channel_id=1, source_target_pairs={{0,4},{2,6},{4,0},{6,2},{1,5},{3,7},{5,1},{7,3},{8,12},{10,14},{12... | collective-permute-start | bytes 516104 | tf_op jit(solution)/shard_map/ppermute | solution.py:439
  107.6 5.5 %collective-permute-start.16 = (bf16[672,128]{1,0:T(8,128)(2,1)S(1)}, bf16[672,128]{1,0:T(8,128)(2,1)S(1)}, u32[]{:S(2)}, u32[]{:S(2)}) collective-permute-start(bf16[672,128]{1,0:T(8,128)(2,1)S(1)} %pad_maximum_fusion.5), channel_id=1, source_target_pairs={{0,1},{1,0},{2,3},{3,2},{4,5},{5,4},{6,7},{7,6},{8,9},{9,8},{10,11... | collective-permute-start | bytes 516104 | tf_op jit(solution)/shard_map/ppermute | solution.py:439
  112.8 1.7 %collective-permute-start.11 = (bf16[1344,128]{1,0:T(8,128)(2,1)S(1)}, bf16[1344,128]{1,0:T(8,128)(2,1)S(1)}, u32[]{:S(2)}, u32[]{:S(2)}) collective-permute-start(bf16[1344,128]{1,0:T(8,128)(2,1)S(1)} %pad_maximum_fusion.2), channel_id=1, source_target_pairs={{0,2},{2,0},{4,6},{6,4},{1,3},{3,1},{5,7},{7,5},{8,10},{10,8},{12,... | collective-permute-start | bytes 1032200 | tf_op jit(solution)/shard_map/ppermute | solution.py:439
  113.2 1.9 %collective-permute-start.17 = (bf16[1344,128]{1,0:T(8,128)(2,1)S(1)}, bf16[1344,128]{1,0:T(8,128)(2,1)S(1)}, u32[]{:S(2)}, u32[]{:S(2)}) collective-permute-start(bf16[1344,128]{1,0:T(8,128)(2,1)S(1)} %pad_maximum_fusion.3), channel_id=1, source_target_pairs={{0,2},{2,0},{4,6},{6,4},{1,3},{3,1},{5,7},{7,5},{8,10},{10,8},{12,... | collective-permute-start | bytes 1032200 | tf_op jit(solution)/shard_map/ppermute | solution.py:439
Sparse Core Ops, SparseCore 0:
  78.1 61.7 all-reduce.1
where the time goes:
time: 150 us; the launch traced here: 149 us
  waiting for transfers between devices  50.2 us (33%)
  Pallas kernels  45.2 us (30%)
  starting transfers between devices  23.3 us (16%)
  between operations  14.3 us (10%)
  local copies, waits for them, and re-layouts  8.96 us (6%)
  other arithmetic  7.19 us (5%)
    pallas_call x5, Pallas kernels, call(): pl.pallas_call(kernel, out_shape=[jax.ShapeDtypeStruct(s, d) for s, d in...  45.2 us
    psum x1, waiting for transfers between devices, body(): grad_wa = lax.psum(grad_wa, ('gx', 'gy')).reshape(TAPS, 96, 96)  22.6 us
    ppermute x6, waiting for transfers between devices, sum_region(): piece = kept + lax.ppermute(sent, *perms[step]).astype(F32)  10.6 us
    ppermute x6, waiting for transfers between devices, sum_region(): other = lax.ppermute(piece, *perms[step])  8.93 us
    ppermute x2, waiting for transfers between devices, exchange(): from_plus = lax.ppermute(minus, 'gx', down)  6.92 us
    ppermute x6, starting transfers between devices, sum_region(): piece = kept + lax.ppermute(sent, *perms[step]).astype(F32)  6.62 us
    ppermute x2, starting transfers between devices, exchange(): from_minus = lax.ppermute(plus, 'gx', up)  6.6 us
    ppermute x6, starting transfers between devices, sum_region(): other = lax.ppermute(piece, *perms[step])  4.47 us
  transfers between devices with their start and end apart: 19, of which 12 were waited for; matrix products, arithmetic and copies ran while one was open for 5% of the time, Pallas kernels for 9%

commit v1 on v0

v1 whole, which is shorter than its diff:
```python
import functools

import jax
import jax.numpy as jnp
from jax import lax
from jax.experimental import pallas as pl
from jax.experimental.pallas import tpu as pltpu
from jax.sharding import PartitionSpec as P

EDGE = 8
VOX = 512
TAPS = 27
PLANE = 80
PADDED = 896
OUTER = 640
FIRST = 88
FACE = 128
FAR = 100
HALO = 512
HALF = 4096
STORED = 2688
NT = (((1,), (1,)), ((), ()))
BF = jnp.bfloat16
F32 = jnp.float32
VMEM = pl.BlockSpec(memory_space=pltpu.VMEM)
FAR_SPEC = pl.BlockSpec(memory_space=pltpu.HBM)
SMEM = pl.BlockSpec(memory_space=pltpu.SMEM)
LIMIT = 58 * 1024 * 1024
MIB = 1024 * 1024


def iota(shape, dim):
    return lax.broadcasted_iota(jnp.int32, shape, dim)


def one_hot(cond):
    return jnp.where(cond, 1.0, 0.0).astype(BF)


def slot_places(send_ref):
    places = []
    for slot in range(2):
        px = py = pz = held = jnp.int32(0)
        for x in range(2):
            for y in range(2):
                for z in range(2):
                    here = (send_ref[x, y, z] == slot).astype(jnp.int32)
                    held = held + here
                    px = px + here * x
                    py = py + here * y
                    pz = pz + here * z
        places.append((px, py, pz, held))
    return places


def lane_mask(occ_ref, slot, width, plane):
    lane = iota((8, width), 1)
    if plane == 64:
        voxel = lane
        inside = lane >= 0
    else:
        x = lax.shift_right_logical(lane * 205, 14)
        rest = lane - x * plane
        voxel = x * 64 + rest
        inside = rest < 64
    word = lax.shift_right_logical(voxel * 2185, 16)
    bit = voxel - word * 30
    total = jnp.zeros((8, width), jnp.int32)
    for w in range(18):
        total = jnp.where(word == w, occ_ref[slot, w], total)
    on = lax.shift_right_logical(total, bit) & 1
    return jnp.where(inside, on, 0).astype(F32)[:1]


def y_side(dirs, q, receiving):
    if dirs == 1:
        return 1 - lax.axis_index("gy")
    return q if receiving else 1 - q


def send_choices(send_ref, dirs):
    places = slot_places(send_ref)

    def split(row):
        return row >> 6, (row >> 3) & 7, row & 7

    along_x = []
    lane = iota((FACE, FACE), 1)
    for side in (1, 0):
        i, j, l = split(iota((FACE, FACE), 0) + 384 * side)
        ahead = jnp.int32(0)
        picks = []
        for px, py, pz, held in places:
            facing = (px == side).astype(jnp.int32) * held
            at_face = i == 7 * side
            blocks = [
                one_hot(jnp.where(at_face & (facing == 1), ahead * 64 + j * 8 + l, -1) == lane)
            ]
            ahead = ahead + facing
            for q in range(dirs):
                col = y_side(dirs, q, False)
                here = at_face & (j == 7 * col) & ((facing == 1) & (py == col))
                edge = jnp.where(here, 16 * (1 - side) + pz * 8 + l, -1)
                blocks.append(one_hot(edge == (lane & 31)))
            picks.append(jnp.concatenate(blocks, axis=1))
        along_x.append(picks)
    along_y = []
    lane = iota((VOX, FACE), 1)
    i, j, l = split(iota((VOX, FACE), 0))
    for q in range(dirs):
        col = y_side(dirs, q, False)
        ahead = jnp.int32(0)
        picks = []
        for px, py, pz, held in places:
            facing = (py == col).astype(jnp.int32) * held
            here = (j == 7 * col) & (facing == 1)
            picks.append(one_hot(jnp.where(here, ahead * 64 + i * 8 + l, -1) == lane))
            ahead = ahead + facing
        along_y.append(picks)
    return along_x, along_y


def pack_sends(own_ref, send_ref, dirs, plus_ref, minus_ref, y_ref):
    channels = own_ref.shape[1]
    group = channels // 4
    along_x, along_y = send_choices(send_ref, dirs)
    glane = iota((group, FACE), 1) >> 5
    for side, picks, ref in ((1, along_x[0], plus_ref), (0, along_x[1], minus_ref)):
        lanes = slice(384 * side, 384 * side + 128)
        wide = jnp.dot(own_ref[0, :, lanes], picks[0], preferred_element_type=F32) + jnp.dot(
            own_ref[1, :, lanes], picks[1], preferred_element_type=F32
        )
        ref[:channels, :] = wide[:, :FACE].astype(BF)
        for q in range(dirs):
            at = FACE * (1 + q)
            packed = jnp.zeros((group, FACE), F32)
            for g in range(4):
                packed = jnp.where(
                    glane == g, wide[group * g : group * g + group, at : at + FACE], packed
                )
            ref[channels + group * q : channels + group * q + group, :] = packed.astype(BF)
    for q in range(dirs):
        y_ref[q, :, :] = (
            jnp.dot(own_ref[0], along_y[q][0], preferred_element_type=F32)
            + jnp.dot(own_ref[1], along_y[q][1], preferred_element_type=F32)
        ).astype(BF)


def ring_of(x, y):
    return jnp.where(x == 0, y, jnp.where(x == 9, 10 + y, jnp.where(y == 0, 19 + x, 27 + x)))


def encode(x, y, z, ok):
    ok = ok & (x >= 0) & (x <= 9) & (y >= 0) & (y <= 9) & (z >= -1) & (z <= 8)
    side = ring_of(x, y) * 8 + z
    ends = 288 + (x * 10 + y) * 2 + jnp.where(z > 7, 1, 0)
    return jnp.where(ok, jnp.where((z < 0) | (z > 7), ends, side), -1)


def halo_choice(so_ref, sr_ref, n, send_ref, near_ref, dirs):
    places = slot_places(send_ref)
    nx, ny, nz, _ = places[n]
    px, py, pz, _ = places[1 - n]

    def put(ref, at, rows, target):
        for b in range(HALO // 128):
            ref[n, at : at + rows, 128 * b : 128 * b + 128] = one_hot(
                target == iota((rows, 128), 1) + 128 * b
            )

    row = iota((VOX, 128), 0)
    put(
        so_ref,
        0,
        VOX,
        encode(
            (row >> 6) + 1 + 8 * (px - nx),
            ((row >> 3) & 7) + 1 + 8 * (py - ny),
            (row & 7) + 8 * (pz - nz),
            row >= 0,
        ),
    )

    def ranked(offset_of):
        count = jnp.int32(0)
        firsts = [jnp.int32(FAR), jnp.int32(FAR)]
        depths = [jnp.int32(0), jnp.int32(0)]
        for across in range(2):
            for z in range(2):
                there = (near_ref[n, offset_of(across, z)] >= 0).astype(jnp.int32)
                for rank in range(2):
                    take = (there == 1) & (count == rank)
                    firsts[rank] = jnp.where(take, across, firsts[rank])
                    depths[rank] = jnp.where(take, z, depths[rank])
                count = count + there
        return firsts, depths

    row = iota((FACE, 128), 0)
    high = row >= 64
    u = (row >> 3) & 7
    l = row & 7
    nought = jnp.zeros((FACE, 128), jnp.int32)
    firsts, depths = ranked(
        lambda across, z: 18 * nx + 3 * (across - ny + 1) + (z - nz + 1)
    )
    across = jnp.where(high, firsts[1], firsts[0])
    depth = jnp.where(high, depths[1], depths[0])
    for side in range(2):
        put(
            sr_ref,
            FACE * side,
            FACE,
            encode(
                nought + 9 * side,
                u + 1 + 8 * (across - ny),
                l + 8 * (depth - nz),
                nought + nx == side,
            ),
        )
    firsts, depths = ranked(
        lambda across, z: 9 * (across - nx + 1) + 6 * ny + (z - nz + 1)
    )
    across = jnp.where(high, firsts[1], firsts[0])
    depth = jnp.where(high, depths[1], depths[0])
    e = row & 31
    from_side = e >> 4
    for q in range(dirs):
        side = y_side(dirs, q, True)
        put(
            sr_ref,
            FACE * (2 + q),
            FACE,
            encode(
                u + 1 + 8 * (across - nx),
                nought + 9 * side,
                l + 8 * (depth - nz),
                nought + ny == side,
            ),
        )
        put(
            sr_ref,
            FACE * (2 + dirs + q),
            FACE,
            encode(
                9 * from_side,
                nought + 9 * side,
                (e & 7) + 8 * (((e >> 3) & 1) - nz),
                (from_side == nx) & (nought + ny == side),
            ),
        )


def padded_choice(stat_ref):
    lane = iota((8, PADDED), 1)
    x = lax.shift_right_logical(lane * 205, 14)
    rest = lane - x * PLANE
    y = rest >> 3
    l = rest & 7
    within = (x >= 1) & (x <= 8) & (y >= 1) & (y <= 8)
    own = jnp.where(within, (x - 1) * 64 + (y - 1) * 8 + l, -1)
    side = jnp.where(within | (x > 9), -1, ring_of(x, y) * 8 + l)
    ends = jnp.where(
        (x <= 9) & ((l == 0) | (l == 7)), 288 + (x * 10 + y) * 2 + jnp.where(l == 7, 1, 0), -1
    )
    row = iota((HALO, PADDED), 0)
    for index, target in enumerate((own, side, ends)):
        stat_ref[index] = one_hot(row == target[:1])


def fill_padded(own_ref, part_ref, recv_minus, recv_plus, recv_y, sr_ref, stat_ref, d_ref, xh_ref, dirs, outs, ready):
    channels = own_ref.shape[1]
    group = channels // 4
    d_ref[:, :FACE] = recv_minus[:channels, :]
    d_ref[:, FACE : 2 * FACE] = recv_plus[:channels, :]
    glane = iota((group, FACE), 1) >> 5
    for q in range(dirs):
        at = FACE * (2 + q)
        d_ref[:, at : at + FACE] = recv_y[q, :channels, :]
        packed = recv_y[q, channels : channels + group, :].astype(F32)
        spread = jnp.concatenate([jnp.where(glane == g, packed, 0.0) for g in range(4)], axis=0)
        at = FACE * (2 + dirs + q)
        d_ref[:, at : at + FACE] = spread.astype(BF)
    ready(0)
    halos = [jnp.dot(d_ref[...], sr_ref[n], preferred_element_type=F32) for n in range(2)]
    ready(1)
    for n in range(2):
        rows = slice(channels * n, channels * n + channels)
        xh_ref[rows, :VOX] = own_ref[n]
        xh_ref[rows, VOX:] = (halos[n] + part_ref[n].astype(F32)).astype(BF)
    middle = jnp.dot(xh_ref[:, :VOX], stat_ref[0], preferred_element_type=F32) + jnp.dot(
        xh_ref[:, VOX:], stat_ref[1], preferred_element_type=F32
    )
    ends = jnp.dot(xh_ref[:, VOX:], stat_ref[2], preferred_element_type=F32)
    for ref, first, count, flip in outs:
        l = iota((count, PADDED), 1) & 7
        for n in range(2):
            rows = slice(channels * n + first, channels * n + first + count)
            mid = middle[rows]
            end = ends[rows]
            at = slice(PADDED * n, PADDED * n + PADDED)
            below = jnp.where(l == 0, end, pltpu.roll(mid, 1, 1)).astype(BF)
            above = jnp.where(l == 7, end, pltpu.roll(mid, PADDED - 1, 1)).astype(BF)
            low, high = (above, below) if flip else (below, above)
            ref[:count, at] = low
            ref[count : 2 * count, at] = mid.astype(BF)
            ref[2 * count :, at] = high


def fill_patches(p_ref, z_ref):
    for k in range(TAPS):
        a, b, c = k // 9, k // 3 % 3, k % 3
        for n in range(2):
            at = PADDED * n + PLANE * a + 8 * b
            p_ref[96 * k : 96 * k + 96, OUTER * n : OUTER * n + OUTER] = z_ref[
                96 * c : 96 * c + 96, at : at + OUTER
            ]


def shifted_sum(s_ref, n, flip):
    total = None
    for ab in range(9):
        a, b = ab // 3, ab % 3
        if flip:
            a, b = 2 - a, 2 - b
        at = PADDED * n + PLANE * a + 8 * b
        part = s_ref[96 * ab : 96 * ab + 96, at : at + OUTER]
        total = part if total is None else total + part
    return total


def compaction():
    row = iota((OUTER, VOX), 0)
    x = lax.shift_right_logical(row * 205, 14)
    rest = row - x * PLANE
    return one_hot(jnp.where(rest < 64, x * 64 + rest, -1) == iota((OUTER, VOX), 1))


def fetch(pairs, sems):
    copies = [pltpu.make_async_copy(p[0], p[1], sems.at[k]) for k, p in enumerate(pairs)]
    for copy in copies:
        copy.start()
    return copies


def pack_kernel(dirs, feat_ref, cot_ref, occ_ref, send_ref, own_ref, plus_ref, minus_ref, y_ref):
    for n in range(2):
        mask = lane_mask(occ_ref, n, VOX, 64)
        own_ref[n, :96, :] = jnp.where(mask > 0.5, feat_ref[n].astype(F32), 0.0).astype(BF)
        own_ref[n, 96:, :] = jnp.where(mask > 0.5, cot_ref[n].astype(F32), 0.0).astype(BF)
    pack_sends(own_ref, send_ref, dirs, plus_ref, minus_ref, y_ref)


def prepare_kernel(
    dirs, own_ref, near_ref, send_ref, wa_ref,
    so_ref, sr_ref, stat_ref, part_ref, wa9_ref,
):
    for n in range(2):
        halo_choice(so_ref, sr_ref, n, send_ref, near_ref, dirs)
    padded_choice(stat_ref)
    for n in range(2):
        part_ref[n] = jnp.dot(own_ref[1 - n], so_ref[n], preferred_element_type=F32).astype(BF)
    for k in range(TAPS):
        c, ab = k % 3, k // 3
        wa9_ref[96 * ab : 96 * ab + 96, 96 * c : 96 * c + 96] = wa_ref[k].astype(F32).T.astype(BF)


def first_kernel(
    dirs, fm_ref, fp_ref, fy_ref, sr_ref, occ_ref, send_ref, own_ref, part_ref, stat_ref, wa_ref, wb_ref,
    zx_ref, gpre_ref, hid_ref, plus_ref, minus_ref, y_ref,
    d_ref, xh_ref, zg_ref, s9_ref, pre_ref, wb9_ref,
):
    fill_padded(
        own_ref, part_ref, fm_ref, fp_ref, fy_ref, sr_ref, stat_ref, d_ref, xh_ref, dirs,
        ((zx_ref, 0, 96, False), (zg_ref, 96, 256, True)),
        lambda stage: None,
    )
    s9_ref[...] = jnp.dot(wa_ref[...], zx_ref[...], preferred_element_type=F32)
    for n in range(2):
        pre_ref[:, OUTER * n : OUTER * n + OUTER] = shifted_sum(s9_ref, n, False)
    for k in range(TAPS):
        c, ab = k % 3, k // 3
        wb9_ref[96 * ab : 96 * ab + 96, 256 * c : 256 * c + 256] = wb_ref[k]
    s9_ref[...] = jnp.dot(wb9_ref[...], zg_ref[...], preferred_element_type=F32)
    squeeze = compaction()
    for n in range(2):
        at = slice(OUTER * n, OUTER * n + OUTER)
        mask = lane_mask(occ_ref, n, OUTER, PLANE)
        pre = pre_ref[:, at] * mask
        gate = 1.0 / (1.0 + jnp.exp(-pre))
        hidden = (pre * gate).astype(BF)
        grad_pre = (
            shifted_sum(s9_ref, n, True) * gate * (1.0 + pre * (1.0 - gate)) * mask
        ).astype(BF)
        gpre_ref[:, at] = grad_pre
        both = jnp.concatenate([hidden, grad_pre], axis=0)
        hid_ref[n] = jnp.dot(both, squeeze, preferred_element_type=F32).astype(BF)
    pack_sends(hid_ref, send_ref, dirs, plus_ref, minus_ref, y_ref)


def weight_a_kernel(
    scale, zx_ref, gpre_ref, own_ref, stat_ref, hid_ref, so_ref, wb_ref,
    out_hbm, hpart_hbm, gout_hbm, wbt_hbm,
    g9_ref, out_ref, hpart_ref, gout_ref, wbt_ref, sems,
):
    def store(source, target, k):
        copy = pltpu.make_async_copy(source, target, sems.at[k])
        copy.start()
        return copy

    for n in range(2):
        hpart_ref[n] = jnp.dot(hid_ref[1 - n], so_ref[n], preferred_element_type=F32).astype(BF)
        spread = jnp.dot(own_ref[n, 96:, :], stat_ref[0], preferred_element_type=F32)
        gout_ref[:, OUTER * n : OUTER * n + OUTER] = spread[:, FIRST : FIRST + OUTER].astype(BF)
    stores = [store(hpart_ref, hpart_hbm, 0), store(gout_ref, gout_hbm, 1)]
    for k in range(TAPS):
        wbt_ref[:, 96 * k : 96 * k + 96] = wb_ref[k].astype(F32).T.astype(BF)
    stores.append(store(wbt_ref, wbt_hbm, 2))
    g9_ref[...] = jnp.zeros_like(g9_ref)
    for ab in range(9):
        for n in range(2):
            at = PADDED * n + PLANE * (ab // 3) + 8 * (ab % 3)
            g9_ref[128 * ab : 128 * ab + 96, at : at + OUTER] = gpre_ref[
                :, OUTER * n : OUTER * n + OUTER
            ]
    out_ref[...] = jnp.zeros_like(out_ref)
    total = scale * lax.dot_general(
        zx_ref[...], g9_ref[...], NT, preferred_element_type=F32
    )
    for k in range(TAPS):
        half, at = k // 14, 96 * (k % 14)
        c, ab = k % 3, k // 3
        out_ref[half, at : at + 96, :] = total[96 * c : 96 * c + 96, 128 * ab : 128 * ab + 128]
    stores.append(store(out_ref, out_hbm, 3))
    for copy in stores:
        copy.wait()


def weight_b_kernel(
    scale, dirs, split, fm_ref, fp_ref, fy_ref, own_ref, stat_ref,
    sr_hbm, part_hbm, gout_hbm, wa_hbm, zh_hbm, zp_hbm, keep_ref, *rest,
):
    sr_ref, part_ref, gout_ref, wa_ref, zh_ref, zp_ref, d_ref, xh_ref, p_ref, sum_ref, sems = rest[-11:]
    copies = fetch(
        ((sr_hbm, sr_ref), (part_hbm, part_ref), (gout_hbm, gout_ref), (wa_hbm, wa_ref)), sems
    )
    fill_padded(
        own_ref, part_ref, fm_ref, fp_ref, fy_ref, sr_ref, stat_ref, d_ref, xh_ref, dirs,
        ((zh_ref, 0, 96, False), (zp_ref, 96, 96, True)),
        lambda stage: copies[stage].wait(),
    )
    stores = fetch(((zh_ref, zh_hbm), (zp_ref, zp_hbm)), sems.at[pl.ds(4, 2)])
    fill_patches(p_ref, zh_ref)
    copies[2].wait()
    rows = TAPS * 96
    total = scale * lax.dot_general(p_ref[...], gout_ref[...], NT, preferred_element_type=F32)
    copies[3].wait()
    for half in range(2):
        sum_ref[half, :rows, :] = total[:, 128 * half : 128 * half + 128]
        sum_ref[half, rows:STORED, :] = jnp.zeros((STORED - rows, 128), F32)
        sum_ref[half, STORED:, :] = wa_ref[half]
    if split:
        core = lax.axis_index("gx") & 1
        keep = pl.multiple_of(core * (HALF // 2), HALF // 2)
        send = pl.multiple_of((1 - core) * (HALF // 2), HALF // 2)
        keep_ref[...] = sum_ref[:, pl.ds(keep, HALF // 2), :]
        rest[0][...] = sum_ref[:, pl.ds(send, HALF // 2), :].astype(BF)
    else:
        keep_ref[...] = sum_ref[...]
    for store in stores:
        store.wait()


def out_kernel(occ_ref, zh_hbm, wbt_hbm, out_ref, p_ref, zh_ref, wbt_ref, sems):
    copies = fetch(((zh_hbm, zh_ref), (wbt_hbm, wbt_ref)), sems)
    squeeze = compaction()
    copies[0].wait()
    fill_patches(p_ref, zh_ref)
    copies[1].wait()
    total = jnp.dot(wbt_ref[...], p_ref[...], preferred_element_type=F32)
    for n in range(2):
        mask = lane_mask(occ_ref, n, OUTER, PLANE)
        part = total[:, OUTER * n : OUTER * n + OUTER] * mask
        out_ref[n] = jnp.dot(part.astype(BF), squeeze, preferred_element_type=F32).astype(BF)


def grad_kernel(occ_ref, zp_hbm, wa_hbm, grad_ref, s9_ref, wg9_ref, zp_ref, wa_ref, sems):
    copies = fetch(((wa_hbm, wa_ref), (zp_hbm, zp_ref)), sems)
    squeeze = compaction()
    copies[0].wait()
    for k in range(TAPS):
        c, ab = k % 3, k // 3
        wg9_ref[96 * ab : 96 * ab + 96, 96 * c : 96 * c + 96] = wa_ref[k]
    copies[1].wait()
    s9_ref[...] = jnp.dot(wg9_ref[...], zp_ref[...], preferred_element_type=F32)
    for n in range(2):
        mask = lane_mask(occ_ref, n, OUTER, PLANE)
        grad_ref[n] = jnp.dot(
            (shifted_sum(s9_ref, n, True) * mask).astype(BF), squeeze, preferred_element_type=F32
        ).astype(BF)


def unpack_kernel(mine_ref, other_ref, wa_hbm, wb_hbm, all_ref, wa_ref, wb_ref, sems):
    core = lax.axis_index("gx") & 1
    for index, ref in enumerate((mine_ref, other_ref)):
        at = core if index == 0 else 1 - core
        at = pl.multiple_of(at * (HALF // 2), HALF // 2)
        all_ref[:, pl.ds(at, HALF // 2), :] = ref[...]
    copies = []

    def store(source, target):
        copies.append(pltpu.make_async_copy(source, target, sems.at[len(copies)]))
        copies[-1].start()

    for k in range(TAPS):
        for side in range(2):
            wb_ref[k, :, 128 * side : 128 * side + 128] = all_ref[
                side, 96 * k : 96 * k + 96, :
            ].astype(F32)
        if k % 9 == 8:
            store(wb_ref.at[pl.ds(k - 8, 9)], wb_hbm.at[pl.ds(k - 8, 9)])
    for k in range(TAPS):
        half, at = k // 14, STORED + 96 * (k % 14)
        wa_ref[k] = all_ref[half, at : at + 96, :96].astype(F32)
    store(wa_ref, wa_hbm)
    for copy in copies:
        copy.wait()


def call(kernel, outs, ins, scratch=(), flops=0, moved=0, far_ins=0, far_outs=0, sems=0, limit=LIMIT):
    specs = [SMEM if jnp.issubdtype(x.dtype, jnp.integer) else VMEM for x in ins]
    for k in range(far_ins):
        specs[len(ins) - 1 - k] = FAR_SPEC
    out_specs = [VMEM] * len(outs)
    for k in range(far_outs):
        out_specs[k] = FAR_SPEC
    scratch = [pltpu.VMEM(s, d) for s, d in scratch]
    if sems:
        scratch.append(pltpu.SemaphoreType.DMA((sems,)))
    return pl.pallas_call(
        kernel,
        out_shape=[jax.ShapeDtypeStruct(s, d) for s, d in outs],
        in_specs=specs,
        out_specs=out_specs,
        scratch_shapes=scratch,
        compiler_params=pltpu.CompilerParams(vmem_limit_bytes=limit),
        cost_estimate=pl.CostEstimate(flops=flops, bytes_accessed=moved, transcendentals=0),
    )(*ins)


def exchange(channels, plus, minus, faces, count_x, count_y, cover):
    up = [(k, k + 1) for k in range(count_x - 1)]
    down = [(k + 1, k) for k in range(count_x - 1)]
    from_minus = lax.ppermute(plus, "gx", up)
    from_plus = lax.ppermute(minus, "gx", down)
    covered = cover()
    faces, covered = lax.optimization_barrier((faces, covered))
    group = channels // 4
    dirs = faces.shape[0]
    if dirs == 1:
        perms = [[(0, 1), (1, 0)]]
    else:
        perms = [
            [(k, k + 1) for k in range(count_y - 1)],
            [(k + 1, k) for k in range(count_y - 1)],
        ]
    arrived = []
    for q in range(dirs):
        at = channels + group * q
        edges = from_minus[at : at + group] + from_plus[at : at + group]
        arrived.append(
            lax.ppermute(jnp.concatenate([faces[q], edges], axis=0), "gy", perms[q])
        )
    return from_minus, from_plus, jnp.stack(arrived, axis=0), covered


def swap_or_keep(piece, bit):
    rows = piece.shape[0] // 2
    low, high = piece[:rows], piece[rows:]
    return jnp.where(bit == 0, high, low).astype(BF), jnp.where(bit == 0, low, high)


def body(features, occupancy, neighbours, send_slots, weight_a, weight_b, cotangent):
    count_x = lax.axis_size("gx")
    count_y = lax.axis_size("gy")
    dirs = 1 if count_y == 2 else 2
    split = count_x == 4 and count_y == 2
    scale = float(features.shape[0] * VOX * count_x * count_y) ** -0.5
    lanes = FACE * (2 + 2 * dirs)
    wide = 2 * PADDED
    outer = 2 * OUTER

    rows = 352 + 88 * dirs
    own, plus, minus, faces = call(
        functools.partial(pack_kernel, dirs),
        [((2, 352, VOX), BF), ((rows, FACE), BF), ((rows, FACE), BF), ((dirs, 352, FACE), BF)],
        [features, cotangent, occupancy, send_slots],
        flops=352 * 1024 * 1024,
        moved=2 * 1024 * 1024,
    )

    def prepare():
        return call(
            functools.partial(prepare_kernel, dirs),
            [
                ((2, VOX, HALO), BF),
                ((2, lanes, HALO), BF),
                ((3, HALO, PADDED), BF),
                ((2, 352, HALO), BF),
                ((864, 288), BF),
            ],
            [own, neighbours, send_slots, weight_a],
            flops=10**9,
            moved=8 * MIB,
            limit=8 * MIB,
        )

    from_minus, from_plus, from_y, prepared = exchange(
        352, plus, minus, faces, count_x, count_y, prepare
    )
    halo_own, halo_far, padded, part, wa9 = prepared

    rows = 192 + 48 * dirs
    zx, gpre, hid, plus, minus, faces = call(
        functools.partial(first_kernel, dirs),
        [
            ((288, wide), BF),
            ((96, outer), BF),
            ((2, 192, VOX), BF),
            ((rows, FACE), BF),
            ((rows, FACE), BF),
            ((dirs, 192, FACE), BF),
        ],
        [
            from_minus, from_plus, from_y, halo_far, occupancy, send_slots,
            own, part, padded, wa9, weight_b,
        ],
        [
            ((352, lanes), BF),
            ((704, 1024), BF),
            ((768, wide), BF),
            ((864, wide), F32),
            ((96, outer), F32),
            ((864, 768), BF),
        ],
        flops=5 * 10**9,
        moved=8 * MIB,
        limit=20 * MIB,
    )

    def first_weights():
        return call(
            functools.partial(weight_a_kernel, scale),
            [
                ((2, HALF - STORED, 128), F32),
                ((2, 192, HALO), BF),
                ((256, outer), BF),
                ((256, TAPS * 96), BF),
            ],
            [zx, gpre, own, padded, hid, halo_own, weight_b],
            [
                ((9 * 128, wide), BF),
                ((2, HALF - STORED, 128), F32),
                ((2, 192, HALO), BF),
                ((256, outer), BF),
                ((256, TAPS * 96), BF),
            ],
            flops=2 * 10**9,
            moved=6 * MIB,
            far_outs=4,
            sems=4,
            limit=20 * MIB,
        )

    from_minus, from_plus, from_y, covered = exchange(
        192, plus, minus, faces, count_x, count_y, first_weights
    )
    grad_wa, hpart, gout, wbt = covered
    sums = [((2, HALF, 128), F32)]
    if split:
        sums = [((2, HALF // 2, 128), F32), ((2, HALF // 2, 128), BF)]
    zh, zp, *sums = call(
        functools.partial(weight_b_kernel, scale, dirs, split),
        [((288, wide), BF), ((288, wide), BF)] + sums,
        [from_minus, from_plus, from_y, hid, padded, halo_far, hpart, gout, grad_wa],
        [
            ((2, lanes, HALO), BF),
            ((2, 192, HALO), BF),
            ((256, outer), BF),
            ((2, HALF - STORED, 128), F32),
            ((288, wide), BF),
            ((288, wide), BF),
            ((192, lanes), BF),
            ((384, 1024), BF),
            ((TAPS * 96, outer), BF),
            ((2, HALF, 128), F32),
        ],
        flops=2 * 10**9,
        moved=4 * MIB,
        far_ins=4,
        far_outs=2,
        sems=6,
        limit=22 * MIB,
    )

    def layer(zh):
        return call(
            out_kernel,
            [((2, 256, VOX), BF)],
            [occupancy, zh, wbt],
            [((TAPS * 96, outer), BF), ((288, wide), BF), ((256, TAPS * 96), BF)],
            flops=2 * 10**9,
            moved=3 * MIB,
            far_ins=2,
            sems=2,
            limit=20 * MIB,
        )[0]

    def data_grad(zp):
        return call(
            grad_kernel,
            [((2, 96, VOX), BF)],
            [occupancy, zp, weight_a],
            [((864, wide), F32), ((864, 288), BF), ((288, wide), BF), ((TAPS, 96, 96), BF)],
            flops=2 * 10**9,
            moved=2 * MIB,
            far_ins=2,
            sems=2,
            limit=20 * MIB,
        )[0]

    if not split:
        total = lax.psum(sums[0], ("gx", "gy"))
        grad_wb = jnp.concatenate([total[0, : TAPS * 96], total[1, : TAPS * 96]], axis=1)
        first = total[0, STORED : STORED + 14 * 96, :96]
        second = total[1, STORED : STORED + 13 * 96, :96]
        grad_wa = jnp.concatenate([first, second], axis=0)
        return layer(zh), data_grad(zp), grad_wa.reshape(TAPS, 96, 96), grad_wb.reshape(TAPS, 96, 256)

    along_y = ("gx", [(k, k ^ 2) for k in range(4)])
    along_x = ("gy", [(0, 1), (1, 0)])
    bit_y = lax.axis_index("gx") >> 1
    bit_x = lax.axis_index("gy")
    swap = ("gx", [(k, k ^ 1) for k in range(4)])
    keep, send = sums
    summed = keep + lax.ppermute(send, *swap).astype(F32)
    send_a, keep_a = swap_or_keep(summed[0], bit_y)
    send_b, keep_b = swap_or_keep(summed[1], bit_x)
    zh, send_a, send_b = lax.optimization_barrier((zh, send_a, send_b))
    got_a = lax.ppermute(send_a, *along_y)
    got_b = lax.ppermute(send_b, *along_x)
    layer_out = layer(zh)
    got_a, got_b, layer_out = lax.optimization_barrier((got_a, got_b, layer_out))
    half_a = keep_a + got_a.astype(F32)
    half_b = keep_b + got_b.astype(F32)
    send_a, keep_a = swap_or_keep(half_a, bit_x)
    send_b, keep_b = swap_or_keep(half_b, bit_y)
    got_a = lax.ppermute(send_a, *along_x)
    got_b = lax.ppermute(send_b, *along_y)
    part_a = (keep_a + got_a.astype(F32)).astype(BF)
    part_b = (keep_b + got_b.astype(F32)).astype(BF)

    def joined(piece, other, bit):
        first = bit == 0
        return jnp.concatenate(
            [jnp.where(first, piece, other), jnp.where(first, other, piece)], axis=0
        )

    part_a, part_b = (
        joined(part_a, lax.ppermute(part_a, *along_x), bit_x),
        joined(part_b, lax.ppermute(part_b, *along_y), bit_y),
    )
    zp, part_a, part_b = lax.optimization_barrier((zp, part_a, part_b))
    other_a = lax.ppermute(part_a, *along_y)
    other_b = lax.ppermute(part_b, *along_x)
    grad_features = data_grad(zp)
    other_a, other_b, grad_features = lax.optimization_barrier((other_a, other_b, grad_features))
    mine = jnp.stack([joined(part_a, other_a, bit_y), joined(part_b, other_b, bit_x)], axis=0)
    other = lax.ppermute(mine, *swap)
    grad_wa, grad_wb = call(
        unpack_kernel,
        [((TAPS, 96, 96), F32), ((TAPS, 96, 256), F32)],
        [mine, other],
        [((2, HALF, 128), BF), ((TAPS, 96, 96), F32), ((TAPS, 96, 256), F32)],
        moved=6 * MIB,
        far_outs=2,
        sems=4,
        limit=20 * MIB,
    )
    return layer_out, grad_features, grad_wa, grad_wb


def solution(mesh):
    in_specs = (
        P(("dp", "gx", "gy"), None, None),
        P(("dp", "gx", "gy"), None),
        P(("dp", "gx", "gy"), None),
        P(("dp", "gx"), "gy", None),
        P(),
        P(),
        P(("dp", "gx", "gy"), None, None),
    )
    out_specs = (
        P(("dp", "gx", "gy"), None, None),
        P(("dp", "gx", "gy"), None, None),
        P("dp", None, None),
        P("dp", None, None),
    )
    return jax.shard_map(body, mesh=mesh, in_specs=in_specs, out_specs=out_specs, check_vma=False)
```

time: 150 us -> 97 us (0.65)
  waiting for transfers between devices: 50.2 us -> 19.2 us
  between operations: 14.3 us -> 1.16 us
  other arithmetic: 7.19 us -> 2.21 us
  local copies, waits for them, and re-layouts: 8.96 us -> 5.5 us
  starting transfers between devices: 23.3 us -> 25.4 us
  Pallas kernels: 45.2 us -> 43.2 us
    psum x1 -> x0, waiting for transfers between devices: 22.6 us -> none  [body(): grad_wa = lax.psum(grad_wa, ('gx', 'gy')).reshape(TAPS, 96, 96)]
    ppermute x2, waiting for transfers between devices: 6.92 us -> 0.01 us  [exchange(): from_plus = lax.ppermute(minus, 'gx', down)]
    ppermute x12 -> x10, waiting for transfers between devices: 19.5 us -> 13.7 us  [the longest x1 3.63 us: body(): got_b = lax.ppermute(send_b, *along_y)]
    reshape x3 -> x0, local copies, waits for them, and re-layouts: 4.87 us -> none  [the longest x1 2.14 us: body(): wat = weight_a.transpose(2, 0, 1).reshape(96, TAPS * 96)]
    ppermute x2, waiting for transfers between devices: 1.14 us -> 5.47 us  [exchange(): lax.ppermute(jnp.concatenate([faces[q], edges], axis=0), 'gy', perms[q])]
    pallas_call x5 -> x8, Pallas kernels: 45.2 us -> 43.2 us  [call(): pl.pallas_call(kernel, out_shape=[jax.ShapeDtypeStruct(s, d) for s, d in...]
    reshape x1 -> x0, other arithmetic: 1.82 us -> none  [body(): sum_region(grad_wb, count_x, count_y)[:TAPS * 96].reshape(TAPS, 96, 256)]
    convert_element_type x7 -> x5, other arithmetic: 2.01 us -> 0.23 us  [the longest x3 0.15 us: swap_or_keep(): jnp.where(bit == 0, high, low).astype(BF)]
  transfers between devices with their start and end apart: 19 -> 16, of which waited for: 12 -> 8; matrix products, arithmetic and copies ran while one was open for 5% -> 0% of each run, Pallas kernels for 9% -> 21%
where the time goes in v1:
time: 97 us; the launch traced here: 96.6 us
  Pallas kernels  43.2 us (45%)
  starting transfers between devices  25.4 us (26%)
  waiting for transfers between devices  19.2 us (20%)
  local copies, waits for them, and re-layouts  5.5 us (6%)
  other arithmetic  2.21 us (2%)
  between operations  1.16 us (1%)
    pallas_call x8, Pallas kernels, call(): pl.pallas_call(kernel, out_shape=[jax.ShapeDtypeStruct(s, d) for s, d in...  43.2 us
    ppermute x2, starting transfers between devices, exchange(): from_minus = lax.ppermute(plus, 'gx', up)  6.19 us
    unnamed x28, local copies, waits for them, and re-layouts  5.5 us
    ppermute x2, waiting for transfers between devices, exchange(): lax.ppermute(jnp.concatenate([faces[q], edges], axis=0), 'gy', perms[q])  5.47 us
    ppermute x2, starting transfers between devices, exchange(): lax.ppermute(jnp.concatenate([faces[q], edges], axis=0), 'gy', perms[q])  3.95 us
    ppermute x1, waiting for transfers between devices, body(): got_b = lax.ppermute(send_b, *along_y)  3.63 us
    ppermute x1, waiting for transfers between devices, body(): lax.ppermute(part_b, *along_y)  3.61 us
    ppermute x1, starting transfers between devices, body(): got_a = lax.ppermute(send_a, *along_y)  3.2 us
  transfers between devices with their start and end apart: 16, of which 8 were waited for; matrix products, arithmetic and copies ran while one was open for 0% of the time, Pallas kernels for 21%

profile of v1, /device:TPU:0, one launch (start us, length us, event | category | flops | bytes accessed | tf_op | source)
XLA Modules:
  0.0 96.6 jit_solution(1042007931199605113)
XLA Ops:
  0.6 0.0 copy-start.6
  0.7 2.7 %shard_map.102 = (bf16[2,352,512]{2,1,0:T(8,128)(2,1)}, bf16[440,128]{1,0:T(8,128)(2,1)}, bf16[440,128]{1,0:T(8,128)(2,1)}, bf16[1,352,128]{2,1,0:T(8,128)(2,1)}) custom-call(bf16[2,96,512]{2,1,0:T(8,128)(2,1)} %feat_ref.1, bf16[2,256,512]{2,1,0:T(8,128)(2,1)} %cot_ref.1, s32[2,18]{1,0:T(2,128)} %occ_ref.7, s32[2,2,2]{2,1,0:T(2,128)} %send_ref.5), custom_call_target="tpu_custom_call" | custom-call | flops 369098752 | bytes 2097152 | tf_op jit(solution)/shard_map/pallas_call | solution.py:539
  3.3 2.5 %collective-permute-start = (bf16[440,128]{1,0:T(8,128)(2,1)}, bf16[440,128]{1,0:T(8,128)(2,1)S(1)}, u32[]{:S(2)}, u32[]{:S(2)}) collective-permute-start(bf16[440,128]{1,0:T(8,128)(2,1)} %get-tuple-element.52), channel_id=1, source_target_pairs={{0,2},{2,4},{4,6},{1,3},{3,5},{5,7},{8,10},{10,12},{12,14},{9,11},... | collective-permute-start | bytes 337928 | tf_op jit(solution)/shard_map/ppermute | solution.py:553
  5.8 1.3 %collective-permute-start.1 = (bf16[440,128]{1,0:T(8,128)(2,1)}, bf16[440,128]{1,0:T(8,128)(2,1)S(1)}, u32[]{:S(2)}, u32[]{:S(2)}) collective-permute-start(bf16[440,128]{1,0:T(8,128)(2,1)} %get-tuple-element.53), channel_id=1, source_target_pairs={{2,0},{4,2},{6,4},{3,1},{5,3},{7,5},{10,8},{12,10},{14,12},{11,9},... | collective-permute-start | bytes 337928 | tf_op jit(solution)/shard_map/ppermute | solution.py:554
  7.1 0.0 copy-start.1
  7.1 1.1 %copy-done.1 = bf16[2,352,512]{2,1,0:T(8,128)(2,1)S(1)} copy-done((bf16[2,352,512]{2,1,0:T(8,128)(2,1)S(1)}, bf16[2,352,512]{2,1,0:T(8,128)(2,1)}, u32[]{:S(2)}) %copy-start.1) | copy-done | bytes 720920
  8.2 1.1 %copy-done.3 = bf16[27,96,96]{2,1,0:T(8,128)(2,1)S(1)} copy-done((bf16[27,96,96]{2,1,0:T(8,128)(2,1)S(1)}, bf16[27,96,96]{2,1,0:T(8,128)(2,1)}, u32[]{:S(2)}) %copy-start.3) | copy-done | bytes 497688
  9.3 0.7 copy-done.5
  10.0 0.7 copy-done.7
  10.7 3.7 %shard_map.103 = (bf16[2,512,512]{2,1,0:T(8,128)(2,1)S(1)}, bf16[2,512,512]{2,1,0:T(8,128)(2,1)S(1)}, bf16[3,512,896]{2,1,0:T(8,128)(2,1)S(1)}, bf16[2,352,512]{2,1,0:T(8,128)(2,1)S(1)}, bf16[864,288]{1,0:T(8,128)(2,1)S(1)}) custom-call(bf16[2,352,512]{2,1,0:T(8,128)(2,1)S(1)} %copy-done.1, s32[2,27]{1,0:T(2,128)S(1)} %copy-done.7, ...), custom_call_target="tpu_custom_call" | custom-call | flops 1000000000 | bytes 8388608 | tf_op jit(solution)/shard_map/pallas_call | solution.py:539
  14.4 0.0 collective-permute-done.fm_ref
  14.5 2.4 %collective-permute-start.2 = (bf16[440,128]{1,0:T(8,128)(2,1)S(1)}, bf16[440,128]{1,0:T(8,128)(2,1)S(1)}, u32[]{:S(2)}, u32[]{:S(2)}) collective-permute-start(bf16[440,128]{1,0:T(8,128)(2,1)S(1)} %pad_maximum_fusion.3), channel_id=1, source_target_pairs={{0,1},{1,0},{2,3},{3,2},{4,5},{5,4},{6,7},{7,6},{8,9},{9,8},{10,11... | collective-permute-start | bytes 337928 | tf_op jit(solution)/shard_map/ppermute | solution.py:571
  16.8 2.8 %collective-permute-done.2 = bf16[440,128]{1,0:T(8,128)(2,1)S(1)} collective-permute-done((bf16[440,128]{1,0:T(8,128)(2,1)S(1)}, bf16[440,128]{1,0:T(8,128)(2,1)S(1)}, u32[]{:S(2)}, u32[]{:S(2)}) %collective-permute-start.2) | collective-permute-done | bytes 112672 | tf_op jit(solution)/shard_map/ppermute | solution.py:571
  19.6 9.2 %shard_map.104 = (bf16[288,1792]{1,0:T(8,128)(2,1)S(1)}, bf16[96,1280]{1,0:T(8,128)(2,1)S(1)}, bf16[2,192,512]{2,1,0:T(8,128)(2,1)S(1)}, bf16[240,128]{1,0:T(8,1...) custom-call(bf16[440,128]{1,0:T(8,128)(2,1)S(1)} %collective-permute-done.fm_ref, ...), custom_call_target="tpu_custom_call" | custom-call | flops 5000000000 | bytes 8388608 | tf_op jit(solution)/shard_map/pallas_call | solution.py:539
  28.8 3.7 %collective-permute-start.3 = (bf16[240,128]{1,0:T(8,128)(2,1)S(1)}, bf16[240,128]{1,0:T(8,128)(2,1)S(1)}, u32[]{:S(2)}, u32[]{:S(2)}) collective-permute-start(bf16[240,128]{1,0:T(8,128)(2,1)S(1)} %get-tuple-element.66), channel_id=1, source_target_pairs={{0,2},{2,4},{4,6},{1,3},{3,5},{5,7},{8,10},{10,12},{12,14},{9,11},... | collective-permute-start | bytes 184328 | tf_op jit(solution)/shard_map/ppermute | solution.py:553
  32.5 1.5 %collective-permute-start.4 = (bf16[240,128]{1,0:T(8,128)(2,1)S(1)}, bf16[240,128]{1,0:T(8,128)(2,1)S(1)}, u32[]{:S(2)}, u32[]{:S(2)}) collective-permute-start(bf16[240,128]{1,0:T(8,128)(2,1)S(1)} %get-tuple-element.67), channel_id=1, source_target_pairs={{2,0},{4,2},{6,4},{3,1},{5,3},{7,5},{10,8},{12,10},{14,12},{11,9},... | collective-permute-start | bytes 184328 | tf_op jit(solution)/shard_map/ppermute | solution.py:554
  34.0 4.9 %shard_map.105 = (f32[2,1408,128]{2,1,0:T(8,128)S(1)}, bf16[2,192,512]{2,1,0:T(8,128)(2,1)S(1)}, bf16[256,1280]{1,0:T(8,128)(2,1)S(1)}, bf16[256,2592]{1,0:T(8,128)(2,1)S(1)}) custom-call(bf16[288,1792]{1,0:T(8,128)(2,1)S(1)} %get-tuple-element.69.zx_ref, bf16[96,1280]{1,0:T(8,128)(2,1)S(1)} %get-tuple-element.70.gpre_ref, ...), custom_call_target="tpu_custom_call" | custom-call | flops 2000000000 | bytes 6291456 | tf_op jit(solution)/shard_map/pallas_call | solution.py:539
  38.8 0.0 collective-permute-done.3.fm_ref
  38.9 1.6 %collective-permute-start.5 = (bf16[240,128]{1,0:T(8,128)(2,1)S(1)}, bf16[240,128]{1,0:T(8,128)(2,1)S(1)}, u32[]{:S(2)}, u32[]{:S(2)}) collective-permute-start(bf16[240,128]{1,0:T(8,128)(2,1)S(1)} %pad_maximum_fusion.4), channel_id=1, source_target_pairs={{0,1},{1,0},{2,3},{3,2},{4,5},{5,4},{6,7},{7,6},{8,9},{9,8},{10,11... | collective-permute-start | bytes 184328 | tf_op jit(solution)/shard_map/ppermute | solution.py:571
  40.5 2.7 %collective-permute-done.5 = bf16[240,128]{1,0:T(8,128)(2,1)S(1)} collective-permute-done((bf16[240,128]{1,0:T(8,128)(2,1)S(1)}, bf16[240,128]{1,0:T(8,128)(2,1)S(1)}, u32[]{:S(2)}, u32[]{:S(2)}) %collective-permute-start.5) | collective-permute-done | bytes 61472 | tf_op jit(solution)/shard_map/ppermute | solution.py:571
  43.2 8.7 %shard_map.106 = (bf16[288,1792]{1,0:T(8,128)(2,1)S(1)}, bf16[288,1792]{1,0:T(8,128)(2,1)S(1)}, f32[2,2048,128]{2,1,0:T(8,128)S(1)}, bf16[2,2048,128]{2,1,0:T(8,128)(2,1)}) custom-call(bf16[240,128]{1,0:T(8,128)(2,1)S(1)} %collective-permute-done.3.fm_ref, bf16[240,128]{1,0:T(8,128)(2,1)S(1)} %collective-permute-done.4.fp_ref, ...), custom_call_target="tpu_custom_call" | custom-call | flops 2000000000 | bytes 4194304 | tf_op jit(solution)/shard_map/pallas_call | solution.py:539
  51.9 1.0 copy-done.9
  52.9 1.0 copy-done.11
  53.8 2.4 %collective-permute-start.6 = (bf16[2,2048,128]{2,1,0:T(8,128)(2,1)}, bf16[2,2048,128]{2,1,0:T(8,128)(2,1)}, u32[]{:S(2)}, u32[]{:S(2)}) collective-permute-start(bf16[2,2048,128]{2,1,0:T(8,128)(2,1)} %get-tuple-element.83), channel_id=1, source_target_pairs={{0,2},{2,0},{4,6},{6,4},{1,3},{3,1},{5,7},{7,5},{8,10},{10,8},{12,... | collective-permute-start | bytes 3145736 | tf_op jit(solution)/shard_map/ppermute | solution.py:745
  56.2 2.6 %collective-permute-done.6 = bf16[2,2048,128]{2,1,0:T(8,128)(2,1)} collective-permute-done((bf16[2,2048,128]{2,1,0:T(8,128)(2,1)}, bf16[2,2048,128]{2,1,0:T(8,128)(2,1)}, u32[]{:S(2)}, u32[]{:S(2)}) %collective-permute-start.6) | collective-permute-done | bytes 1048608 | tf_op jit(solution)/shard_map/ppermute | solution.py:745
  58.9 1.5 %convert_add_fusion = f32[2,2048,128]{2,1,0:T(8,128)S(1)} fusion(f32[2,2048,128]{2,1,0:T(8,128)S(1)} %get-tuple-element.82, bf16[2,2048,128]{2,1,0:T(8,128)(2,1)} %collective-permute-done.6), kind=kLoop, calls=%fused_computation | loop fusion | flops 1048576 | bytes 5242880 | tf_op jit(solution)/shard_map/add | solution.py:745
  60.3 0.1 fusion.1
  60.4 3.2 %collective-permute-start.7 = (bf16[1024,128]{1,0:T(8,128)(2,1)S(1)}, bf16[1024,128]{1,0:T(8,128)(2,1)S(1)}, u32[]{:S(2)}, u32[]{:S(2)}) collective-permute-start(bf16[1024,128]{1,0:T(8,128)(2,1)S(1)} %get-tuple-element.84), channel_id=1, source_target_pairs={{0,4},{2,6},{4,0},{6,2},{1,5},{3,7},{5,1},{7,3},{8,12},{10,14},{12... | collective-permute-start | bytes 786440 | tf_op jit(solution)/shard_map/ppermute | solution.py:749
  63.6 1.5 %collective-permute-start.8 = (bf16[1024,128]{1,0:T(8,128)(2,1)S(1)}, bf16[1024,128]{1,0:T(8,128)(2,1)S(1)}, u32[]{:S(2)}, u32[]{:S(2)}) collective-permute-start(bf16[1024,128]{1,0:T(8,128)(2,1)S(1)} %get-tuple-element.85), channel_id=1, source_target_pairs={{0,1},{1,0},{2,3},{3,2},{4,5},{5,4},{6,7},{7,6},{8,9},{9,8},{10,11... | collective-permute-start | bytes 786440 | tf_op jit(solution)/shard_map/ppermute | solution.py:750
  65.1 7.1 %shard_map.107 = bf16[2,256,512]{2,1,0:T(8,128)(2,1)} custom-call(s32[2,18]{1,0:T(2,128)S(1)} %copy-done.8, bf16[288,1792]{1,0:T(8,128)(2,1)S(1)} %copy-done.12, bf16[256,2592]{1,0:T(8,128)(2,1)S(1)} %get-tuple-element.87.wbt_hbm), custom_call_target="tpu_custom_call" | custom-call | flops 2000000000 | bytes 3145728 | tf_op jit(solution)/shard_map/pallas_call | solution.py:539
  72.3 0.1 bitcast_add_fusion
  72.5 0.0 copy-start.4
  72.5 0.1 collective-permute-start.11
  72.7 1.2 %collective-permute-start.9 = (bf16[512,128]{1,0:T(8,128)(2,1)S(1)}, bf16[512,128]{1,0:T(8,128)(2,1)S(1)}, u32[]{:S(2)}, u32[]{:S(2)}) collective-permute-start(bf16[512,128]{1,0:T(8,128)(2,1)S(1)} %select_convert_fusion.3), channel_id=1, source_target_pairs={{0,1},{1,0},{2,3},{3,2},{4,5},{5,4},{6,7},{7,6},{8,9},{9,8},{10,11... | collective-permute-start | bytes 393224 | tf_op jit(solution)/shard_map/ppermute | solution.py:757
  73.9 3.6 %collective-permute-done.11 = bf16[512,128]{1,0:T(8,128)(2,1)S(1)} collective-permute-done((bf16[512,128]{1,0:T(8,128)(2,1)S(1)}, bf16[512,128]{1,0:T(8,128)(2,1)S(1)}, u32[]{:S(2)}, u32[]{:S(2)}) %collective-permute-start.11) | collective-permute-done | bytes 131104 | tf_op jit(solution)/shard_map/ppermute | solution.py:758
  77.6 0.4 collective-permute-start.12
  78.1 1.0 collective-permute-start.10
  79.0 3.6 %collective-permute-done.12 = bf16[512,128]{1,0:T(8,128)(2,1)S(1)} collective-permute-done((bf16[512,128]{1,0:T(8,128)(2,1)S(1)}, bf16[512,128]{1,0:T(8,128)(2,1)S(1)}, u32[]{:S(2)}, u32[]{:S(2)}) %collective-permute-start.12) | collective-permute-done | bytes 131104 | tf_op jit(solution)/shard_map/ppermute | solution.py:770
  82.6 0.4 collective-permute-done.10
  83.2 1.7 %collective-permute-start.13 = (bf16[1024,128]{1,0:T(8,128)(2,1)S(1)}, bf16[1024,128]{1,0:T(8,128)(2,1)S(1)}, u32[]{:S(2)}, u32[]{:S(2)}) collective-permute-start(bf16[1024,128]{1,0:T(8,128)(2,1)S(1)} %get-tuple-element.92), channel_id=1, source_target_pairs={{0,4},{2,6},{4,0},{6,2},{1,5},{3,7},{5,1},{7,3},{8,12},{10,14},{12... | collective-permute-start | bytes 786440 | tf_op jit(solution)/shard_map/ppermute | solution.py:773
  84.9 0.9 collective-permute-start.14
  85.8 4.7 %shard_map.108 = bf16[2,96,512]{2,1,0:T(8,128)(2,1)} custom-call(s32[2,18]{1,0:T(2,128)S(1)} %copy-done.8, bf16[288,1792]{1,0:T(8,128)(2,1)S(1)} %copy-done.10, bf16[27,96,96]{2,1,0:T(8,128)(2,1)S(1)} %copy-done.4), custom_call_target="tpu_custom_call" | custom-call | flops 2000000000 | bytes 2097152 | tf_op jit(solution)/shard_map/pallas_call | solution.py:539
  90.5 0.0 collective-permute-done.13
  90.5 0.7 collective-permute-done.14
  91.4 0.1 pad_maximum_fusion.mine_ref
  91.6 0.1 collective-permute-start.15
  91.6 2.6 %collective-permute-done.15.other_ref = bf16[2,2048,128]{2,1,0:T(8,128)(2,1)S(1)} collective-permute-done((bf16[2,2048,128]{2,1,0:T(8,128)(2,1)S(1)}, bf16[2,2048,128]{2,1,0:T(8,128)(2,1)S(1)}, u32[]{:S(2)}, u32[]{:S(2)}) %collective-permute-start.15) | collective-permute-done | bytes 1048608 | tf_op jit(solution)/shard_map/ppermute | solution.py:778
  94.3 2.2 %shard_map.109 = (f32[27,96,96]{2,1,0:T(8,128)}, f32[27,96,256]{2,1,0:T(8,128)}) custom-call(bf16[2,2048,128]{2,1,0:T(8,128)(2,1)S(1)} %pad_maximum_fusion.mine_ref, bf16[2,2048,128]{2,1,0:T(8,128)(2,1)S(1)} %collective-permute-done.15.other_ref), custom_call_target="tpu_custom_call" | custom-call | bytes 6291456 | tf_op jit(solution)/shard_map/pallas_call | solution.py:539
  (39 shorter events, 0.4 us)
Async XLA Ops:
  0.6 19.0 %copy-start.6 = (s32[2,2,2]{2,1,0:T(2,128)S(1)}, s32[2,2,2]{2,1,0:T(2,128)}, u32[]{:S(2)}) copy-start(s32[2,2,2]{2,1,0:T(2,128)} %send_ref.5) | copy-start | bytes 100
  0.6 19.0 %copy-start.8 = (s32[2,18]{1,0:T(2,128)S(1)}, s32[2,18]{1,0:T(2,128)}, u32[]{:S(2)}) copy-start(s32[2,18]{1,0:T(2,128)} %occ_ref.7) | copy-start | bytes 436
  3.3 16.3 %copy-start = (bf16[27,96,256]{2,1,0:T(8,128)(2,1)S(1)}, bf16[27,96,256]{2,1,0:T(8,128)(2,1)}, u32[]{:S(2)}) copy-start(bf16[27,96,256]{2,1,0:T(8,128)(2,1)} %wb_ref.3) | copy-start | bytes 3981316
  3.3 11.1 %collective-permute-start = (bf16[440,128]{1,0:T(8,128)(2,1)}, bf16[440,128]{1,0:T(8,128)(2,1)S(1)}, u32[]{:S(2)}, u32[]{:S(2)}) collective-permute-start(bf16[440,128]{1,0:T(8,128)(2,1)} %get-tuple-element.52), channel_id=1, source_target_pairs={{0,2},{2,4},{4,6},{1,3},{3,5},{5,7},{8,10},{10,12},{12,14},{9,11},... | collective-permute-start | bytes 337928 | tf_op jit(solution)/shard_map/ppermute | solution.py:553
  5.8 8.6 %collective-permute-start.1 = (bf16[440,128]{1,0:T(8,128)(2,1)}, bf16[440,128]{1,0:T(8,128)(2,1)S(1)}, u32[]{:S(2)}, u32[]{:S(2)}) collective-permute-start(bf16[440,128]{1,0:T(8,128)(2,1)} %get-tuple-element.53), channel_id=1, source_target_pairs={{2,0},{4,2},{6,4},{3,1},{5,3},{7,5},{10,8},{12,10},{14,12},{11,9},... | collective-permute-start | bytes 337928 | tf_op jit(solution)/shard_map/ppermute | solution.py:554
  7.1 1.1 %copy-start.1 = (bf16[2,352,512]{2,1,0:T(8,128)(2,1)S(1)}, bf16[2,352,512]{2,1,0:T(8,128)(2,1)}, u32[]{:S(2)}) copy-start(bf16[2,352,512]{2,1,0:T(8,128)(2,1)} %get-tuple-element.55.own_ref) | copy-start | bytes 2162692
  8.2 1.1 %copy-start.3 = (bf16[27,96,96]{2,1,0:T(8,128)(2,1)S(1)}, bf16[27,96,96]{2,1,0:T(8,128)(2,1)}, u32[]{:S(2)}) copy-start(bf16[27,96,96]{2,1,0:T(8,128)(2,1)} %wa_hbm.1) | copy-start | bytes 1492996
  9.3 0.7 copy-start.5
  10.0 0.7 copy-start.7
  10.7 3.8 %copy-start.13 = (bf16[1,352,128]{2,1,0:T(8,128)(2,1)S(1)}, bf16[1,352,128]{2,1,0:T(8,128)(2,1)}, u32[]{:S(2)}) copy-start(bf16[1,352,128]{2,1,0:T(8,128)(2,1)} %get-tuple-element.61) | copy-start | bytes 270340
  10.7 8.9 %copy-start.2 = (bf16[2,352,512]{2,1,0:T(8,128)(2,1)S(1)}, bf16[2,352,512]{2,1,0:T(8,128)(2,1)}, u32[]{:S(2)}) copy-start(bf16[2,352,512]{2,1,0:T(8,128)(2,1)} %get-tuple-element.55.own_ref) | copy-start | bytes 2162692
  14.5 5.1 %collective-permute-start.2 = (bf16[440,128]{1,0:T(8,128)(2,1)S(1)}, bf16[440,128]{1,0:T(8,128)(2,1)S(1)}, u32[]{:S(2)}, u32[]{:S(2)}) collective-permute-start(bf16[440,128]{1,0:T(8,128)(2,1)S(1)} %pad_maximum_fusion.3), channel_id=1, source_target_pairs={{0,1},{1,0},{2,3},{3,2},{4,5},{5,4},{6,7},{7,6},{8,9},{9,8},{10,11... | collective-permute-start | bytes 337928 | tf_op jit(solution)/shard_map/ppermute | solution.py:571
  28.8 10.1 %collective-permute-start.3 = (bf16[240,128]{1,0:T(8,128)(2,1)S(1)}, bf16[240,128]{1,0:T(8,128)(2,1)S(1)}, u32[]{:S(2)}, u32[]{:S(2)}) collective-permute-start(bf16[240,128]{1,0:T(8,128)(2,1)S(1)} %get-tuple-element.66), channel_id=1, source_target_pairs={{0,2},{2,4},{4,6},{1,3},{3,5},{5,7},{8,10},{10,12},{12,14},{9,11},... | collective-permute-start | bytes 184328 | tf_op jit(solution)/shard_map/ppermute | solution.py:553
  32.5 6.4 %collective-permute-start.4 = (bf16[240,128]{1,0:T(8,128)(2,1)S(1)}, bf16[240,128]{1,0:T(8,128)(2,1)S(1)}, u32[]{:S(2)}, u32[]{:S(2)}) collective-permute-start(bf16[240,128]{1,0:T(8,128)(2,1)S(1)} %get-tuple-element.67), channel_id=1, source_target_pairs={{2,0},{4,2},{6,4},{3,1},{5,3},{7,5},{10,8},{12,10},{14,12},{11,9},... | collective-permute-start | bytes 184328 | tf_op jit(solution)/shard_map/ppermute | solution.py:554
  38.9 4.3 %collective-permute-start.5 = (bf16[240,128]{1,0:T(8,128)(2,1)S(1)}, bf16[240,128]{1,0:T(8,128)(2,1)S(1)}, u32[]{:S(2)}, u32[]{:S(2)}) collective-permute-start(bf16[240,128]{1,0:T(8,128)(2,1)S(1)} %pad_maximum_fusion.4), channel_id=1, source_target_pairs={{0,1},{1,0},{2,3},{3,2},{4,5},{5,4},{6,7},{7,6},{8,9},{9,8},{10,11... | collective-permute-start | bytes 184328 | tf_op jit(solution)/shard_map/ppermute | solution.py:571
  51.9 1.0 copy-start.9
  52.9 1.0 copy-start.11
  53.8 5.0 %collective-permute-start.6 = (bf16[2,2048,128]{2,1,0:T(8,128)(2,1)}, bf16[2,2048,128]{2,1,0:T(8,128)(2,1)}, u32[]{:S(2)}, u32[]{:S(2)}) collective-permute-start(bf16[2,2048,128]{2,1,0:T(8,128)(2,1)} %get-tuple-element.83), channel_id=1, source_target_pairs={{0,2},{2,0},{4,6},{6,4},{1,3},{3,1},{5,7},{7,5},{8,10},{10,8},{12,... | collective-permute-start | bytes 3145736 | tf_op jit(solution)/shard_map/ppermute | solution.py:745
  58.8 6.3 %copy-start.12 = (bf16[288,1792]{1,0:T(8,128)(2,1)S(1)}, bf16[288,1792]{1,0:T(8,128)(2,1)}, u32[]{:S(2)}) copy-start(bf16[288,1792]{1,0:T(8,128)(2,1)} %copy-done.11) | copy-start | bytes 3096580
  60.4 11.8 %collective-permute-start.7 = (bf16[1024,128]{1,0:T(8,128)(2,1)S(1)}, bf16[1024,128]{1,0:T(8,128)(2,1)S(1)}, u32[]{:S(2)}, u32[]{:S(2)}) collective-permute-start(bf16[1024,128]{1,0:T(8,128)(2,1)S(1)} %get-tuple-element.84), channel_id=1, source_target_pairs={{0,4},{2,6},{4,0},{6,2},{1,5},{3,7},{5,1},{7,3},{8,12},{10,14},{12... | collective-permute-start | bytes 786440 | tf_op jit(solution)/shard_map/ppermute | solution.py:749
  63.6 8.7 %collective-permute-start.8 = (bf16[1024,128]{1,0:T(8,128)(2,1)S(1)}, bf16[1024,128]{1,0:T(8,128)(2,1)S(1)}, u32[]{:S(2)}, u32[]{:S(2)}) collective-permute-start(bf16[1024,128]{1,0:T(8,128)(2,1)S(1)} %get-tuple-element.85), channel_id=1, source_target_pairs={{0,1},{1,0},{2,3},{3,2},{4,5},{5,4},{6,7},{7,6},{8,9},{9,8},{10,11... | collective-permute-start | bytes 786440 | tf_op jit(solution)/shard_map/ppermute | solution.py:750
  72.5 13.3 %copy-start.4 = (bf16[27,96,96]{2,1,0:T(8,128)(2,1)S(1)}, bf16[27,96,96]{2,1,0:T(8,128)(2,1)}, u32[]{:S(2)}) copy-start(bf16[27,96,96]{2,1,0:T(8,128)(2,1)} %wa_hbm.1) | copy-start | bytes 1492996
  72.5 13.3 %copy-start.10 = (bf16[288,1792]{1,0:T(8,128)(2,1)S(1)}, bf16[288,1792]{1,0:T(8,128)(2,1)}, u32[]{:S(2)}) copy-start(bf16[288,1792]{1,0:T(8,128)(2,1)} %copy-done.9) | copy-start | bytes 3096580
  72.5 5.0 %collective-permute-start.11 = (bf16[512,128]{1,0:T(8,128)(2,1)S(1)}, bf16[512,128]{1,0:T(8,128)(2,1)S(1)}, u32[]{:S(2)}, u32[]{:S(2)}) collective-permute-start(bf16[512,128]{1,0:T(8,128)(2,1)S(1)} %select_convert_fusion.2), channel_id=1, source_target_pairs={{0,4},{2,6},{4,0},{6,2},{1,5},{3,7},{5,1},{7,3},{8,12},{10,14},{12... | collective-permute-start | bytes 393224 | tf_op jit(solution)/shard_map/ppermute | solution.py:758
  72.7 5.3 %collective-permute-start.9 = (bf16[512,128]{1,0:T(8,128)(2,1)S(1)}, bf16[512,128]{1,0:T(8,128)(2,1)S(1)}, u32[]{:S(2)}, u32[]{:S(2)}) collective-permute-start(bf16[512,128]{1,0:T(8,128)(2,1)S(1)} %select_convert_fusion.3), channel_id=1, source_target_pairs={{0,1},{1,0},{2,3},{3,2},{4,5},{5,4},{6,7},{7,6},{8,9},{9,8},{10,11... | collective-permute-start | bytes 393224 | tf_op jit(solution)/shard_map/ppermute | solution.py:757
  77.6 5.0 %collective-permute-start.12 = (bf16[512,128]{1,0:T(8,128)(2,1)S(1)}, bf16[512,128]{1,0:T(8,128)(2,1)S(1)}, u32[]{:S(2)}, u32[]{:S(2)}) collective-permute-start(bf16[512,128]{1,0:T(8,128)(2,1)S(1)} %add_convert_fusion), channel_id=1, source_target_pairs={{0,4},{2,6},{4,0},{6,2},{1,5},{3,7},{5,1},{7,3},{8,12},{10,14},{12... | collective-permute-start | bytes 393224 | tf_op jit(solution)/shard_map/ppermute | solution.py:770
  78.1 5.0 %collective-permute-start.10 = (bf16[512,128]{1,0:T(8,128)(2,1)S(1)}, bf16[512,128]{1,0:T(8,128)(2,1)S(1)}, u32[]{:S(2)}, u32[]{:S(2)}) collective-permute-start(bf16[512,128]{1,0:T(8,128)(2,1)S(1)} %add_convert_fusion.1), channel_id=1, source_target_pairs={{0,1},{1,0},{2,3},{3,2},{4,5},{5,4},{6,7},{7,6},{8,9},{9,8},{10,11... | collective-permute-start | bytes 393224 | tf_op jit(solution)/shard_map/ppermute | solution.py:769
  83.2 7.4 %collective-permute-start.13 = (bf16[1024,128]{1,0:T(8,128)(2,1)S(1)}, bf16[1024,128]{1,0:T(8,128)(2,1)S(1)}, u32[]{:S(2)}, u32[]{:S(2)}) collective-permute-start(bf16[1024,128]{1,0:T(8,128)(2,1)S(1)} %get-tuple-element.92), channel_id=1, source_target_pairs={{0,4},{2,6},{4,0},{6,2},{1,5},{3,7},{5,1},{7,3},{8,12},{10,14},{12... | collective-permute-start | bytes 786440 | tf_op jit(solution)/shard_map/ppermute | solution.py:773
  84.9 6.4 %collective-permute-start.14 = (bf16[1024,128]{1,0:T(8,128)(2,1)S(1)}, bf16[1024,128]{1,0:T(8,128)(2,1)S(1)}, u32[]{:S(2)}, u32[]{:S(2)}) collective-permute-start(bf16[1024,128]{1,0:T(8,128)(2,1)S(1)} %get-tuple-element.93), channel_id=1, source_target_pairs={{0,1},{1,0},{2,3},{3,2},{4,5},{5,4},{6,7},{7,6},{8,9},{9,8},{10,11... | collective-permute-start | bytes 786440 | tf_op jit(solution)/shard_map/ppermute | solution.py:774
  91.6 2.7 %collective-permute-start.15 = (bf16[2,2048,128]{2,1,0:T(8,128)(2,1)S(1)}, bf16[2,2048,128]{2,1,0:T(8,128)(2,1)S(1)}, u32[]{:S(2)}, u32[]{:S(2)}) collective-permute-start(bf16[2,2048,128]{2,1,0:T(8,128)(2,1)S(1)} %pad_maximum_fusion.mine_ref), channel_id=1, source_target_pairs={{0,2},{2,0},{4,6},{6,4},{1,3},{3,1},{5,7},{7,5},{8,10},{10,8},{12,... | collective-permute-start | bytes 3145736 | tf_op jit(solution)/shard_map/ppermute | solution.py:778

commit v2 on v1

--- a/solution.py
+++ b/solution.py
@@ -78,6 +78,11 @@
     return q if receiving else 1 - q
 
 
+def x_side(which):
+    odd = lax.axis_index("gx") & 1
+    return odd if which else 1 - odd
+
+
 def send_choices(send_ref, dirs):
     places = slot_places(send_ref)
 
@@ -86,7 +91,8 @@
 
     along_x = []
     lane = iota((FACE, FACE), 1)
-    for side in (1, 0):
+    for which in range(2):
+        side = x_side(which)
         i, j, l = split(iota((FACE, FACE), 0) + 384 * side)
         ahead = jnp.int32(0)
         picks = []
@@ -120,13 +126,13 @@
     return along_x, along_y
 
 
-def pack_sends(own_ref, send_ref, dirs, plus_ref, minus_ref, y_ref):
+def pack_sends(own_ref, send_ref, dirs, one_ref, two_ref, y_ref):
     channels = own_ref.shape[1]
     group = channels // 4
     along_x, along_y = send_choices(send_ref, dirs)
     glane = iota((group, FACE), 1) >> 5
-    for side, picks, ref in ((1, along_x[0], plus_ref), (0, along_x[1], minus_ref)):
-        lanes = slice(384 * side, 384 * side + 128)
+    for which, (picks, ref) in enumerate(zip(along_x, (one_ref, two_ref))):
+        lanes = pl.ds(pl.multiple_of(384 * x_side(which), 128), 128)
         wide = jnp.dot(own_ref[0, :, lanes], picks[0], preferred_element_type=F32) + jnp.dot(
             own_ref[1, :, lanes], picks[1], preferred_element_type=F32
         )
@@ -205,10 +211,11 @@
     )
     across = jnp.where(high, firsts[1], firsts[0])
     depth = jnp.where(high, depths[1], depths[0])
-    for side in range(2):
+    for which in range(2):
+        side = x_side(which)
         put(
             sr_ref,
-            FACE * side,
+            FACE * which,
             FACE,
             encode(
                 nought + 9 * side,
@@ -267,11 +274,11 @@
         stat_ref[index] = one_hot(row == target[:1])
 
 
-def fill_padded(own_ref, part_ref, recv_minus, recv_plus, recv_y, sr_ref, stat_ref, d_ref, xh_ref, dirs, outs, ready):
+def fill_padded(own_ref, part_ref, recv_one, recv_two, recv_y, sr_ref, stat_ref, d_ref, xh_ref, dirs, outs):
     channels = own_ref.shape[1]
     group = channels // 4
-    d_ref[:, :FACE] = recv_minus[:channels, :]
-    d_ref[:, FACE : 2 * FACE] = recv_plus[:channels, :]
+    d_ref[:, :FACE] = recv_one[:channels, :]
+    d_ref[:, FACE : 2 * FACE] = recv_two[:channels, :]
     glane = iota((group, FACE), 1) >> 5
     for q in range(dirs):
         at = FACE * (2 + q)
@@ -280,9 +287,7 @@
         spread = jnp.concatenate([jnp.where(glane == g, packed, 0.0) for g in range(4)], axis=0)
         at = FACE * (2 + dirs + q)
         d_ref[:, at : at + FACE] = spread.astype(BF)
-    ready(0)
     halos = [jnp.dot(d_ref[...], sr_ref[n], preferred_element_type=F32) for n in range(2)]
-    ready(1)
     for n in range(2):
         rows = slice(channels * n, channels * n + channels)
         xh_ref[rows, :VOX] = own_ref[n]
@@ -306,16 +311,6 @@
             ref[2 * count :, at] = high
 
 
-def fill_patches(p_ref, z_ref):
-    for k in range(TAPS):
-        a, b, c = k // 9, k // 3 % 3, k % 3
-        for n in range(2):
-            at = PADDED * n + PLANE * a + 8 * b
-            p_ref[96 * k : 96 * k + 96, OUTER * n : OUTER * n + OUTER] = z_ref[
-                96 * c : 96 * c + 96, at : at + OUTER
-            ]
-
-
 def shifted_sum(s_ref, n, flip):
     total = None
     for ab in range(9):
@@ -342,37 +337,37 @@
     return copies
 
 
-def pack_kernel(dirs, feat_ref, cot_ref, occ_ref, send_ref, own_ref, plus_ref, minus_ref, y_ref):
+def pack_kernel(dirs, feat_ref, cot_ref, occ_ref, send_ref, own_ref, one_ref, two_ref, y_ref):
     for n in range(2):
         mask = lane_mask(occ_ref, n, VOX, 64)
         own_ref[n, :96, :] = jnp.where(mask > 0.5, feat_ref[n].astype(F32), 0.0).astype(BF)
         own_ref[n, 96:, :] = jnp.where(mask > 0.5, cot_ref[n].astype(F32), 0.0).astype(BF)
-    pack_sends(own_ref, send_ref, dirs, plus_ref, minus_ref, y_ref)
-
-
-def prepare_kernel(
-    dirs, own_ref, near_ref, send_ref, wa_ref,
-    so_ref, sr_ref, stat_ref, part_ref, wa9_ref,
-):
+    pack_sends(own_ref, send_ref, dirs, one_ref, two_ref, y_ref)
+
+
+def halo_kernel(dirs, own_ref, near_ref, send_ref, so_ref, sr_ref, part_ref):
     for n in range(2):
         halo_choice(so_ref, sr_ref, n, send_ref, near_ref, dirs)
-    padded_choice(stat_ref)
     for n in range(2):
         part_ref[n] = jnp.dot(own_ref[1 - n], so_ref[n], preferred_element_type=F32).astype(BF)
+
+
+def layout_kernel(wa_ref, wb_ref, stat_ref, wa9_ref, wbt_ref):
+    padded_choice(stat_ref)
     for k in range(TAPS):
         c, ab = k % 3, k // 3
         wa9_ref[96 * ab : 96 * ab + 96, 96 * c : 96 * c + 96] = wa_ref[k].astype(F32).T.astype(BF)
+        wbt_ref[:, 96 * k : 96 * k + 96] = wb_ref[k].astype(F32).T.astype(BF)
 
 
 def first_kernel(
-    dirs, fm_ref, fp_ref, fy_ref, sr_ref, occ_ref, send_ref, own_ref, part_ref, stat_ref, wa_ref, wb_ref,
-    zx_ref, gpre_ref, hid_ref, plus_ref, minus_ref, y_ref,
-    d_ref, xh_ref, zg_ref, s9_ref, pre_ref, wb9_ref,
+    dirs, f1_ref, f2_ref, fy_ref, sr_ref, occ_ref, send_ref, own_ref, part_ref, stat_ref, wa_ref, wb_ref,
+    zx_ref, zg_ref, gpre_ref, wide_ref, hid_ref, one_ref, two_ref, y_ref,
+    d_ref, xh_ref, s9_ref, pre_ref, wb9_ref,
 ):
     fill_padded(
-        own_ref, part_ref, fm_ref, fp_ref, fy_ref, sr_ref, stat_ref, d_ref, xh_ref, dirs,
+        own_ref, part_ref, f1_ref, f2_ref, fy_ref, sr_ref, stat_ref, d_ref, xh_ref, dirs,
         ((zx_ref, 0, 96, False), (zg_ref, 96, 256, True)),
-        lambda stage: None,
     )
     s9_ref[...] = jnp.dot(wa_ref[...], zx_ref[...], preferred_element_type=F32)
     for n in range(2):
@@ -392,72 +387,39 @@
             shifted_sum(s9_ref, n, True) * gate * (1.0 + pre * (1.0 - gate)) * mask
         ).astype(BF)
         gpre_ref[:, at] = grad_pre
+        wide_ref[:, at] = hidden
         both = jnp.concatenate([hidden, grad_pre], axis=0)
         hid_ref[n] = jnp.dot(both, squeeze, preferred_element_type=F32).astype(BF)
-    pack_sends(hid_ref, send_ref, dirs, plus_ref, minus_ref, y_ref)
-
-
-def weight_a_kernel(
-    scale, zx_ref, gpre_ref, own_ref, stat_ref, hid_ref, so_ref, wb_ref,
-    out_hbm, hpart_hbm, gout_hbm, wbt_hbm,
-    g9_ref, out_ref, hpart_ref, gout_ref, wbt_ref, sems,
-):
-    def store(source, target, k):
-        copy = pltpu.make_async_copy(source, target, sems.at[k])
-        copy.start()
-        return copy
-
-    for n in range(2):
-        hpart_ref[n] = jnp.dot(hid_ref[1 - n], so_ref[n], preferred_element_type=F32).astype(BF)
-        spread = jnp.dot(own_ref[n, 96:, :], stat_ref[0], preferred_element_type=F32)
-        gout_ref[:, OUTER * n : OUTER * n + OUTER] = spread[:, FIRST : FIRST + OUTER].astype(BF)
-    stores = [store(hpart_ref, hpart_hbm, 0), store(gout_ref, gout_hbm, 1)]
-    for k in range(TAPS):
-        wbt_ref[:, 96 * k : 96 * k + 96] = wb_ref[k].astype(F32).T.astype(BF)
-    stores.append(store(wbt_ref, wbt_hbm, 2))
+    pack_sends(hid_ref, send_ref, dirs, one_ref, two_ref, y_ref)
+
+
+def weights_kernel(scale, split, zx_ref, zg_ref, gpre_ref, wide_ref, keep_ref, *rest):
+    g9_ref, h9_ref, sum_ref = rest[-3:]
+    h9_ref[...] = jnp.zeros_like(h9_ref)
     g9_ref[...] = jnp.zeros_like(g9_ref)
     for ab in range(9):
         for n in range(2):
+            own = slice(OUTER * n, OUTER * n + OUTER)
+            at = PADDED * n + PLANE * (2 - ab // 3) + 8 * (2 - ab % 3)
+            h9_ref[96 * ab : 96 * ab + 96, at : at + OUTER] = wide_ref[:, own]
             at = PADDED * n + PLANE * (ab // 3) + 8 * (ab % 3)
-            g9_ref[128 * ab : 128 * ab + 96, at : at + OUTER] = gpre_ref[
-                :, OUTER * n : OUTER * n + OUTER
+            g9_ref[128 * ab : 128 * ab + 96, at : at + OUTER] = gpre_ref[:, own]
+    total = scale * lax.dot_general(h9_ref[...], zg_ref[...], NT, preferred_element_type=F32)
+    rows = TAPS * 96
+    sum_ref[:, rows:STORED, :] = jnp.zeros((2, STORED - rows, 128), F32)
+    sum_ref[:, STORED + 14 * 96 :, :] = jnp.zeros((2, HALF - STORED - 14 * 96, 128), F32)
+    sum_ref[1, STORED + 13 * 96 : STORED + 14 * 96, :] = jnp.zeros((96, 128), F32)
+    for k in range(TAPS):
+        c, ab = k % 3, k // 3
+        for half in range(2):
+            sum_ref[half, 96 * k : 96 * k + 96, :] = total[
+                96 * ab : 96 * ab + 96, 256 * c + 128 * half : 256 * c + 128 * half + 128
             ]
-    out_ref[...] = jnp.zeros_like(out_ref)
-    total = scale * lax.dot_general(
-        zx_ref[...], g9_ref[...], NT, preferred_element_type=F32
-    )
+    total = scale * lax.dot_general(zx_ref[...], g9_ref[...], NT, preferred_element_type=F32)
     for k in range(TAPS):
-        half, at = k // 14, 96 * (k % 14)
+        half, at = k // 14, STORED + 96 * (k % 14)
         c, ab = k % 3, k // 3
-        out_ref[half, at : at + 96, :] = total[96 * c : 96 * c + 96, 128 * ab : 128 * ab + 128]
-    stores.append(store(out_ref, out_hbm, 3))
-    for copy in stores:
-        copy.wait()
-
-
-def weight_b_kernel(
-    scale, dirs, split, fm_ref, fp_ref, fy_ref, own_ref, stat_ref,
-    sr_hbm, part_hbm, gout_hbm, wa_hbm, zh_hbm, zp_hbm, keep_ref, *rest,
-):
-    sr_ref, part_ref, gout_ref, wa_ref, zh_ref, zp_ref, d_ref, xh_ref, p_ref, sum_ref, sems = rest[-11:]
-    copies = fetch(
-        ((sr_hbm, sr_ref), (part_hbm, part_ref), (gout_hbm, gout_ref), (wa_hbm, wa_ref)), sems
-    )
-    fill_padded(
-        own_ref, part_ref, fm_ref, fp_ref, fy_ref, sr_ref, stat_ref, d_ref, xh_ref, dirs,
-        ((zh_ref, 0, 96, False), (zp_ref, 96, 96, True)),
-        lambda stage: copies[stage].wait(),
-    )
-    stores = fetch(((zh_ref, zh_hbm), (zp_ref, zp_hbm)), sems.at[pl.ds(4, 2)])
-    fill_patches(p_ref, zh_ref)
-    copies[2].wait()
-    rows = TAPS * 96
-    total = scale * lax.dot_general(p_ref[...], gout_ref[...], NT, preferred_element_type=F32)
-    copies[3].wait()
-    for half in range(2):
-        sum_ref[half, :rows, :] = total[:, 128 * half : 128 * half + 128]
-        sum_ref[half, rows:STORED, :] = jnp.zeros((STORED - rows, 128), F32)
-        sum_ref[half, STORED:, :] = wa_ref[half]
+        sum_ref[half, at : at + 96, :] = total[96 * c : 96 * c + 96, 128 * ab : 128 * ab + 128]
     if split:
         core = lax.axis_index("gx") & 1
         keep = pl.multiple_of(core * (HALF // 2), HALF // 2)
@@ -466,21 +428,36 @@
         rest[0][...] = sum_ref[:, pl.ds(send, HALF // 2), :].astype(BF)
     else:
         keep_ref[...] = sum_ref[...]
-    for store in stores:
-        store.wait()
-
-
-def out_kernel(occ_ref, zh_hbm, wbt_hbm, out_ref, p_ref, zh_ref, wbt_ref, sems):
-    copies = fetch(((zh_hbm, zh_ref), (wbt_hbm, wbt_ref)), sems)
+
+
+def second_kernel(
+    dirs, f1_ref, f2_ref, fy_ref, sr_ref, so_ref, own_ref, stat_ref, zh_ref, zp_ref, d_ref, xh_ref, part_ref
+):
+    for n in range(2):
+        part_ref[n] = jnp.dot(own_ref[1 - n], so_ref[n], preferred_element_type=F32).astype(BF)
+    fill_padded(
+        own_ref, part_ref, f1_ref, f2_ref, fy_ref, sr_ref, stat_ref, d_ref, xh_ref, dirs,
+        ((zh_ref, 0, 96, False), (zp_ref, 96, 96, True)),
+    )
+
+
+def out_kernel(n, occ_ref, zh_hbm, wbt_hbm, *rest):
+    out_hbm, p_ref, zh_ref, wbt_ref, out_ref, sems = rest[-6:]
+    lanes = pl.ds(PADDED * n, PADDED)
+    copies = fetch(((zh_hbm.at[:, lanes], zh_ref), (wbt_hbm, wbt_ref)), sems)
     squeeze = compaction()
     copies[0].wait()
-    fill_patches(p_ref, zh_ref)
+    for k in range(TAPS):
+        a, b, c = k // 9, k // 3 % 3, k % 3
+        at = PLANE * a + 8 * b
+        p_ref[96 * k : 96 * k + 96, :] = zh_ref[96 * c : 96 * c + 96, at : at + OUTER]
     copies[1].wait()
     total = jnp.dot(wbt_ref[...], p_ref[...], preferred_element_type=F32)
-    for n in range(2):
-        mask = lane_mask(occ_ref, n, OUTER, PLANE)
-        part = total[:, OUTER * n : OUTER * n + OUTER] * mask
-        out_ref[n] = jnp.dot(part.astype(BF), squeeze, preferred_element_type=F32).astype(BF)
+    total = (total * lane_mask(occ_ref, n, OUTER, PLANE)).astype(BF)
+    out_ref[...] = jnp.dot(total, squeeze, preferred_element_type=F32).astype(BF)
+    store = pltpu.make_async_copy(out_ref, out_hbm.at[n], sems.at[2])
+    store.start()
+    store.wait()
 
 
 def grad_kernel(occ_ref, zp_hbm, wa_hbm, grad_ref, s9_ref, wg9_ref, zp_ref, wa_ref, sems):
@@ -526,7 +503,7 @@
         copy.wait()
 
 
-def call(kernel, outs, ins, scratch=(), flops=0, moved=0, far_ins=0, far_outs=0, sems=0, limit=LIMIT):
+def call(kernel, outs, ins, scratch=(), flops=0, moved=0, far_ins=0, far_outs=0, sems=0, limit=LIMIT, aliases={}):
     specs = [SMEM if jnp.issubdtype(x.dtype, jnp.integer) else VMEM for x in ins]
     for k in range(far_ins):
         specs[len(ins) - 1 - k] = FAR_SPEC
@@ -542,18 +519,21 @@
         in_specs=specs,
         out_specs=out_specs,
         scratch_shapes=scratch,
+        input_output_aliases=aliases,
         compiler_params=pltpu.CompilerParams(vmem_limit_bytes=limit),
         cost_estimate=pl.CostEstimate(flops=flops, bytes_accessed=moved, transcendentals=0),
     )(*ins)
 
 
-def exchange(channels, plus, minus, faces, count_x, count_y, cover):
-    up = [(k, k + 1) for k in range(count_x - 1)]
-    down = [(k + 1, k) for k in range(count_x - 1)]
-    from_minus = lax.ppermute(plus, "gx", up)
-    from_plus = lax.ppermute(minus, "gx", down)
-    covered = cover()
-    faces, covered = lax.optimization_barrier((faces, covered))
+def exchange_x(one, two, count_x):
+    def pairs(first):
+        starts = range(first, count_x - 1, 2)
+        return [(k, k + 1) for k in starts] + [(k + 1, k) for k in starts]
+
+    return lax.ppermute(one, "gx", pairs(0)), lax.ppermute(two, "gx", pairs(1))
+
+
+def exchange_y(channels, faces, from_one, from_two, count_y):
     group = channels // 4
     dirs = faces.shape[0]
     if dirs == 1:
@@ -566,17 +546,26 @@
     arrived = []
     for q in range(dirs):
         at = channels + group * q
-        edges = from_minus[at : at + group] + from_plus[at : at + group]
+        edges = from_one[at : at + group] + from_two[at : at + group]
         arrived.append(
             lax.ppermute(jnp.concatenate([faces[q], edges], axis=0), "gy", perms[q])
         )
-    return from_minus, from_plus, jnp.stack(arrived, axis=0), covered
+    return jnp.stack(arrived, axis=0)
+
+
+def half_rows(piece, which):
+    rows = piece.shape[0] // 2
+    return lax.dynamic_slice_in_dim(piece, which * rows, rows, axis=0)
 
 
 def swap_or_keep(piece, bit):
     rows = piece.shape[0] // 2
     low, high = piece[:rows], piece[rows:]
     return jnp.where(bit == 0, high, low).astype(BF), jnp.where(bit == 0, low, high)
+
+
+def half_sum(kept, got, which):
+    return half_rows(kept, which) + half_rows(got, which).astype(F32)
 
 
 def body(features, occupancy, neighbours, send_slots, weight_a, weight_b, cotangent):
@@ -590,7 +579,7 @@
     outer = 2 * OUTER
 
     rows = 352 + 88 * dirs
-    own, plus, minus, faces = call(
+    own, one, two, faces = call(
         functools.partial(pack_kernel, dirs),
         [((2, 352, VOX), BF), ((rows, FACE), BF), ((rows, FACE), BF), ((dirs, 352, FACE), BF)],
         [features, cotangent, occupancy, send_slots],
@@ -598,32 +587,34 @@
         moved=2 * 1024 * 1024,
     )
 
-    def prepare():
-        return call(
-            functools.partial(prepare_kernel, dirs),
-            [
-                ((2, VOX, HALO), BF),
-                ((2, lanes, HALO), BF),
-                ((3, HALO, PADDED), BF),
-                ((2, 352, HALO), BF),
-                ((864, 288), BF),
-            ],
-            [own, neighbours, send_slots, weight_a],
-            flops=10**9,
-            moved=8 * MIB,
-            limit=8 * MIB,
-        )
-
-    from_minus, from_plus, from_y, prepared = exchange(
-        352, plus, minus, faces, count_x, count_y, prepare
-    )
-    halo_own, halo_far, padded, part, wa9 = prepared
+    from_one, from_two = exchange_x(one, two, count_x)
+    halo_own, halo_far, part = call(
+        functools.partial(halo_kernel, dirs),
+        [((2, VOX, HALO), BF), ((2, lanes, HALO), BF), ((2, 352, HALO), BF)],
+        [own, neighbours, send_slots],
+        flops=10**9,
+        moved=4 * MIB,
+    )
+    faces, part = lax.optimization_barrier((faces, part))
+    from_y = exchange_y(352, faces, from_one, from_two, count_y)
+    weight_a, weight_b, part = lax.optimization_barrier((weight_a, weight_b, part))
+    padded, wa9, wbt = call(
+        layout_kernel,
+        [((3, HALO, PADDED), BF), ((864, 288), BF), ((256, TAPS * 96), BF)],
+        [weight_a, weight_b],
+        moved=6 * MIB,
+        flops=10**8,
+        limit=8 * MIB,
+    )
+    from_y, padded = lax.optimization_barrier((from_y, padded))
 
     rows = 192 + 48 * dirs
-    zx, gpre, hid, plus, minus, faces = call(
+    zx, zg, gpre, hidden, hid, one, two, faces = call(
         functools.partial(first_kernel, dirs),
         [
             ((288, wide), BF),
+            ((768, wide), BF),
+            ((96, outer), BF),
             ((96, outer), BF),
             ((2, 192, VOX), BF),
             ((rows, FACE), BF),
@@ -631,13 +622,12 @@
             ((dirs, 192, FACE), BF),
         ],
         [
-            from_minus, from_plus, from_y, halo_far, occupancy, send_slots,
+            from_one, from_two, from_y, halo_far, occupancy, send_slots,
             own, part, padded, wa9, weight_b,
         ],
         [
             ((352, lanes), BF),
             ((704, 1024), BF),
-            ((768, wide), BF),
             ((864, wide), F32),
             ((96, outer), F32),
             ((864, 768), BF),
@@ -646,73 +636,47 @@
         moved=8 * MIB,
         limit=20 * MIB,
     )
-
-    def first_weights():
-        return call(
-            functools.partial(weight_a_kernel, scale),
-            [
-                ((2, HALF - STORED, 128), F32),
-                ((2, 192, HALO), BF),
-                ((256, outer), BF),
-                ((256, TAPS * 96), BF),
-            ],
-            [zx, gpre, own, padded, hid, halo_own, weight_b],
-            [
-                ((9 * 128, wide), BF),
-                ((2, HALF - STORED, 128), F32),
-                ((2, 192, HALO), BF),
-                ((256, outer), BF),
-                ((256, TAPS * 96), BF),
-            ],
-            flops=2 * 10**9,
-            moved=6 * MIB,
-            far_outs=4,
-            sems=4,
-            limit=20 * MIB,
-        )
-
-    from_minus, from_plus, from_y, covered = exchange(
-        192, plus, minus, faces, count_x, count_y, first_weights
-    )
-    grad_wa, hpart, gout, wbt = covered
+    from_one, from_two = exchange_x(one, two, count_x)
     sums = [((2, HALF, 128), F32)]
     if split:
         sums = [((2, HALF // 2, 128), F32), ((2, HALF // 2, 128), BF)]
-    zh, zp, *sums = call(
-        functools.partial(weight_b_kernel, scale, dirs, split),
-        [((288, wide), BF), ((288, wide), BF)] + sums,
-        [from_minus, from_plus, from_y, hid, padded, halo_far, hpart, gout, grad_wa],
-        [
-            ((2, lanes, HALO), BF),
-            ((2, 192, HALO), BF),
-            ((256, outer), BF),
-            ((2, HALF - STORED, 128), F32),
-            ((288, wide), BF),
-            ((288, wide), BF),
-            ((192, lanes), BF),
-            ((384, 1024), BF),
-            ((TAPS * 96, outer), BF),
-            ((2, HALF, 128), F32),
-        ],
-        flops=2 * 10**9,
-        moved=4 * MIB,
-        far_ins=4,
-        far_outs=2,
-        sems=6,
-        limit=22 * MIB,
-    )
-
-    def layer(zh):
+    sums = call(
+        functools.partial(weights_kernel, scale, split),
+        sums,
+        [zx, zg, gpre, hidden],
+        [((9 * 128, wide), BF), ((9 * 96, wide), BF), ((2, HALF, 128), F32)],
+        flops=5 * 10**9,
+        moved=6 * MIB,
+        limit=24 * MIB,
+    )
+
+    from_one, from_two, sums = lax.optimization_barrier((from_one, from_two, sums))
+    from_y = exchange_y(192, faces, from_one, from_two, count_y)
+
+    def second(from_one, from_two, from_y):
         return call(
-            out_kernel,
+            functools.partial(second_kernel, dirs),
+            [((288, wide), BF), ((288, wide), BF)],
+            [from_one, from_two, from_y, halo_far, halo_own, hid, padded],
+            [((192, lanes), BF), ((384, 1024), BF), ((2, 192, HALO), BF)],
+            flops=2 * 10**9,
+            moved=6 * MIB,
+            limit=14 * MIB,
+        )
+
+    def layer(n, zh, wbt, *earlier):
+        return call(
+            functools.partial(out_kernel, n),
             [((2, 256, VOX), BF)],
-            [occupancy, zh, wbt],
-            [((TAPS * 96, outer), BF), ((288, wide), BF), ((256, TAPS * 96), BF)],
-            flops=2 * 10**9,
-            moved=3 * MIB,
-            far_ins=2,
-            sems=2,
-            limit=20 * MIB,
+            [occupancy, zh, wbt, *earlier],
+            [((TAPS * 96, OUTER), BF), ((288, PADDED), BF), ((256, TAPS * 96), BF), ((256, VOX), BF)],
+            flops=10**9,
+            moved=2 * MIB,
+            far_ins=2 + len(earlier),
+            far_outs=1,
+            sems=3,
+            limit=14 * MIB,
+            aliases={3: 0} if earlier else {},
         )[0]
 
     def data_grad(zp):
@@ -729,12 +693,14 @@
         )[0]
 
     if not split:
+        zh, zp = second(from_one, from_two, from_y)
         total = lax.psum(sums[0], ("gx", "gy"))
         grad_wb = jnp.concatenate([total[0, : TAPS * 96], total[1, : TAPS * 96]], axis=1)
         first = total[0, STORED : STORED + 14 * 96, :96]
         second = total[1, STORED : STORED + 13 * 96, :96]
         grad_wa = jnp.concatenate([first, second], axis=0)
-        return layer(zh), data_grad(zp), grad_wa.reshape(TAPS, 96, 96), grad_wb.reshape(TAPS, 96, 256)
+        layer_out = layer(1, zh, wbt, layer(0, zh, wbt))
+        return layer_out, data_grad(zp), grad_wa.reshape(TAPS, 96, 96), grad_wb.reshape(TAPS, 96, 256)
 
     along_y = ("gx", [(k, k ^ 2) for k in range(4)])
     along_x = ("gy", [(0, 1), (1, 0)])
@@ -742,22 +708,34 @@
     bit_x = lax.axis_index("gy")
     swap = ("gx", [(k, k ^ 1) for k in range(4)])
     keep, send = sums
-    summed = keep + lax.ppermute(send, *swap).astype(F32)
-    send_a, keep_a = swap_or_keep(summed[0], bit_y)
-    send_b, keep_b = swap_or_keep(summed[1], bit_x)
-    zh, send_a, send_b = lax.optimization_barrier((zh, send_a, send_b))
+    got = lax.ppermute(send, *swap)
+    zh, zp = second(from_one, from_two, from_y)
+    got, zh, zp = lax.optimization_barrier((got, zh, zp))
+    send_a = half_sum(keep[0], got[0], 1 - bit_y).astype(BF)
+    send_b = half_sum(keep[1], got[1], 1 - bit_x).astype(BF)
+    send_a, send_b, keep, got, zh = lax.optimization_barrier((send_a, send_b, keep, got, zh))
     got_a = lax.ppermute(send_a, *along_y)
     got_b = lax.ppermute(send_b, *along_x)
-    layer_out = layer(zh)
-    got_a, got_b, layer_out = lax.optimization_barrier((got_a, got_b, layer_out))
-    half_a = keep_a + got_a.astype(F32)
-    half_b = keep_b + got_b.astype(F32)
-    send_a, keep_a = swap_or_keep(half_a, bit_x)
-    send_b, keep_b = swap_or_keep(half_b, bit_y)
-    got_a = lax.ppermute(send_a, *along_x)
-    got_b = lax.ppermute(send_b, *along_y)
-    part_a = (keep_a + got_a.astype(F32)).astype(BF)
-    part_b = (keep_b + got_b.astype(F32)).astype(BF)
+    keep_a = half_sum(keep[0], got[0], bit_y)
+    keep_b = half_sum(keep[1], got[1], bit_x)
+    layer_out = layer(0, zh, wbt)
+    got_a, got_b, layer_out, keep_a, keep_b = lax.optimization_barrier(
+        (got_a, got_b, layer_out, keep_a, keep_b)
+    )
+    send_a, keep_a = swap_or_keep(keep_a + got_a.astype(F32), bit_x)
+    send_b, keep_b = swap_or_keep(keep_b + got_b.astype(F32), bit_y)
+    zh, send_a, send_b = lax.optimization_barrier((zh, send_a, send_b))
+    other_a = lax.ppermute(send_a, *along_x)
+    other_b = lax.ppermute(send_b, *along_y)
+    layer_out = layer(1, zh, wbt, layer_out)
+    other_a, other_b, layer_out = lax.optimization_barrier((other_a, other_b, layer_out))
+    part_a = (keep_a + other_a.astype(F32)).astype(BF)
+    part_b = (keep_b + other_b.astype(F32)).astype(BF)
+    zp, part_a, part_b = lax.optimization_barrier((zp, part_a, part_b))
+    other_a = lax.ppermute(part_a, *along_x)
+    other_b = lax.ppermute(part_b, *along_y)
+    grad_features = data_grad(zp)
+    other_a, other_b, grad_features = lax.optimization_barrier((other_a, other_b, grad_features))
 
     def joined(piece, other, bit):
         first = bit == 0
@@ -765,15 +743,9 @@
             [jnp.where(first, piece, other), jnp.where(first, other, piece)], axis=0
         )
 
-    part_a, part_b = (
-        joined(part_a, lax.ppermute(part_a, *along_x), bit_x),
-        joined(part_b, lax.ppermute(part_b, *along_y), bit_y),
-    )
-    zp, part_a, part_b = lax.optimization_barrier((zp, part_a, part_b))
+    part_a, part_b = joined(part_a, other_a, bit_x), joined(part_b, other_b, bit_y)
     other_a = lax.ppermute(part_a, *along_y)
     other_b = lax.ppermute(part_b, *along_x)
-    grad_features = data_grad(zp)
-    other_a, other_b, grad_features = lax.optimization_barrier((other_a, other_b, grad_features))
     mine = jnp.stack([joined(part_a, other_a, bit_y), joined(part_b, other_b, bit_x)], axis=0)
     other = lax.ppermute(mine, *swap)
     grad_wa, grad_wb = call(

time: 97 us -> 78.8 us (0.81)
  waiting for transfers between devices: 19.2 us -> 11.8 us
  starting transfers between devices: 25.4 us -> 19.8 us
  local copies, waits for them, and re-layouts: 5.5 us -> 2.78 us
  Pallas kernels: 43.2 us -> 41.9 us
  other arithmetic: 2.21 us -> 1.02 us
    ppermute x11, waiting for transfers between devices: 15.8 us -> 2.22 us  [the longest x2 2.2 us: exchange_y(): lax.ppermute(jnp.concatenate([faces[q], edges], axis=0), 'gy', perms[q])]
    ppermute x1, waiting for transfers between devices: 0.01 us -> 4.22 us  [body(): other_a = lax.ppermute(part_a, *along_y)]
    unnamed x28 -> x20, local copies, waits for them, and re-layouts: 5.5 us -> 2.36 us
    ppermute x11, starting transfers between devices: 18 us -> 15.4 us  [the longest x2 4.52 us: exchange_y(): lax.ppermute(jnp.concatenate([faces[q], edges], axis=0), 'gy', perms[q])]
    ppermute x1, starting transfers between devices: 3.2 us -> 1.14 us  [body(): got_a = lax.ppermute(send_a, *along_y)]
    ppermute x1, waiting for transfers between devices: 0.01 us -> 1.46 us  [body(): got_b = lax.ppermute(send_b, *along_x)]
    add x4 -> x6, other arithmetic: 1.63 us -> 0.27 us  [the longest x2 0.11 us: half_sum(): return half_rows(kept, which) + half_rows(got, which).astype(F32)]
    pallas_call x8 -> x10, Pallas kernels: 43.2 us -> 41.9 us  [call(): pl.pallas_call(kernel, out_shape=[jax.ShapeDtypeStruct(s, d) for s, d in...]
  transfers between devices with their start and end apart: 16 -> 16, of which waited for: 8 -> 6; matrix products, arithmetic and copies ran while one was open for 0% -> 1% of each run, Pallas kernels for 21% -> 36%
where the time goes in v2:
time: 78.8 us; the launch traced here: 78.5 us
  Pallas kernels  41.9 us (53%)
  starting transfers between devices  19.8 us (25%)
  waiting for transfers between devices  11.8 us (15%)
  local copies, waits for them, and re-layouts  2.78 us (4%)
  between operations  1.19 us (2%)
  other arithmetic  1.02 us (1%)
    pallas_call x10, Pallas kernels, call(): pl.pallas_call(kernel, out_shape=[jax.ShapeDtypeStruct(s, d) for s, d in...  41.9 us
    ppermute x2, starting transfers between devices, exchange_y(): lax.ppermute(jnp.concatenate([faces[q], edges], axis=0), 'gy', perms[q])  4.52 us
    ppermute x1, waiting for transfers between devices, body(): other_a = lax.ppermute(part_a, *along_y)  4.22 us
    ppermute x2, starting transfers between devices, exchange_x(): lax.ppermute(one, 'gx', pairs(0))  3.18 us
    ppermute x1, waiting for transfers between devices, body(): other = lax.ppermute(mine, *swap)  2.65 us
    unnamed x20, local copies, waits for them, and re-layouts  2.36 us
    ppermute x2, waiting for transfers between devices, exchange_y(): lax.ppermute(jnp.concatenate([faces[q], edges], axis=0), 'gy', perms[q])  2.2 us
    ppermute x1, starting transfers between devices, body(): got = lax.ppermute(send, *swap)  2.08 us
  transfers between devices with their start and end apart: 16, of which 6 were waited for; matrix products, arithmetic and copies ran while one was open for 1% of the time, Pallas kernels for 36%

profile of v2, /device:TPU:0, one launch (start us, length us, event | category | flops | bytes accessed | tf_op | source)
XLA Modules:
  0.0 78.5 jit_solution(15459595679490912949)
XLA Ops:
  0.6 2.7 %shard_map.102 = (bf16[2,352,512]{2,1,0:T(8,128)(2,1)}, bf16[440,128]{1,0:T(8,128)(2,1)}, bf16[440,128]{1,0:T(8,128)(2,1)}, bf16[1,352,128]{2,1,0:T(8,128)(2,1)}) custom-call(bf16[2,96,512]{2,1,0:T(8,128)(2,1)} %feat_ref.1, bf16[2,256,512]{2,1,0:T(8,128)(2,1)} %cot_ref.1, s32[2,18]{1,0:T(2,128)} %occ_ref.9, s32[2,2,2]{2,1,0:T(2,128)} %send_ref.5), custom_call_target="tpu_custom_call" | custom-call | flops 369098752 | bytes 2097152 | tf_op jit(solution)/shard_map/pallas_call | solution.py:516
  3.3 0.5 collective-permute-start
  3.8 0.8 %collective-permute-start.1 = (bf16[440,128]{1,0:T(8,128)(2,1)}, bf16[440,128]{1,0:T(8,128)(2,1)S(1)}, u32[]{:S(2)}, u32[]{:S(2)}) collective-permute-start(bf16[440,128]{1,0:T(8,128)(2,1)} %get-tuple-element.65), channel_id=1, source_target_pairs={{2,4},{4,2},{3,5},{5,3},{10,12},{12,10},{11,13},{13,11},{18,20},{2... | collective-permute-start | bytes 337928 | tf_op jit(solution)/shard_map/ppermute | solution.py:533
  4.6 4.6 %shard_map.103 = (bf16[2,512,512]{2,1,0:T(8,128)(2,1)}, bf16[2,512,512]{2,1,0:T(8,128)(2,1)}, bf16[2,352,512]{2,1,0:T(8,128)(2,1)}) custom-call(bf16[2,352,512]{2,1,0:T(8,128)(2,1)} %get-tuple-element.67.own_ref, s32[2,27]{1,0:T(2,128)} %near_ref.1, s32[2,2,2]{2,1,0:T(2,128)} %send_ref.5), custom_call_target="tpu_custom_call" | custom-call | flops 1000000000 | bytes 4194304 | tf_op jit(solution)/shard_map/pallas_call | solution.py:516
  9.3 2.6 %collective-permute-start.2 = (bf16[440,128]{1,0:T(8,128)(2,1)S(1)}, bf16[440,128]{1,0:T(8,128)(2,1)S(1)}, u32[]{:S(2)}, u32[]{:S(2)}) collective-permute-start(bf16[440,128]{1,0:T(8,128)(2,1)S(1)} %pad_maximum_fusion.3), channel_id=1, source_target_pairs={{0,1},{1,0},{2,3},{3,2},{4,5},{5,4},{6,7},{7,6},{8,9},{9,8},{10,11... | collective-permute-start | bytes 337928 | tf_op jit(solution)/shard_map/ppermute | solution.py:551
  11.9 2.8 %shard_map.104 = (bf16[3,512,896]{2,1,0:T(8,128)(2,1)S(1)}, bf16[864,288]{1,0:T(8,128)(2,1)S(1)}, bf16[256,2592]{1,0:T(8,128)(2,1)S(1)}) custom-call(bf16[27,96,96]{2,1,0:T(8,128)(2,1)S(1)} %copy-done.1, bf16[27,96,256]{2,1,0:T(8,128)(2,1)S(1)} %copy-done), custom_call_target="tpu_custom_call" | custom-call | flops 100000000 | bytes 6291456 | tf_op jit(solution)/shard_map/pallas_call | solution.py:516
  14.8 1.2 %copy-done.6 = bf16[2,512,512]{2,1,0:T(8,128)(2,1)S(1)} copy-done((bf16[2,512,512]{2,1,0:T(8,128)(2,1)S(1)}, bf16[2,512,512]{2,1,0:T(8,128)(2,1)}, u32[]{:S(2)}) %copy-start.6) | copy-done | bytes 1048600
  16.0 1.1 %copy-done.8 = bf16[2,352,512]{2,1,0:T(8,128)(2,1)S(1)} copy-done((bf16[2,352,512]{2,1,0:T(8,128)(2,1)S(1)}, bf16[2,352,512]{2,1,0:T(8,128)(2,1)}, u32[]{:S(2)}) %copy-start.8) | copy-done | bytes 720920
  17.1 9.2 %shard_map.105 = (bf16[288,1792]{1,0:T(8,128)(2,1)S(1)}, bf16[768,1792]{1,0:T(8,128)(2,1)S(1)}, bf16[96,1280]{1,0:T(8,128)(2,1)S(1)}, bf16[96,1280]{1,0:T(8,128)...) custom-call(bf16[440,128]{1,0:T(8,128)(2,1)S(1)} %collective-permute, ...), custom_call_target="tpu_custom_call" | custom-call | flops 5000000000 | bytes 8388608 | tf_op jit(solution)/shard_map/pallas_call | solution.py:516
  26.3 2.7 %collective-permute-start.3 = (bf16[240,128]{1,0:T(8,128)(2,1)S(1)}, bf16[240,128]{1,0:T(8,128)(2,1)S(1)}, u32[]{:S(2)}, u32[]{:S(2)}) collective-permute-start(bf16[240,128]{1,0:T(8,128)(2,1)S(1)} %get-tuple-element.79), channel_id=1, source_target_pairs={{0,2},{4,6},{2,0},{6,4},{1,3},{5,7},{3,1},{7,5},{8,10},{12,14},{10... | collective-permute-start | bytes 184328 | tf_op jit(solution)/shard_map/ppermute | solution.py:533
  29.0 0.7 collective-permute-start.4
  29.6 5.1 %shard_map.106 = (f32[2,2048,128]{2,1,0:T(8,128)S(1)}, bf16[2,2048,128]{2,1,0:T(8,128)(2,1)S(1)}) custom-call(bf16[288,1792]{1,0:T(8,128)(2,1)S(1)} %get-tuple-element.81.zx_ref, bf16[768,1792]{1,0:T(8,128)(2,1)S(1)} %get-tuple-element.82.zg_ref, bf16[96,1280]{1,0:T(8,128)(2,1)S(1)} %get-tuple-element.83.gpre_ref, ...), custom_call_target="tpu_custom_call" | custom-call | flops 5000000000 | bytes 6291456 | tf_op jit(solution)/shard_map/pallas_call | solution.py:516
  34.8 2.1 %collective-permute-start.5 = (bf16[2,2048,128]{2,1,0:T(8,128)(2,1)S(1)}, bf16[2,2048,128]{2,1,0:T(8,128)(2,1)S(1)}, u32[]{:S(2)}, u32[]{:S(2)}) collective-permute-start(bf16[2,2048,128]{2,1,0:T(8,128)(2,1)S(1)} %get-tuple-element.88), channel_id=1, source_target_pairs={{0,2},{2,0},{4,6},{6,4},{1,3},{3,1},{5,7},{7,5},{8,10},{10,8},{12,... | collective-permute-start | bytes 3145736 | tf_op jit(solution)/shard_map/ppermute | solution.py:711
  36.9 0.0 copy-start.5
  36.9 0.0 copy-start.7
  36.9 1.9 %collective-permute-start.6 = (bf16[240,128]{1,0:T(8,128)(2,1)S(1)}, bf16[240,128]{1,0:T(8,128)(2,1)S(1)}, u32[]{:S(2)}, u32[]{:S(2)}) collective-permute-start(bf16[240,128]{1,0:T(8,128)(2,1)S(1)} %pad_maximum_fusion.4), channel_id=1, source_target_pairs={{0,1},{1,0},{2,3},{3,2},{4,5},{5,4},{6,7},{7,6},{8,9},{9,8},{10,11... | collective-permute-start | bytes 184328 | tf_op jit(solution)/shard_map/ppermute | solution.py:551
  38.9 0.1 fusion.3
  39.0 2.2 %collective-permute-done.6 = bf16[240,128]{1,0:T(8,128)(2,1)S(1)} collective-permute-done((bf16[240,128]{1,0:T(8,128)(2,1)S(1)}, bf16[240,128]{1,0:T(8,128)(2,1)S(1)}, u32[]{:S(2)}, u32[]{:S(2)}) %collective-permute-start.6) | collective-permute-done | bytes 61472 | tf_op jit(solution)/shard_map/ppermute | solution.py:551
  41.2 2.0 %shard_map.107 = (bf16[288,1792]{1,0:T(8,128)(2,1)S(1)}, bf16[288,1792]{1,0:T(8,128)(2,1)S(1)}) custom-call(bf16[240,128]{1,0:T(8,128)(2,1)S(1)} %collective-permute-done.3.f1_ref, bf16[240,128]{1,0:T(8,128)(2,1)S(1)} %collective-permute-done.4.f2_ref, bf16[1,240,128]{2,1,0:T(8,128)(2,1)S(1)} %bitcast.18, bf16[2,512,512]{2,1,0:T(8,128)(2,1)S(1)} %copy-done.7, ...), custom_call_target="tpu_custom_call" | custom-call | flops 2000000000 | bytes 6291456 | tf_op jit(solution)/shard_map/pallas_call | solution.py:516
  43.2 0.1 fusion.5
  43.3 0.1 fusion
  43.4 0.1 fusion.2
  43.5 0.1 fusion.4
  43.6 1.1 %collective-permute-start.7 = (bf16[1024,128]{1,0:T(8,128)(2,1)S(1)}, bf16[1024,128]{1,0:T(8,128)(2,1)S(1)}, u32[]{:S(2)}, u32[]{:S(2)}) collective-permute-start(bf16[1024,128]{1,0:T(8,128)(2,1)S(1)} %get-tuple-element.99), channel_id=1, source_target_pairs={{0,4},{2,6},{4,0},{6,2},{1,5},{3,7},{5,1},{7,3},{8,12},{10,14},{12... | collective-permute-start | bytes 786440 | tf_op jit(solution)/shard_map/ppermute | solution.py:717
  44.7 1.0 %collective-permute-start.8 = (bf16[1024,128]{1,0:T(8,128)(2,1)S(1)}, bf16[1024,128]{1,0:T(8,128)(2,1)S(1)}, u32[]{:S(2)}, u32[]{:S(2)}) collective-permute-start(bf16[1024,128]{1,0:T(8,128)(2,1)S(1)} %get-tuple-element.100), channel_id=1, source_target_pairs={{0,1},{1,0},{2,3},{3,2},{4,5},{5,4},{6,7},{7,6},{8,9},{9,8},{10,11... | collective-permute-start | bytes 786440 | tf_op jit(solution)/shard_map/ppermute | solution.py:718
  45.8 4.4 %shard_map.108.rest_0_ = bf16[2,256,512]{2,1,0:T(8,128)(2,1)} custom-call(s32[2,18]{1,0:T(2,128)S(1)} %copy-done.3, bf16[288,1792]{1,0:T(8,128)(2,1)S(1)} %get-tuple-element.110.zh_hbm, bf16[256,2592]{1,0:T(8,128)(2,1)S(1)} %get-tuple-element.101.wbt_hbm), custom_call_target="tpu_custom_call" | custom-call | flops 1000000000 | bytes 2097152 | tf_op jit(solution)/shard_map/pallas_call | solution.py:516
  50.2 0.1 add_bitcast_fusion
  50.3 0.1 add_bitcast_fusion.1
  50.3 0.6 collective-permute-done.7
  50.9 1.5 %collective-permute-done.8 = bf16[1024,128]{1,0:T(8,128)(2,1)S(1)} collective-permute-done((bf16[1024,128]{1,0:T(8,128)(2,1)S(1)}, bf16[1024,128]{1,0:T(8,128)(2,1)S(1)}, u32[]{:S(2)}, u32[]{:S(2)}) %collective-permute-start.8) | collective-permute-done | bytes 262176 | tf_op jit(solution)/shard_map/ppermute | solution.py:718
  52.4 0.1 convert_add_fusion
  52.5 0.1 convert_add_fusion.1
  52.6 0.4 collective-permute-start.10
  53.0 1.7 %collective-permute-start.9 = (bf16[512,128]{1,0:T(8,128)(2,1)S(1)}, bf16[512,128]{1,0:T(8,128)(2,1)S(1)}, u32[]{:S(2)}, u32[]{:S(2)}) collective-permute-start(bf16[512,128]{1,0:T(8,128)(2,1)S(1)} %select_convert_fusion.1), channel_id=1, source_target_pairs={{0,1},{1,0},{2,3},{3,2},{4,5},{5,4},{6,7},{7,6},{8,9},{9,8},{10,11... | collective-permute-start | bytes 393224 | tf_op jit(solution)/shard_map/ppermute | solution.py:728
  54.7 4.2 %shard_map.109 = bf16[2,256,512]{2,1,0:T(8,128)(2,1)} custom-call(s32[2,18]{1,0:T(2,128)S(1)} %copy-done.3, bf16[288,1792]{1,0:T(8,128)(2,1)S(1)} %get-tuple-element.110.zh_hbm, bf16[256,2592]{1,0:T(8,128)(2,1)S(1)} %get-tuple-element.101.wbt_hbm, bf16[2,256,512]{2,1,0:T(8,128)(2,1)} %shard_map.108.rest_0_), custom_call_target="tpu_custom_call", output_to_operand_aliasing={{}: (3, {})} | custom-call | flops 1000000000 | bytes 2097152 | tf_op jit(solution)/shard_map/pallas_call | solution.py:516
  59.0 0.8 %collective-permute-start.11 = (bf16[512,128]{1,0:T(8,128)(2,1)S(1)}, bf16[512,128]{1,0:T(8,128)(2,1)S(1)}, u32[]{:S(2)}, u32[]{:S(2)}) collective-permute-start(bf16[512,128]{1,0:T(8,128)(2,1)S(1)} %add_convert_fusion.3), channel_id=1, source_target_pairs={{0,1},{1,0},{2,3},{3,2},{4,5},{5,4},{6,7},{7,6},{8,9},{9,8},{10,11... | collective-permute-start | bytes 393224 | tf_op jit(solution)/shard_map/ppermute | solution.py:735
  59.8 1.3 %collective-permute-start.12 = (bf16[512,128]{1,0:T(8,128)(2,1)S(1)}, bf16[512,128]{1,0:T(8,128)(2,1)S(1)}, u32[]{:S(2)}, u32[]{:S(2)}) collective-permute-start(bf16[512,128]{1,0:T(8,128)(2,1)S(1)} %add_convert_fusion.2), channel_id=1, source_target_pairs={{0,4},{2,6},{4,0},{6,2},{1,5},{3,7},{5,1},{7,3},{8,12},{10,14},{12... | collective-permute-start | bytes 393224 | tf_op jit(solution)/shard_map/ppermute | solution.py:736
  61.1 4.7 %shard_map.110 = bf16[2,96,512]{2,1,0:T(8,128)(2,1)} custom-call(s32[2,18]{1,0:T(2,128)S(1)} %copy-done.3, bf16[288,1792]{1,0:T(8,128)(2,1)S(1)} %get-tuple-element.118.zp_hbm, bf16[27,96,96]{2,1,0:T(8,128)(2,1)S(1)} %copy-done.1), custom_call_target="tpu_custom_call" | custom-call | flops 2000000000 | bytes 2097152 | tf_op jit(solution)/shard_map/pallas_call | solution.py:516
  65.9 0.8 %collective-permute-start.13 = (bf16[1024,128]{1,0:T(8,128)(2,1)S(1)}, bf16[1024,128]{1,0:T(8,128)(2,1)S(1)}, u32[]{:S(2)}, u32[]{:S(2)}) collective-permute-start(bf16[1024,128]{1,0:T(8,128)(2,1)S(1)} %pad_maximum_fusion.1), channel_id=1, source_target_pairs={{0,4},{2,6},{4,0},{6,2},{1,5},{3,7},{5,1},{7,3},{8,12},{10,14},{12... | collective-permute-start | bytes 786440 | tf_op jit(solution)/shard_map/ppermute | solution.py:747
  66.8 1.4 %collective-permute-start.14 = (bf16[1024,128]{1,0:T(8,128)(2,1)S(1)}, bf16[1024,128]{1,0:T(8,128)(2,1)S(1)}, u32[]{:S(2)}, u32[]{:S(2)}) collective-permute-start(bf16[1024,128]{1,0:T(8,128)(2,1)S(1)} %pad_maximum_fusion.2), channel_id=1, source_target_pairs={{0,1},{1,0},{2,3},{3,2},{4,5},{5,4},{6,7},{7,6},{8,9},{9,8},{10,11... | collective-permute-start | bytes 786440 | tf_op jit(solution)/shard_map/ppermute | solution.py:748
  68.1 4.2 %collective-permute-done.13 = bf16[1024,128]{1,0:T(8,128)(2,1)S(1)} collective-permute-done((bf16[1024,128]{1,0:T(8,128)(2,1)S(1)}, bf16[1024,128]{1,0:T(8,128)(2,1)S(1)}, u32[]{:S(2)}, u32[]{:S(2)}) %collective-permute-start.13) | collective-permute-done | bytes 262176 | tf_op jit(solution)/shard_map/ppermute | solution.py:747
  72.3 0.1 broadcast_select_fusion.3
  72.5 0.7 collective-permute-done.14
  73.2 0.1 broadcast_select_fusion.1
  73.3 0.1 pad_maximum_fusion.mine_ref
  73.5 0.1 collective-permute-start.15
  73.5 2.6 %collective-permute-done.15.other_ref = bf16[2,2048,128]{2,1,0:T(8,128)(2,1)S(1)} collective-permute-done((bf16[2,2048,128]{2,1,0:T(8,128)(2,1)S(1)}, bf16[2,2048,128]{2,1,0:T(8,128)(2,1)S(1)}, u32[]{:S(2)}, u32[]{:S(2)}) %collective-permute-start.15) | collective-permute-done | bytes 1048608 | tf_op jit(solution)/shard_map/ppermute | solution.py:750
  76.2 2.2 %shard_map.111 = (f32[27,96,96]{2,1,0:T(8,128)}, f32[27,96,256]{2,1,0:T(8,128)}) custom-call(bf16[2,2048,128]{2,1,0:T(8,128)(2,1)S(1)} %pad_maximum_fusion.mine_ref, bf16[2,2048,128]{2,1,0:T(8,128)(2,1)S(1)} %collective-permute-done.15.other_ref), custom_call_target="tpu_custom_call" | custom-call | bytes 6291456 | tf_op jit(solution)/shard_map/pallas_call | solution.py:516
  (40 shorter events, 0.4 us)
Async XLA Ops:
  3.3 6.0 %copy-start.9 = (bf16[1,352,128]{2,1,0:T(8,128)(2,1)S(1)}, bf16[1,352,128]{2,1,0:T(8,128)(2,1)}, u32[]{:S(2)}) copy-start(bf16[1,352,128]{2,1,0:T(8,128)(2,1)} %get-tuple-element.69) | copy-start | bytes 270340
  3.3 8.6 %copy-start = (bf16[27,96,256]{2,1,0:T(8,128)(2,1)S(1)}, bf16[27,96,256]{2,1,0:T(8,128)(2,1)}, u32[]{:S(2)}) copy-start(bf16[27,96,256]{2,1,0:T(8,128)(2,1)} %wb_ref.1) | copy-start | bytes 3981316
  3.3 8.6 %copy-start.1 = (bf16[27,96,96]{2,1,0:T(8,128)(2,1)S(1)}, bf16[27,96,96]{2,1,0:T(8,128)(2,1)}, u32[]{:S(2)}) copy-start(bf16[27,96,96]{2,1,0:T(8,128)(2,1)} %wa_hbm) | copy-start | bytes 1492996
  3.3 5.9 %collective-permute-start = (bf16[440,128]{1,0:T(8,128)(2,1)}, bf16[440,128]{1,0:T(8,128)(2,1)S(1)}, u32[]{:S(2)}, u32[]{:S(2)}) collective-permute-start(bf16[440,128]{1,0:T(8,128)(2,1)} %get-tuple-element.64), channel_id=1, source_target_pairs={{0,2},{4,6},{2,0},{6,4},{1,3},{5,7},{3,1},{7,5},{8,10},{12,14},{10... | collective-permute-start | bytes 337928 | tf_op jit(solution)/shard_map/ppermute | solution.py:533
  3.8 5.4 %collective-permute-start.1 = (bf16[440,128]{1,0:T(8,128)(2,1)}, bf16[440,128]{1,0:T(8,128)(2,1)S(1)}, u32[]{:S(2)}, u32[]{:S(2)}) collective-permute-start(bf16[440,128]{1,0:T(8,128)(2,1)} %get-tuple-element.65), channel_id=1, source_target_pairs={{2,4},{4,2},{3,5},{5,3},{10,12},{12,10},{11,13},{13,11},{18,20},{2... | collective-permute-start | bytes 337928 | tf_op jit(solution)/shard_map/ppermute | solution.py:533
  9.2 5.5 %copy-start.2 = (s32[2,2,2]{2,1,0:T(2,128)S(1)}, s32[2,2,2]{2,1,0:T(2,128)}, u32[]{:S(2)}) copy-start(s32[2,2,2]{2,1,0:T(2,128)} %send_ref.5) | copy-start | bytes 100
  9.2 5.5 %copy-start.3 = (s32[2,18]{1,0:T(2,128)S(1)}, s32[2,18]{1,0:T(2,128)}, u32[]{:S(2)}) copy-start(s32[2,18]{1,0:T(2,128)} %occ_ref.9) | copy-start | bytes 436
  9.2 5.5 %copy-start.4 = (bf16[2,352,512]{2,1,0:T(8,128)(2,1)S(1)}, bf16[2,352,512]{2,1,0:T(8,128)(2,1)}, u32[]{:S(2)}) copy-start(bf16[2,352,512]{2,1,0:T(8,128)(2,1)} %get-tuple-element.67.own_ref) | copy-start | bytes 2162692
  9.3 5.4 %collective-permute-start.2 = (bf16[440,128]{1,0:T(8,128)(2,1)S(1)}, bf16[440,128]{1,0:T(8,128)(2,1)S(1)}, u32[]{:S(2)}, u32[]{:S(2)}) collective-permute-start(bf16[440,128]{1,0:T(8,128)(2,1)S(1)} %pad_maximum_fusion.3), channel_id=1, source_target_pairs={{0,1},{1,0},{2,3},{3,2},{4,5},{5,4},{6,7},{7,6},{8,9},{9,8},{10,11... | collective-permute-start | bytes 337928 | tf_op jit(solution)/shard_map/ppermute | solution.py:551
  14.8 1.2 %copy-start.6 = (bf16[2,512,512]{2,1,0:T(8,128)(2,1)S(1)}, bf16[2,512,512]{2,1,0:T(8,128)(2,1)}, u32[]{:S(2)}) copy-start(bf16[2,512,512]{2,1,0:T(8,128)(2,1)} %get-tuple-element.75.sr_ref) | copy-start | bytes 3145732
  16.0 1.1 %copy-start.8 = (bf16[2,352,512]{2,1,0:T(8,128)(2,1)S(1)}, bf16[2,352,512]{2,1,0:T(8,128)(2,1)}, u32[]{:S(2)}) copy-start(bf16[2,352,512]{2,1,0:T(8,128)(2,1)} %get-tuple-element.76.part_ref) | copy-start | bytes 2162692
  26.3 8.5 %collective-permute-start.3 = (bf16[240,128]{1,0:T(8,128)(2,1)S(1)}, bf16[240,128]{1,0:T(8,128)(2,1)S(1)}, u32[]{:S(2)}, u32[]{:S(2)}) collective-permute-start(bf16[240,128]{1,0:T(8,128)(2,1)S(1)} %get-tuple-element.79), channel_id=1, source_target_pairs={{0,2},{4,6},{2,0},{6,4},{1,3},{5,7},{3,1},{7,5},{8,10},{12,14},{10... | collective-permute-start | bytes 184328 | tf_op jit(solution)/shard_map/ppermute | solution.py:533
  29.0 5.8 %collective-permute-start.4 = (bf16[240,128]{1,0:T(8,128)(2,1)S(1)}, bf16[240,128]{1,0:T(8,128)(2,1)S(1)}, u32[]{:S(2)}, u32[]{:S(2)}) collective-permute-start(bf16[240,128]{1,0:T(8,128)(2,1)S(1)} %get-tuple-element.80), channel_id=1, source_target_pairs={{2,4},{4,2},{3,5},{5,3},{10,12},{12,10},{11,13},{13,11},{18,20},{2... | collective-permute-start | bytes 184328 | tf_op jit(solution)/shard_map/ppermute | solution.py:533
  34.8 8.4 %collective-permute-start.5 = (bf16[2,2048,128]{2,1,0:T(8,128)(2,1)S(1)}, bf16[2,2048,128]{2,1,0:T(8,128)(2,1)S(1)}, u32[]{:S(2)}, u32[]{:S(2)}) collective-permute-start(bf16[2,2048,128]{2,1,0:T(8,128)(2,1)S(1)} %get-tuple-element.88), channel_id=1, source_target_pairs={{0,2},{2,0},{4,6},{6,4},{1,3},{3,1},{5,7},{7,5},{8,10},{10,8},{12,... | collective-permute-start | bytes 3145736 | tf_op jit(solution)/shard_map/ppermute | solution.py:711
  36.9 4.3 %copy-start.5 = (bf16[2,512,512]{2,1,0:T(8,128)(2,1)S(1)}, bf16[2,512,512]{2,1,0:T(8,128)(2,1)}, u32[]{:S(2)}) copy-start(bf16[2,512,512]{2,1,0:T(8,128)(2,1)} %get-tuple-element.92.so_ref) | copy-start | bytes 3145732
  36.9 4.3 %copy-start.7 = (bf16[2,512,512]{2,1,0:T(8,128)(2,1)S(1)}, bf16[2,512,512]{2,1,0:T(8,128)(2,1)}, u32[]{:S(2)}) copy-start(bf16[2,512,512]{2,1,0:T(8,128)(2,1)} %get-tuple-element.75.sr_ref) | copy-start | bytes 3145732
  36.9 4.3 %collective-permute-start.6 = (bf16[240,128]{1,0:T(8,128)(2,1)S(1)}, bf16[240,128]{1,0:T(8,128)(2,1)S(1)}, u32[]{:S(2)}, u32[]{:S(2)}) collective-permute-start(bf16[240,128]{1,0:T(8,128)(2,1)S(1)} %pad_maximum_fusion.4), channel_id=1, source_target_pairs={{0,1},{1,0},{2,3},{3,2},{4,5},{5,4},{6,7},{7,6},{8,9},{9,8},{10,11... | collective-permute-start | bytes 184328 | tf_op jit(solution)/shard_map/ppermute | solution.py:551
  43.6 7.3 %collective-permute-start.7 = (bf16[1024,128]{1,0:T(8,128)(2,1)S(1)}, bf16[1024,128]{1,0:T(8,128)(2,1)S(1)}, u32[]{:S(2)}, u32[]{:S(2)}) collective-permute-start(bf16[1024,128]{1,0:T(8,128)(2,1)S(1)} %get-tuple-element.99), channel_id=1, source_target_pairs={{0,4},{2,6},{4,0},{6,2},{1,5},{3,7},{5,1},{7,3},{8,12},{10,14},{12... | collective-permute-start | bytes 786440 | tf_op jit(solution)/shard_map/ppermute | solution.py:717
  44.7 7.6 %collective-permute-start.8 = (bf16[1024,128]{1,0:T(8,128)(2,1)S(1)}, bf16[1024,128]{1,0:T(8,128)(2,1)S(1)}, u32[]{:S(2)}, u32[]{:S(2)}) collective-permute-start(bf16[1024,128]{1,0:T(8,128)(2,1)S(1)} %get-tuple-element.100), channel_id=1, source_target_pairs={{0,1},{1,0},{2,3},{3,2},{4,5},{5,4},{6,7},{7,6},{8,9},{9,8},{10,11... | collective-permute-start | bytes 786440 | tf_op jit(solution)/shard_map/ppermute | solution.py:718
  52.6 6.3 %collective-permute-start.10 = (bf16[512,128]{1,0:T(8,128)(2,1)S(1)}, bf16[512,128]{1,0:T(8,128)(2,1)S(1)}, u32[]{:S(2)}, u32[]{:S(2)}) collective-permute-start(bf16[512,128]{1,0:T(8,128)(2,1)S(1)} %select_convert_fusion), channel_id=1, source_target_pairs={{0,4},{2,6},{4,0},{6,2},{1,5},{3,7},{5,1},{7,3},{8,12},{10,14},{12... | collective-permute-start | bytes 393224 | tf_op jit(solution)/shard_map/ppermute | solution.py:729
  53.0 5.9 %collective-permute-start.9 = (bf16[512,128]{1,0:T(8,128)(2,1)S(1)}, bf16[512,128]{1,0:T(8,128)(2,1)S(1)}, u32[]{:S(2)}, u32[]{:S(2)}) collective-permute-start(bf16[512,128]{1,0:T(8,128)(2,1)S(1)} %select_convert_fusion.1), channel_id=1, source_target_pairs={{0,1},{1,0},{2,3},{3,2},{4,5},{5,4},{6,7},{7,6},{8,9},{9,8},{10,11... | collective-permute-start | bytes 393224 | tf_op jit(solution)/shard_map/ppermute | solution.py:728
  59.0 6.8 %collective-permute-start.11 = (bf16[512,128]{1,0:T(8,128)(2,1)S(1)}, bf16[512,128]{1,0:T(8,128)(2,1)S(1)}, u32[]{:S(2)}, u32[]{:S(2)}) collective-permute-start(bf16[512,128]{1,0:T(8,128)(2,1)S(1)} %add_convert_fusion.3), channel_id=1, source_target_pairs={{0,1},{1,0},{2,3},{3,2},{4,5},{5,4},{6,7},{7,6},{8,9},{9,8},{10,11... | collective-permute-start | bytes 393224 | tf_op jit(solution)/shard_map/ppermute | solution.py:735
  59.8 6.0 %collective-permute-start.12 = (bf16[512,128]{1,0:T(8,128)(2,1)S(1)}, bf16[512,128]{1,0:T(8,128)(2,1)S(1)}, u32[]{:S(2)}, u32[]{:S(2)}) collective-permute-start(bf16[512,128]{1,0:T(8,128)(2,1)S(1)} %add_convert_fusion.2), channel_id=1, source_target_pairs={{0,4},{2,6},{4,0},{6,2},{1,5},{3,7},{5,1},{7,3},{8,12},{10,14},{12... | collective-permute-start | bytes 393224 | tf_op jit(solution)/shard_map/ppermute | solution.py:736
  65.9 6.4 %collective-permute-start.13 = (bf16[1024,128]{1,0:T(8,128)(2,1)S(1)}, bf16[1024,128]{1,0:T(8,128)(2,1)S(1)}, u32[]{:S(2)}, u32[]{:S(2)}) collective-permute-start(bf16[1024,128]{1,0:T(8,128)(2,1)S(1)} %pad_maximum_fusion.1), channel_id=1, source_target_pairs={{0,4},{2,6},{4,0},{6,2},{1,5},{3,7},{5,1},{7,3},{8,12},{10,14},{12... | collective-permute-start | bytes 786440 | tf_op jit(solution)/shard_map/ppermute | solution.py:747
  66.8 6.4 %collective-permute-start.14 = (bf16[1024,128]{1,0:T(8,128)(2,1)S(1)}, bf16[1024,128]{1,0:T(8,128)(2,1)S(1)}, u32[]{:S(2)}, u32[]{:S(2)}) collective-permute-start(bf16[1024,128]{1,0:T(8,128)(2,1)S(1)} %pad_maximum_fusion.2), channel_id=1, source_target_pairs={{0,1},{1,0},{2,3},{3,2},{4,5},{5,4},{6,7},{7,6},{8,9},{9,8},{10,11... | collective-permute-start | bytes 786440 | tf_op jit(solution)/shard_map/ppermute | solution.py:748
  73.5 2.7 %collective-permute-start.15 = (bf16[2,2048,128]{2,1,0:T(8,128)(2,1)S(1)}, bf16[2,2048,128]{2,1,0:T(8,128)(2,1)S(1)}, u32[]{:S(2)}, u32[]{:S(2)}) collective-permute-start(bf16[2,2048,128]{2,1,0:T(8,128)(2,1)S(1)} %pad_maximum_fusion.mine_ref), channel_id=1, source_target_pairs={{0,2},{2,0},{4,6},{6,4},{1,3},{3,1},{5,7},{7,5},{8,10},{10,8},{12,... | collective-permute-start | bytes 3145736 | tf_op jit(solution)/shard_map/ppermute | solution.py:750

commit v3 on v2

--- a/solution.py
+++ b/solution.py
@@ -17,8 +17,9 @@
 FACE = 128
 FAR = 100
 HALO = 512
-HALF = 4096
-STORED = 2688
+HALF = 3712
+STORED = 2592
+USED = 3600
 NT = (((1,), (1,)), ((), ()))
 BF = jnp.bfloat16
 F32 = jnp.float32
@@ -330,13 +331,6 @@
     return one_hot(jnp.where(rest < 64, x * 64 + rest, -1) == iota((OUTER, VOX), 1))
 
 
-def fetch(pairs, sems):
-    copies = [pltpu.make_async_copy(p[0], p[1], sems.at[k]) for k, p in enumerate(pairs)]
-    for copy in copies:
-        copy.start()
-    return copies
-
-
 def pack_kernel(dirs, feat_ref, cot_ref, occ_ref, send_ref, own_ref, one_ref, two_ref, y_ref):
     for n in range(2):
         mask = lane_mask(occ_ref, n, VOX, 64)
@@ -393,6 +387,14 @@
     pack_sends(hid_ref, send_ref, dirs, one_ref, two_ref, y_ref)
 
 
+def tile_rows(tile):
+    if tile < 3:
+        return [(0, STORED + 288 * tile, 0, 288)]
+    if tile > 3:
+        return [(1, STORED + 288 * (tile - 4), 0, 288)]
+    return [(0, STORED + 864, 0, 144), (1, STORED + 864, 144, 144)]
+
+
 def weights_kernel(scale, split, zx_ref, zg_ref, gpre_ref, wide_ref, keep_ref, *rest):
     g9_ref, h9_ref, sum_ref = rest[-3:]
     h9_ref[...] = jnp.zeros_like(h9_ref)
@@ -403,12 +405,9 @@
             at = PADDED * n + PLANE * (2 - ab // 3) + 8 * (2 - ab % 3)
             h9_ref[96 * ab : 96 * ab + 96, at : at + OUTER] = wide_ref[:, own]
             at = PADDED * n + PLANE * (ab // 3) + 8 * (ab % 3)
-            g9_ref[128 * ab : 128 * ab + 96, at : at + OUTER] = gpre_ref[:, own]
+            g9_ref[96 * ab : 96 * ab + 96, at : at + OUTER] = gpre_ref[:, own]
     total = scale * lax.dot_general(h9_ref[...], zg_ref[...], NT, preferred_element_type=F32)
-    rows = TAPS * 96
-    sum_ref[:, rows:STORED, :] = jnp.zeros((2, STORED - rows, 128), F32)
-    sum_ref[:, STORED + 14 * 96 :, :] = jnp.zeros((2, HALF - STORED - 14 * 96, 128), F32)
-    sum_ref[1, STORED + 13 * 96 : STORED + 14 * 96, :] = jnp.zeros((96, 128), F32)
+    sum_ref[:, USED:, :] = jnp.zeros((2, HALF - USED, 128), F32)
     for k in range(TAPS):
         c, ab = k % 3, k // 3
         for half in range(2):
@@ -416,10 +415,9 @@
                 96 * ab : 96 * ab + 96, 256 * c + 128 * half : 256 * c + 128 * half + 128
             ]
     total = scale * lax.dot_general(zx_ref[...], g9_ref[...], NT, preferred_element_type=F32)
-    for k in range(TAPS):
-        half, at = k // 14, STORED + 96 * (k % 14)
-        c, ab = k % 3, k // 3
-        sum_ref[half, at : at + 96, :] = total[96 * c : 96 * c + 96, 128 * ab : 128 * ab + 128]
+    for tile in range(7):
+        for half, at, start, rows in tile_rows(tile):
+            sum_ref[half, at : at + rows, :] = total[start : start + rows, 128 * tile : 128 * tile + 128]
     if split:
         core = lax.axis_index("gx") & 1
         keep = pl.multiple_of(core * (HALF // 2), HALF // 2)
@@ -441,34 +439,26 @@
     )
 
 
-def out_kernel(n, occ_ref, zh_hbm, wbt_hbm, *rest):
-    out_hbm, p_ref, zh_ref, wbt_ref, out_ref, sems = rest[-6:]
-    lanes = pl.ds(PADDED * n, PADDED)
-    copies = fetch(((zh_hbm.at[:, lanes], zh_ref), (wbt_hbm, wbt_ref)), sems)
-    squeeze = compaction()
-    copies[0].wait()
+def out_kernel(n, occ_ref, zh_ref, wbt_ref, *rest):
+    out_hbm, p_ref, out_ref, sem = rest[-4:]
     for k in range(TAPS):
         a, b, c = k // 9, k // 3 % 3, k % 3
-        at = PLANE * a + 8 * b
+        at = PADDED * n + PLANE * a + 8 * b
         p_ref[96 * k : 96 * k + 96, :] = zh_ref[96 * c : 96 * c + 96, at : at + OUTER]
-    copies[1].wait()
     total = jnp.dot(wbt_ref[...], p_ref[...], preferred_element_type=F32)
     total = (total * lane_mask(occ_ref, n, OUTER, PLANE)).astype(BF)
-    out_ref[...] = jnp.dot(total, squeeze, preferred_element_type=F32).astype(BF)
-    store = pltpu.make_async_copy(out_ref, out_hbm.at[n], sems.at[2])
+    out_ref[...] = jnp.dot(total, compaction(), preferred_element_type=F32).astype(BF)
+    store = pltpu.make_async_copy(out_ref, out_hbm.at[n], sem.at[0])
     store.start()
     store.wait()
 
 
-def grad_kernel(occ_ref, zp_hbm, wa_hbm, grad_ref, s9_ref, wg9_ref, zp_ref, wa_ref, sems):
-    copies = fetch(((wa_hbm, wa_ref), (zp_hbm, zp_ref)), sems)
-    squeeze = compaction()
-    copies[0].wait()
+def grad_kernel(occ_ref, zp_ref, wa_ref, grad_ref, s9_ref, wg9_ref):
     for k in range(TAPS):
         c, ab = k % 3, k // 3
         wg9_ref[96 * ab : 96 * ab + 96, 96 * c : 96 * c + 96] = wa_ref[k]
-    copies[1].wait()
     s9_ref[...] = jnp.dot(wg9_ref[...], zp_ref[...], preferred_element_type=F32)
+    squeeze = compaction()
     for n in range(2):
         mask = lane_mask(occ_ref, n, OUTER, PLANE)
         grad_ref[n] = jnp.dot(
@@ -495,9 +485,14 @@
             ].astype(F32)
         if k % 9 == 8:
             store(wb_ref.at[pl.ds(k - 8, 9)], wb_hbm.at[pl.ds(k - 8, 9)])
+    tiles = []
+    for tile in range(7):
+        parts = [all_ref[half, at : at + rows, :].astype(F32) for half, at, _, rows in tile_rows(tile)]
+        tiles.append(parts[0] if len(parts) == 1 else jnp.concatenate(parts, axis=0))
+    total = jnp.concatenate(tiles, axis=1)
     for k in range(TAPS):
-        half, at = k // 14, STORED + 96 * (k % 14)
-        wa_ref[k] = all_ref[half, at : at + 96, :96].astype(F32)
+        c, ab = k % 3, k // 3
+        wa_ref[k] = total[96 * c : 96 * c + 96, 96 * ab : 96 * ab + 96]
     store(wa_ref, wa_hbm)
     for copy in copies:
         copy.wait()
@@ -644,7 +639,7 @@
         functools.partial(weights_kernel, scale, split),
         sums,
         [zx, zg, gpre, hidden],
-        [((9 * 128, wide), BF), ((9 * 96, wide), BF), ((2, HALF, 128), F32)],
+        [((7 * 128, wide), BF), ((9 * 96, wide), BF), ((2, HALF, 128), F32)],
         flops=5 * 10**9,
         moved=6 * MIB,
         limit=24 * MIB,
@@ -669,13 +664,13 @@
             functools.partial(out_kernel, n),
             [((2, 256, VOX), BF)],
             [occupancy, zh, wbt, *earlier],
-            [((TAPS * 96, OUTER), BF), ((288, PADDED), BF), ((256, TAPS * 96), BF), ((256, VOX), BF)],
+            [((TAPS * 96, OUTER), BF), ((256, VOX), BF)],
             flops=10**9,
             moved=2 * MIB,
-            far_ins=2 + len(earlier),
+            far_ins=len(earlier),
             far_outs=1,
-            sems=3,
-            limit=14 * MIB,
+            sems=1,
+            limit=12 * MIB,
             aliases={3: 0} if earlier else {},
         )[0]
 
@@ -684,21 +679,22 @@
             grad_kernel,
             [((2, 96, VOX), BF)],
             [occupancy, zp, weight_a],
-            [((864, wide), F32), ((864, 288), BF), ((288, wide), BF), ((TAPS, 96, 96), BF)],
+            [((864, wide), F32), ((864, 288), BF)],
             flops=2 * 10**9,
             moved=2 * MIB,
-            far_ins=2,
-            sems=2,
-            limit=20 * MIB,
+            limit=14 * MIB,
         )[0]
 
     if not split:
         zh, zp = second(from_one, from_two, from_y)
         total = lax.psum(sums[0], ("gx", "gy"))
         grad_wb = jnp.concatenate([total[0, : TAPS * 96], total[1, : TAPS * 96]], axis=1)
-        first = total[0, STORED : STORED + 14 * 96, :96]
-        second = total[1, STORED : STORED + 13 * 96, :96]
-        grad_wa = jnp.concatenate([first, second], axis=0)
+        tiles = []
+        for tile in range(7):
+            parts = [total[half, at : at + rows] for half, at, _, rows in tile_rows(tile)]
+            tiles.append(jnp.concatenate(parts, axis=0))
+        grad_wa = jnp.concatenate(tiles, axis=1)[:, :864].reshape(3, 96, 9, 96)
+        grad_wa = grad_wa.transpose(2, 0, 1, 3)
         layer_out = layer(1, zh, wbt, layer(0, zh, wbt))
         return layer_out, data_grad(zp), grad_wa.reshape(TAPS, 96, 96), grad_wb.reshape(TAPS, 96, 256)
 

time: 78.8 us -> 76.2 us (0.967)
  Pallas kernels: 41.9 us -> 39.5 us
  local copies, waits for them, and re-layouts: 2.78 us -> 1.52 us
    pallas_call x10, Pallas kernels: 41.9 us -> 39.5 us  [call(): pl.pallas_call(kernel, out_shape=[jax.ShapeDtypeStruct(s, d) for s, d in...]
    unnamed x20 -> x18, local copies, waits for them, and re-layouts: 2.36 us -> 1.14 us
  transfers between devices with their start and end apart: 16 -> 16, of which waited for: 6 -> 7; matrix products, arithmetic and copies ran while one was open for 1% -> 1% of each run, Pallas kernels for 36% -> 33%
where the time goes in v3:
time: 76.2 us; the launch traced here: 76 us
  Pallas kernels  39.5 us (52%)
  starting transfers between devices  20.4 us (27%)
  waiting for transfers between devices  12.5 us (16%)
  local copies, waits for them, and re-layouts  1.52 us (2%)
  between operations  1.16 us (2%)
  other arithmetic  0.9 us (1%)
    pallas_call x10, Pallas kernels, call(): pl.pallas_call(kernel, out_shape=[jax.ShapeDtypeStruct(s, d) for s, d in...  39.5 us
    ppermute x2, starting transfers between devices, exchange_y(): lax.ppermute(jnp.concatenate([faces[q], edges], axis=0), 'gy', perms[q])  4.65 us
    ppermute x1, waiting for transfers between devices, body(): other_a = lax.ppermute(part_a, *along_y)  3.63 us
    ppermute x2, starting transfers between devices, exchange_x(): lax.ppermute(one, 'gx', pairs(0))  3.12 us
    ppermute x1, waiting for transfers between devices, body(): other = lax.ppermute(mine, *swap)  2.51 us
    ppermute x2, waiting for transfers between devices, exchange_y(): lax.ppermute(jnp.concatenate([faces[q], edges], axis=0), 'gy', perms[q])  2.21 us
    ppermute x1, starting transfers between devices, body(): got = lax.ppermute(send, *swap)  2.09 us
    ppermute x1, starting transfers between devices, body(): other_a = lax.ppermute(send_a, *along_x)  1.66 us
  transfers between devices with their start and end apart: 16, of which 7 were waited for; matrix products, arithmetic and copies ran while one was open for 1% of the time, Pallas kernels for 33%

profile of v3, /device:TPU:0, one launch (start us, length us, event | category | flops | bytes accessed | tf_op | source)
XLA Modules:
  0.0 76.0 jit_solution(11477363248492789891)
XLA Ops:
  0.6 2.6 %shard_map.102 = (bf16[2,352,512]{2,1,0:T(8,128)(2,1)}, bf16[440,128]{1,0:T(8,128)(2,1)}, bf16[440,128]{1,0:T(8,128)(2,1)}, bf16[1,352,128]{2,1,0:T(8,128)(2,1)}) custom-call(bf16[2,96,512]{2,1,0:T(8,128)(2,1)} %feat_ref.1, bf16[2,256,512]{2,1,0:T(8,128)(2,1)} %cot_ref.1, s32[2,18]{1,0:T(2,128)} %occ_ref.9, s32[2,2,2]{2,1,0:T(2,128)} %send_ref.5), custom_call_target="tpu_custom_call" | custom-call | flops 369098752 | bytes 2097152 | tf_op jit(solution)/shard_map/pallas_call | solution.py:511
  3.3 0.5 collective-permute-start
  3.7 0.7 collective-permute-start.1
  4.4 0.0 copy-start
  4.4 0.0 copy-start.1
  4.4 4.8 %shard_map.103 = (bf16[2,512,512]{2,1,0:T(8,128)(2,1)}, bf16[2,512,512]{2,1,0:T(8,128)(2,1)}, bf16[2,352,512]{2,1,0:T(8,128)(2,1)}) custom-call(bf16[2,352,512]{2,1,0:T(8,128)(2,1)} %get-tuple-element.67.own_ref, s32[2,27]{1,0:T(2,128)} %near_ref.1, s32[2,2,2]{2,1,0:T(2,128)} %send_ref.5), custom_call_target="tpu_custom_call" | custom-call | flops 1000000000 | bytes 4194304 | tf_op jit(solution)/shard_map/pallas_call | solution.py:511
  9.2 0.0 collective-permute-done.f1_ref
  9.3 2.7 %collective-permute-start.2 = (bf16[440,128]{1,0:T(8,128)(2,1)S(1)}, bf16[440,128]{1,0:T(8,128)(2,1)S(1)}, u32[]{:S(2)}, u32[]{:S(2)}) collective-permute-start(bf16[440,128]{1,0:T(8,128)(2,1)S(1)} %pad_maximum_fusion.3), channel_id=1, source_target_pairs={{0,1},{1,0},{2,3},{3,2},{4,5},{5,4},{6,7},{7,6},{8,9},{9,8},{10,11... | collective-permute-start | bytes 337928 | tf_op jit(solution)/shard_map/ppermute | solution.py:546
  12.0 2.8 %shard_map.104 = (bf16[3,512,896]{2,1,0:T(8,128)(2,1)S(1)}, bf16[864,288]{1,0:T(8,128)(2,1)S(1)}, bf16[256,2592]{1,0:T(8,128)(2,1)S(1)}) custom-call(bf16[27,96,96]{2,1,0:T(8,128)(2,1)S(1)} %copy-done.1, bf16[27,96,256]{2,1,0:T(8,128)(2,1)S(1)} %copy-done), custom_call_target="tpu_custom_call" | custom-call | flops 100000000 | bytes 6291456 | tf_op jit(solution)/shard_map/pallas_call | solution.py:511
  14.9 1.1 %copy-done.7 = bf16[2,352,512]{2,1,0:T(8,128)(2,1)S(1)} copy-done((bf16[2,352,512]{2,1,0:T(8,128)(2,1)S(1)}, bf16[2,352,512]{2,1,0:T(8,128)(2,1)}, u32[]{:S(2)}) %copy-start.7) | copy-done | bytes 720920
  16.0 9.2 %shard_map.105 = (bf16[288,1792]{1,0:T(8,128)(2,1)S(1)}, bf16[768,1792]{1,0:T(8,128)(2,1)S(1)}, bf16[96,1280]{1,0:T(8,128)(2,1)S(1)}, bf16[96,1280]{1,0:T(8,128)...) custom-call(bf16[440,128]{1,0:T(8,128)(2,1)S(1)} %collective-permute, ...), custom_call_target="tpu_custom_call" | custom-call | flops 5000000000 | bytes 8388608 | tf_op jit(solution)/shard_map/pallas_call | solution.py:511
  25.2 2.7 %collective-permute-start.3 = (bf16[240,128]{1,0:T(8,128)(2,1)S(1)}, bf16[240,128]{1,0:T(8,128)(2,1)S(1)}, u32[]{:S(2)}, u32[]{:S(2)}) collective-permute-start(bf16[240,128]{1,0:T(8,128)(2,1)S(1)} %get-tuple-element.79), channel_id=1, source_target_pairs={{0,2},{4,6},{2,0},{6,4},{1,3},{5,7},{3,1},{7,5},{8,10},{12,14},{10... | collective-permute-start | bytes 184328 | tf_op jit(solution)/shard_map/ppermute | solution.py:528
  27.8 0.7 collective-permute-start.4
  28.5 4.9 %shard_map.106 = (f32[2,1856,128]{2,1,0:T(8,128)S(1)}, bf16[2,1856,128]{2,1,0:T(8,128)(2,1)S(1)}) custom-call(bf16[288,1792]{1,0:T(8,128)(2,1)S(1)} %get-tuple-element.81.zx_ref, bf16[768,1792]{1,0:T(8,128)(2,1)S(1)} %get-tuple-element.82.zg_ref, bf16[96,1280]{1,0:T(8,128)(2,1)S(1)} %get-tuple-element.83.gpre_ref, ...), custom_call_target="tpu_custom_call" | custom-call | flops 5000000000 | bytes 6291456 | tf_op jit(solution)/shard_map/pallas_call | solution.py:511
  33.4 2.1 %collective-permute-start.5 = (bf16[2,1856,128]{2,1,0:T(8,128)(2,1)S(1)}, bf16[2,1856,128]{2,1,0:T(8,128)(2,1)S(1)}, u32[]{:S(2)}, u32[]{:S(2)}) collective-permute-start(bf16[2,1856,128]{2,1,0:T(8,128)(2,1)S(1)} %get-tuple-element.88), channel_id=1, source_target_pairs={{0,2},{2,0},{4,6},{6,4},{1,3},{3,1},{5,7},{7,5},{8,10},{10,8},{12,... | collective-permute-start | bytes 2850824 | tf_op jit(solution)/shard_map/ppermute | solution.py:707
  35.5 0.0 copy-start.5
  35.5 1.9 %collective-permute-start.6 = (bf16[240,128]{1,0:T(8,128)(2,1)S(1)}, bf16[240,128]{1,0:T(8,128)(2,1)S(1)}, u32[]{:S(2)}, u32[]{:S(2)}) collective-permute-start(bf16[240,128]{1,0:T(8,128)(2,1)S(1)} %pad_maximum_fusion.4), channel_id=1, source_target_pairs={{0,1},{1,0},{2,3},{3,2},{4,5},{5,4},{6,7},{7,6},{8,9},{9,8},{10,11... | collective-permute-start | bytes 184328 | tf_op jit(solution)/shard_map/ppermute | solution.py:546
  37.5 0.1 fusion.3
  37.6 2.2 %collective-permute-done.6 = bf16[240,128]{1,0:T(8,128)(2,1)S(1)} collective-permute-done((bf16[240,128]{1,0:T(8,128)(2,1)S(1)}, bf16[240,128]{1,0:T(8,128)(2,1)S(1)}, u32[]{:S(2)}, u32[]{:S(2)}) %collective-permute-start.6) | collective-permute-done | bytes 61472 | tf_op jit(solution)/shard_map/ppermute | solution.py:546
  39.8 1.9 %shard_map.107 = (bf16[288,1792]{1,0:T(8,128)(2,1)S(1)}, bf16[288,1792]{1,0:T(8,128)(2,1)S(1)}) custom-call(bf16[240,128]{1,0:T(8,128)(2,1)S(1)} %collective-permute-done.3.f1_ref, bf16[240,128]{1,0:T(8,128)(2,1)S(1)} %collective-permute-done.4.f2_ref, bf16[1,240,128]{2,1,0:T(8,128)(2,1)S(1)} %bitcast.18, bf16[2,512,512]{2,1,0:T(8,128)(2,1)S(1)} %copy-done.6, ...), custom_call_target="tpu_custom_call" | custom-call | flops 2000000000 | bytes 6291456 | tf_op jit(solution)/shard_map/pallas_call | solution.py:511
  41.8 0.1 fusion.5
  41.8 0.1 fusion
  42.0 0.1 fusion.2
  42.1 0.1 fusion.4
  42.2 1.1 %collective-permute-start.7 = (bf16[928,128]{1,0:T(8,128)(2,1)S(1)}, bf16[928,128]{1,0:T(8,128)(2,1)S(1)}, u32[]{:S(2)}, u32[]{:S(2)}) collective-permute-start(bf16[928,128]{1,0:T(8,128)(2,1)S(1)} %get-tuple-element.99), channel_id=1, source_target_pairs={{0,4},{2,6},{4,0},{6,2},{1,5},{3,7},{5,1},{7,3},{8,12},{10,14},{12... | collective-permute-start | bytes 712712 | tf_op jit(solution)/shard_map/ppermute | solution.py:713
  43.3 1.0 %collective-permute-start.8 = (bf16[928,128]{1,0:T(8,128)(2,1)S(1)}, bf16[928,128]{1,0:T(8,128)(2,1)S(1)}, u32[]{:S(2)}, u32[]{:S(2)}) collective-permute-start(bf16[928,128]{1,0:T(8,128)(2,1)S(1)} %get-tuple-element.100), channel_id=1, source_target_pairs={{0,1},{1,0},{2,3},{3,2},{4,5},{5,4},{6,7},{7,6},{8,9},{9,8},{10,11... | collective-permute-start | bytes 712712 | tf_op jit(solution)/shard_map/ppermute | solution.py:714
  44.3 3.4 %shard_map.108.rest_0_ = bf16[2,256,512]{2,1,0:T(8,128)(2,1)} custom-call(s32[2,18]{1,0:T(2,128)S(1)} %copy-done.3, bf16[288,1792]{1,0:T(8,128)(2,1)S(1)} %get-tuple-element.110.zh_ref, bf16[256,2592]{1,0:T(8,128)(2,1)S(1)} %get-tuple-element.101.wbt_ref), custom_call_target="tpu_custom_call" | custom-call | flops 1000000000 | bytes 2097152 | tf_op jit(solution)/shard_map/pallas_call | solution.py:511
  47.7 0.1 add_bitcast_fusion
  47.8 0.1 add_bitcast_fusion.1
  47.9 1.1 %collective-permute-done.7 = bf16[928,128]{1,0:T(8,128)(2,1)S(1)} collective-permute-done((bf16[928,128]{1,0:T(8,128)(2,1)S(1)}, bf16[928,128]{1,0:T(8,128)(2,1)S(1)}, u32[]{:S(2)}, u32[]{:S(2)}) %collective-permute-start.7) | collective-permute-done | bytes 237600 | tf_op jit(solution)/shard_map/ppermute | solution.py:713
  49.0 1.5 %collective-permute-done.8 = bf16[928,128]{1,0:T(8,128)(2,1)S(1)} collective-permute-done((bf16[928,128]{1,0:T(8,128)(2,1)S(1)}, bf16[928,128]{1,0:T(8,128)(2,1)S(1)}, u32[]{:S(2)}, u32[]{:S(2)}) %collective-permute-start.8) | collective-permute-done | bytes 237600 | tf_op jit(solution)/shard_map/ppermute | solution.py:714
  50.6 0.4 collective-permute-start.10
  51.0 1.7 %collective-permute-start.9 = (bf16[464,128]{1,0:T(8,128)(2,1)S(1)}, bf16[464,128]{1,0:T(8,128)(2,1)S(1)}, u32[]{:S(2)}, u32[]{:S(2)}) collective-permute-start(bf16[464,128]{1,0:T(8,128)(2,1)S(1)} %select_convert_fusion.1), channel_id=1, source_target_pairs={{0,1},{1,0},{2,3},{3,2},{4,5},{5,4},{6,7},{7,6},{8,9},{9,8},{10,11... | collective-permute-start | bytes 356360 | tf_op jit(solution)/shard_map/ppermute | solution.py:724
  52.7 3.4 %shard_map.109 = bf16[2,256,512]{2,1,0:T(8,128)(2,1)} custom-call(s32[2,18]{1,0:T(2,128)S(1)} %copy-done.3, bf16[288,1792]{1,0:T(8,128)(2,1)S(1)} %get-tuple-element.110.zh_ref, bf16[256,2592]{1,0:T(8,128)(2,1)S(1)} %get-tuple-element.101.wbt_ref, bf16[2,256,512]{2,1,0:T(8,128)(2,1)} %shard_map.108.rest_0_), custom_call_target="tpu_custom_call", output_to_operand_aliasing={{}: (3, {})} | custom-call | flops 1000000000 | bytes 2097152 | tf_op jit(solution)/shard_map/pallas_call | solution.py:511
  56.2 1.5 %collective-permute-start.11 = (bf16[464,128]{1,0:T(8,128)(2,1)S(1)}, bf16[464,128]{1,0:T(8,128)(2,1)S(1)}, u32[]{:S(2)}, u32[]{:S(2)}) collective-permute-start(bf16[464,128]{1,0:T(8,128)(2,1)S(1)} %add_convert_fusion.3), channel_id=1, source_target_pairs={{0,1},{1,0},{2,3},{3,2},{4,5},{5,4},{6,7},{7,6},{8,9},{9,8},{10,11... | collective-permute-start | bytes 356360 | tf_op jit(solution)/shard_map/ppermute | solution.py:731
  57.7 0.9 %collective-permute-start.12 = (bf16[464,128]{1,0:T(8,128)(2,1)S(1)}, bf16[464,128]{1,0:T(8,128)(2,1)S(1)}, u32[]{:S(2)}, u32[]{:S(2)}) collective-permute-start(bf16[464,128]{1,0:T(8,128)(2,1)S(1)} %add_convert_fusion.2), channel_id=1, source_target_pairs={{0,4},{2,6},{4,0},{6,2},{1,5},{3,7},{5,1},{7,3},{8,12},{10,14},{12... | collective-permute-start | bytes 356360 | tf_op jit(solution)/shard_map/ppermute | solution.py:732
  58.7 3.9 %shard_map.110 = bf16[2,96,512]{2,1,0:T(8,128)(2,1)} custom-call(s32[2,18]{1,0:T(2,128)S(1)} %copy-done.3, bf16[288,1792]{1,0:T(8,128)(2,1)S(1)} %get-tuple-element.118.zp_ref, bf16[27,96,96]{2,1,0:T(8,128)(2,1)S(1)} %copy-done.1), custom_call_target="tpu_custom_call" | custom-call | flops 2000000000 | bytes 2097152 | tf_op jit(solution)/shard_map/pallas_call | solution.py:511
  62.6 0.3 collective-permute-done.12
  62.9 1.4 %collective-permute-start.13 = (bf16[928,128]{1,0:T(8,128)(2,1)S(1)}, bf16[928,128]{1,0:T(8,128)(2,1)S(1)}, u32[]{:S(2)}, u32[]{:S(2)}) collective-permute-start(bf16[928,128]{1,0:T(8,128)(2,1)S(1)} %pad_maximum_fusion.1), channel_id=1, source_target_pairs={{0,4},{2,6},{4,0},{6,2},{1,5},{3,7},{5,1},{7,3},{8,12},{10,14},{12... | collective-permute-start | bytes 712712 | tf_op jit(solution)/shard_map/ppermute | solution.py:743
  64.3 1.1 %collective-permute-start.14 = (bf16[928,128]{1,0:T(8,128)(2,1)S(1)}, bf16[928,128]{1,0:T(8,128)(2,1)S(1)}, u32[]{:S(2)}, u32[]{:S(2)}) collective-permute-start(bf16[928,128]{1,0:T(8,128)(2,1)S(1)} %pad_maximum_fusion.2), channel_id=1, source_target_pairs={{0,1},{1,0},{2,3},{3,2},{4,5},{5,4},{6,7},{7,6},{8,9},{9,8},{10,11... | collective-permute-start | bytes 712712 | tf_op jit(solution)/shard_map/ppermute | solution.py:744
  65.4 3.6 %collective-permute-done.13 = bf16[928,128]{1,0:T(8,128)(2,1)S(1)} collective-permute-done((bf16[928,128]{1,0:T(8,128)(2,1)S(1)}, bf16[928,128]{1,0:T(8,128)(2,1)S(1)}, u32[]{:S(2)}, u32[]{:S(2)}) %collective-permute-start.13) | collective-permute-done | bytes 237600 | tf_op jit(solution)/shard_map/ppermute | solution.py:743
  69.1 0.1 broadcast_select_fusion.3
  69.2 1.3 %collective-permute-done.14 = bf16[928,128]{1,0:T(8,128)(2,1)S(1)} collective-permute-done((bf16[928,128]{1,0:T(8,128)(2,1)S(1)}, bf16[928,128]{1,0:T(8,128)(2,1)S(1)}, u32[]{:S(2)}, u32[]{:S(2)}) %collective-permute-start.14) | collective-permute-done | bytes 237600 | tf_op jit(solution)/shard_map/ppermute | solution.py:744
  70.5 0.1 broadcast_select_fusion.1
  70.7 0.1 pad_maximum_fusion.mine_ref
  70.8 0.1 collective-permute-start.15
  70.8 2.5 %collective-permute-done.15.other_ref = bf16[2,1856,128]{2,1,0:T(8,128)(2,1)S(1)} collective-permute-done((bf16[2,1856,128]{2,1,0:T(8,128)(2,1)S(1)}, bf16[2,1856,128]{2,1,0:T(8,128)(2,1)S(1)}, u32[]{:S(2)}, u32[]{:S(2)}) %collective-permute-start.15) | collective-permute-done | bytes 950304 | tf_op jit(solution)/shard_map/ppermute | solution.py:746
  73.3 2.5 %shard_map.111 = (f32[27,96,96]{2,1,0:T(8,128)}, f32[27,96,256]{2,1,0:T(8,128)}) custom-call(bf16[2,1856,128]{2,1,0:T(8,128)(2,1)S(1)} %pad_maximum_fusion.mine_ref, bf16[2,1856,128]{2,1,0:T(8,128)(2,1)S(1)} %collective-permute-done.15.other_ref), custom_call_target="tpu_custom_call" | custom-call | bytes 6291456 | tf_op jit(solution)/shard_map/pallas_call | solution.py:511
  (38 shorter events, 0.4 us)
Async XLA Ops:
  3.3 6.0 %copy-start.8 = (bf16[1,352,128]{2,1,0:T(8,128)(2,1)S(1)}, bf16[1,352,128]{2,1,0:T(8,128)(2,1)}, u32[]{:S(2)}) copy-start(bf16[1,352,128]{2,1,0:T(8,128)(2,1)} %get-tuple-element.69) | copy-start | bytes 270340
  3.3 5.9 %collective-permute-start = (bf16[440,128]{1,0:T(8,128)(2,1)}, bf16[440,128]{1,0:T(8,128)(2,1)S(1)}, u32[]{:S(2)}, u32[]{:S(2)}) collective-permute-start(bf16[440,128]{1,0:T(8,128)(2,1)} %get-tuple-element.64), channel_id=1, source_target_pairs={{0,2},{4,6},{2,0},{6,4},{1,3},{5,7},{3,1},{7,5},{8,10},{12,14},{10... | collective-permute-start | bytes 337928 | tf_op jit(solution)/shard_map/ppermute | solution.py:528
  3.7 5.5 %collective-permute-start.1 = (bf16[440,128]{1,0:T(8,128)(2,1)}, bf16[440,128]{1,0:T(8,128)(2,1)S(1)}, u32[]{:S(2)}, u32[]{:S(2)}) collective-permute-start(bf16[440,128]{1,0:T(8,128)(2,1)} %get-tuple-element.65), channel_id=1, source_target_pairs={{2,4},{4,2},{3,5},{5,3},{10,12},{12,10},{11,13},{13,11},{18,20},{2... | collective-permute-start | bytes 337928 | tf_op jit(solution)/shard_map/ppermute | solution.py:528
  4.4 7.6 %copy-start = (bf16[27,96,256]{2,1,0:T(8,128)(2,1)S(1)}, bf16[27,96,256]{2,1,0:T(8,128)(2,1)}, u32[]{:S(2)}) copy-start(bf16[27,96,256]{2,1,0:T(8,128)(2,1)} %wb_ref.1) | copy-start | bytes 3981316
  4.4 7.6 %copy-start.1 = (bf16[27,96,96]{2,1,0:T(8,128)(2,1)S(1)}, bf16[27,96,96]{2,1,0:T(8,128)(2,1)}, u32[]{:S(2)}) copy-start(bf16[27,96,96]{2,1,0:T(8,128)(2,1)} %wa_ref.1) | copy-start | bytes 1492996
  9.2 5.6 %copy-start.2 = (s32[2,2,2]{2,1,0:T(2,128)S(1)}, s32[2,2,2]{2,1,0:T(2,128)}, u32[]{:S(2)}) copy-start(s32[2,2,2]{2,1,0:T(2,128)} %send_ref.5) | copy-start | bytes 100
  9.2 5.7 %copy-start.3 = (s32[2,18]{1,0:T(2,128)S(1)}, s32[2,18]{1,0:T(2,128)}, u32[]{:S(2)}) copy-start(s32[2,18]{1,0:T(2,128)} %occ_ref.9) | copy-start | bytes 436
  9.2 5.7 %copy-start.4 = (bf16[2,352,512]{2,1,0:T(8,128)(2,1)S(1)}, bf16[2,352,512]{2,1,0:T(8,128)(2,1)}, u32[]{:S(2)}) copy-start(bf16[2,352,512]{2,1,0:T(8,128)(2,1)} %get-tuple-element.67.own_ref) | copy-start | bytes 2162692
  9.3 5.6 %collective-permute-start.2 = (bf16[440,128]{1,0:T(8,128)(2,1)S(1)}, bf16[440,128]{1,0:T(8,128)(2,1)S(1)}, u32[]{:S(2)}, u32[]{:S(2)}) collective-permute-start(bf16[440,128]{1,0:T(8,128)(2,1)S(1)} %pad_maximum_fusion.3), channel_id=1, source_target_pairs={{0,1},{1,0},{2,3},{3,2},{4,5},{5,4},{6,7},{7,6},{8,9},{9,8},{10,11... | collective-permute-start | bytes 337928 | tf_op jit(solution)/shard_map/ppermute | solution.py:546
  12.0 2.9 %copy-start.6 = (bf16[2,512,512]{2,1,0:T(8,128)(2,1)S(1)}, bf16[2,512,512]{2,1,0:T(8,128)(2,1)}, u32[]{:S(2)}) copy-start(bf16[2,512,512]{2,1,0:T(8,128)(2,1)} %get-tuple-element.75.sr_ref) | copy-start | bytes 3145732
  14.9 1.1 %copy-start.7 = (bf16[2,352,512]{2,1,0:T(8,128)(2,1)S(1)}, bf16[2,352,512]{2,1,0:T(8,128)(2,1)}, u32[]{:S(2)}) copy-start(bf16[2,352,512]{2,1,0:T(8,128)(2,1)} %get-tuple-element.76.part_ref) | copy-start | bytes 2162692
  25.2 8.2 %collective-permute-start.3 = (bf16[240,128]{1,0:T(8,128)(2,1)S(1)}, bf16[240,128]{1,0:T(8,128)(2,1)S(1)}, u32[]{:S(2)}, u32[]{:S(2)}) collective-permute-start(bf16[240,128]{1,0:T(8,128)(2,1)S(1)} %get-tuple-element.79), channel_id=1, source_target_pairs={{0,2},{4,6},{2,0},{6,4},{1,3},{5,7},{3,1},{7,5},{8,10},{12,14},{10... | collective-permute-start | bytes 184328 | tf_op jit(solution)/shard_map/ppermute | solution.py:528
  27.8 5.6 %collective-permute-start.4 = (bf16[240,128]{1,0:T(8,128)(2,1)S(1)}, bf16[240,128]{1,0:T(8,128)(2,1)S(1)}, u32[]{:S(2)}, u32[]{:S(2)}) collective-permute-start(bf16[240,128]{1,0:T(8,128)(2,1)S(1)} %get-tuple-element.80), channel_id=1, source_target_pairs={{2,4},{4,2},{3,5},{5,3},{10,12},{12,10},{11,13},{13,11},{18,20},{2... | collective-permute-start | bytes 184328 | tf_op jit(solution)/shard_map/ppermute | solution.py:528
  33.4 8.4 %collective-permute-start.5 = (bf16[2,1856,128]{2,1,0:T(8,128)(2,1)S(1)}, bf16[2,1856,128]{2,1,0:T(8,128)(2,1)S(1)}, u32[]{:S(2)}, u32[]{:S(2)}) collective-permute-start(bf16[2,1856,128]{2,1,0:T(8,128)(2,1)S(1)} %get-tuple-element.88), channel_id=1, source_target_pairs={{0,2},{2,0},{4,6},{6,4},{1,3},{3,1},{5,7},{7,5},{8,10},{10,8},{12,... | collective-permute-start | bytes 2850824 | tf_op jit(solution)/shard_map/ppermute | solution.py:707
  35.5 4.3 %copy-start.5 = (bf16[2,512,512]{2,1,0:T(8,128)(2,1)S(1)}, bf16[2,512,512]{2,1,0:T(8,128)(2,1)}, u32[]{:S(2)}) copy-start(bf16[2,512,512]{2,1,0:T(8,128)(2,1)} %get-tuple-element.92.so_ref) | copy-start | bytes 3145732
  35.5 4.3 %collective-permute-start.6 = (bf16[240,128]{1,0:T(8,128)(2,1)S(1)}, bf16[240,128]{1,0:T(8,128)(2,1)S(1)}, u32[]{:S(2)}, u32[]{:S(2)}) collective-permute-start(bf16[240,128]{1,0:T(8,128)(2,1)S(1)} %pad_maximum_fusion.4), channel_id=1, source_target_pairs={{0,1},{1,0},{2,3},{3,2},{4,5},{5,4},{6,7},{7,6},{8,9},{9,8},{10,11... | collective-permute-start | bytes 184328 | tf_op jit(solution)/shard_map/ppermute | solution.py:546
  42.2 6.8 %collective-permute-start.7 = (bf16[928,128]{1,0:T(8,128)(2,1)S(1)}, bf16[928,128]{1,0:T(8,128)(2,1)S(1)}, u32[]{:S(2)}, u32[]{:S(2)}) collective-permute-start(bf16[928,128]{1,0:T(8,128)(2,1)S(1)} %get-tuple-element.99), channel_id=1, source_target_pairs={{0,4},{2,6},{4,0},{6,2},{1,5},{3,7},{5,1},{7,3},{8,12},{10,14},{12... | collective-permute-start | bytes 712712 | tf_op jit(solution)/shard_map/ppermute | solution.py:713
  43.3 7.1 %collective-permute-start.8 = (bf16[928,128]{1,0:T(8,128)(2,1)S(1)}, bf16[928,128]{1,0:T(8,128)(2,1)S(1)}, u32[]{:S(2)}, u32[]{:S(2)}) collective-permute-start(bf16[928,128]{1,0:T(8,128)(2,1)S(1)} %get-tuple-element.100), channel_id=1, source_target_pairs={{0,1},{1,0},{2,3},{3,2},{4,5},{5,4},{6,7},{7,6},{8,9},{9,8},{10,11... | collective-permute-start | bytes 712712 | tf_op jit(solution)/shard_map/ppermute | solution.py:714
  50.6 5.5 %collective-permute-start.10 = (bf16[464,128]{1,0:T(8,128)(2,1)S(1)}, bf16[464,128]{1,0:T(8,128)(2,1)S(1)}, u32[]{:S(2)}, u32[]{:S(2)}) collective-permute-start(bf16[464,128]{1,0:T(8,128)(2,1)S(1)} %select_convert_fusion), channel_id=1, source_target_pairs={{0,4},{2,6},{4,0},{6,2},{1,5},{3,7},{5,1},{7,3},{8,12},{10,14},{12... | collective-permute-start | bytes 356360 | tf_op jit(solution)/shard_map/ppermute | solution.py:725
  51.0 5.1 %collective-permute-start.9 = (bf16[464,128]{1,0:T(8,128)(2,1)S(1)}, bf16[464,128]{1,0:T(8,128)(2,1)S(1)}, u32[]{:S(2)}, u32[]{:S(2)}) collective-permute-start(bf16[464,128]{1,0:T(8,128)(2,1)S(1)} %select_convert_fusion.1), channel_id=1, source_target_pairs={{0,1},{1,0},{2,3},{3,2},{4,5},{5,4},{6,7},{7,6},{8,9},{9,8},{10,11... | collective-permute-start | bytes 356360 | tf_op jit(solution)/shard_map/ppermute | solution.py:724
  56.2 6.4 %collective-permute-start.11 = (bf16[464,128]{1,0:T(8,128)(2,1)S(1)}, bf16[464,128]{1,0:T(8,128)(2,1)S(1)}, u32[]{:S(2)}, u32[]{:S(2)}) collective-permute-start(bf16[464,128]{1,0:T(8,128)(2,1)S(1)} %add_convert_fusion.3), channel_id=1, source_target_pairs={{0,1},{1,0},{2,3},{3,2},{4,5},{5,4},{6,7},{7,6},{8,9},{9,8},{10,11... | collective-permute-start | bytes 356360 | tf_op jit(solution)/shard_map/ppermute | solution.py:731
  57.7 5.1 %collective-permute-start.12 = (bf16[464,128]{1,0:T(8,128)(2,1)S(1)}, bf16[464,128]{1,0:T(8,128)(2,1)S(1)}, u32[]{:S(2)}, u32[]{:S(2)}) collective-permute-start(bf16[464,128]{1,0:T(8,128)(2,1)S(1)} %add_convert_fusion.2), channel_id=1, source_target_pairs={{0,4},{2,6},{4,0},{6,2},{1,5},{3,7},{5,1},{7,3},{8,12},{10,14},{12... | collective-permute-start | bytes 356360 | tf_op jit(solution)/shard_map/ppermute | solution.py:732
  62.9 6.2 %collective-permute-start.13 = (bf16[928,128]{1,0:T(8,128)(2,1)S(1)}, bf16[928,128]{1,0:T(8,128)(2,1)S(1)}, u32[]{:S(2)}, u32[]{:S(2)}) collective-permute-start(bf16[928,128]{1,0:T(8,128)(2,1)S(1)} %pad_maximum_fusion.1), channel_id=1, source_target_pairs={{0,4},{2,6},{4,0},{6,2},{1,5},{3,7},{5,1},{7,3},{8,12},{10,14},{12... | collective-permute-start | bytes 712712 | tf_op jit(solution)/shard_map/ppermute | solution.py:743
  64.3 6.2 %collective-permute-start.14 = (bf16[928,128]{1,0:T(8,128)(2,1)S(1)}, bf16[928,128]{1,0:T(8,128)(2,1)S(1)}, u32[]{:S(2)}, u32[]{:S(2)}) collective-permute-start(bf16[928,128]{1,0:T(8,128)(2,1)S(1)} %pad_maximum_fusion.2), channel_id=1, source_target_pairs={{0,1},{1,0},{2,3},{3,2},{4,5},{5,4},{6,7},{7,6},{8,9},{9,8},{10,11... | collective-permute-start | bytes 712712 | tf_op jit(solution)/shard_map/ppermute | solution.py:744
  70.8 2.6 %collective-permute-start.15 = (bf16[2,1856,128]{2,1,0:T(8,128)(2,1)S(1)}, bf16[2,1856,128]{2,1,0:T(8,128)(2,1)S(1)}, u32[]{:S(2)}, u32[]{:S(2)}) collective-permute-start(bf16[2,1856,128]{2,1,0:T(8,128)(2,1)S(1)} %pad_maximum_fusion.mine_ref), channel_id=1, source_target_pairs={{0,2},{2,0},{4,6},{6,4},{1,3},{3,1},{5,7},{7,5},{8,10},{10,8},{12,... | collective-permute-start | bytes 2850824 | tf_op jit(solution)/shard_map/ppermute | solution.py:746
